TPU v7x, 32 devices: a whole 2x2x4 slice. The times are simulated.
32 devices in a mesh: gx: 2 (over core), gy: 16 (over z, y, x).
Axes of the slice: x: 2, y: 2, z: 4, core: 2. Of those that a mesh axis runs over, the one named last changes fastest.
Arguments:
- krylov: float32 [2, 256, 8, 2, 256], P('gx', 'gy'), may hold values from -6 to 6
- block_inverse: float32 [2, 256, 2, 2, 256], P('gx', 'gy'), may hold values from -0.02 to 0.07, as said below
- back_coupling: float32 [2, 256, 2, 2, 256], P('gx', 'gy'), may hold values from -0.3 to 0.06, as said below
- front_coupling: float32 [2, 256, 2, 2, 256], P('gx', 'gy'), may hold values from -0.3 to 0.06, as said below
- left_coupling: float32 [2, 256, 2, 2, 256], P('gx', 'gy'), may hold values from -10240 to 10240, as said below
- right_coupling: float32 [2, 256, 2, 2, 256], P('gx', 'gy'), may hold values from -10240 to 10240, as said below
Outputs:
- preconditioned: float32 [2, 256, 8, 2, 256], P('gx', 'gy')
Inputs may be any that keep to these rules, and one draw needn't show every extreme that they name: `block_inverse`: a 2x2 block for each cell. `back_coupling`: a 2x2 block for each cell. `front_coupling`: a 2x2 block for each cell. `left_coupling`: a 2x2 block for each cell. `right_coupling`: a 2x2 block for each cell.
All inputs are finite; a program needn't handle non-finite values.
Results may differ from a plain program's by a relative error of at most 0.00018.
Values sent between devices are 32-bit elements; how exact they have to be, the bound alone decides.
No kernel may reach another device: no remote copies, remote signals or barrier semaphores. Data moves between devices by JAX's collectives and lax.ppermute only.
A program may use at most 64 MiB of HBM per device.

v0:
```python
import jax
import jax.numpy as jnp
from jax import lax
from jax.sharding import PartitionSpec as P


def entering(x, axis, combine, identity, reverse):
    size, place = (lax.axis_size(axis), lax.axis_index(axis))
    everything = jax.tree.map(lambda part: lax.all_gather(part, axis), x)
    start = jax.tree.map(
        lambda part, zero: jnp.broadcast_to(jnp.asarray(zero, part.dtype), part.shape), x, identity
    )

    def step(k, before):
        at = size - 1 - k if reverse else k
        reached = at > place if reverse else at < place
        new = combine(before, jax.tree.map(lambda part: part[at], everything))
        return jax.tree.map(lambda a, b: jnp.where(reached, a, b), new, before)

    return lax.fori_loop(0, size, step, start)


def passed_along(value, axis, steps):
    count = lax.axis_size(axis)
    initial, last = (max(0, -steps), min(count, count - steps))
    return lax.ppermute(value, axis, [(source, source + steps) for source in range(initial, last)])


def apply_block(matrix, vector):
    spread_matrix = matrix[..., None, :, :, :]
    return (
        spread_matrix[..., 0, :] * vector[..., 0:1, :]
        + spread_matrix[..., 1, :] * vector[..., 1:2, :]
    )


def block_product(left_block, right_block):
    return (
        left_block[..., :, 0:1, :] * right_block[..., 0:1, :, :]
        + left_block[..., :, 1:2, :] * right_block[..., 1:2, :, :]
    )


def compose(earlier, later):
    earlier_map, earlier_offset = earlier
    later_map, later_offset = later
    return (
        block_product(later_map, earlier_map),
        apply_block(later_map, earlier_offset) + later_offset,
    )


def solve_plane(source, inverse, forward_maps, backward_maps, identity):
    scaled = apply_block(inverse, source)
    matrices, offsets = lax.associative_scan(compose, (forward_maps, scaled))
    _, state_in = entering(
        (matrices[-1], offsets[-1]), "gy", compose, (identity, jnp.zeros_like(offsets[-1])), False
    )
    forward_state = apply_block(matrices, state_in[None]) + offsets
    back_matrices, back_offsets = lax.associative_scan(
        compose, (backward_maps, forward_state), reverse=True
    )
    _, upper_neighbour_state = entering(
        (back_matrices[0], back_offsets[0]),
        "gy",
        compose,
        (identity, jnp.zeros_like(back_offsets[0])),
        True,
    )
    return apply_block(back_matrices, upper_neighbour_state[None]) + back_offsets


def per_device(krylov, block_inverse, back_coupling, front_coupling, left_coupling, right_coupling):
    plane_count, line_count, vector_count, _, cell_count = krylov.shape
    forward_maps = -block_product(block_inverse, left_coupling)
    backward_maps = -block_product(block_inverse, right_coupling)
    identity = jnp.broadcast_to(jnp.eye(2, dtype=jnp.float32)[:, :, None], (2, 2, cell_count))
    group_count = 1
    group_width = vector_count // group_count
    chain_size = lax.axis_size("gx")
    chain_index = lax.axis_index("gx")
    reverse_index = chain_size - 1 - chain_index
    turn_total = chain_size + group_count - 1
    empty_boundary = jnp.zeros((line_count, group_width, 2, cell_count), jnp.float32)

    def forward_turn(turn_index, carry):
        result, incoming = carry
        group_index = jnp.clip(turn_index - chain_index, 0, group_count - 1)
        group_start = group_index * group_width
        previous = incoming
        source = krylov[0]
        swept = solve_plane(
            source - apply_block(back_coupling[0], previous),
            block_inverse[0],
            forward_maps[0],
            backward_maps[0],
            identity,
        )
        result = result.at[0].set(lax.dynamic_update_slice_in_dim(result[0], swept, group_start, 1))
        incoming = passed_along(swept, "gx", 1)
        return (result, incoming)

    swept_all, _ = lax.fori_loop(
        0, turn_total, forward_turn, (jnp.zeros_like(krylov), empty_boundary)
    )

    def backward_turn(turn_index, carry):
        result, incoming = carry
        group_index = jnp.clip(turn_index - reverse_index, 0, group_count - 1)
        group_start = group_index * group_width
        following = incoming
        for plane in reversed(range(plane_count)):
            swept = swept_all[plane]
            sweep_out = swept - solve_plane(
                apply_block(front_coupling[plane], following),
                block_inverse[plane],
                forward_maps[plane],
                backward_maps[plane],
                identity,
            )
            result = result.at[plane].set(
                lax.dynamic_update_slice_in_dim(result[plane], sweep_out, group_start, 1)
            )
            following = sweep_out
        incoming = passed_along(following, "gx", -1)
        return (result, incoming)

    preconditioned, _ = lax.fori_loop(
        0, turn_total, backward_turn, (jnp.zeros_like(krylov), empty_boundary)
    )
    return preconditioned


def solution(mesh):
    return jax.shard_map(
        per_device,
        mesh=mesh,
        in_specs=(
            P("gx", "gy", None, None, None),
            P("gx", "gy", None, None, None),
            P("gx", "gy", None, None, None),
            P("gx", "gy", None, None, None),
            P("gx", "gy", None, None, None),
            P("gx", "gy", None, None, None),
        ),
        out_specs=P("gx", "gy", None, None, None),
        check_vma=False,
    )
```

profile of v0, /device:TPU:0, one launch (start us, length us, event | category | flops | bytes accessed | tf_op | source)
XLA Modules:
  0.0 687.1 jit_solution(686120172287409337)
XLA Ops:
  5.3 341.1 %while.176 = (s32[]{:T(128)}, f32[1,16,8,2,256]{4,2,3,1,0:T(8,128)}, f32[16,8,2,256]{3,1,2,0:T(8,128)S(1)}, f32[1,16,2,2,256]{4,3,2,1,0:T(2,128)S(1)}, f32[1,16,...) while((s32[]{:T(128)}, f32[1,16,8,2,256]{4,2,3,1,0:T(8,128)}, ...), condition=%wide.region_5.6_spmd, body=%wide.region_0.5_spmd.sunk | while | flops 2887698 | bytes 27456480 | solution.py:103
  12.4 42.8 %all_gather.88 = f32[16,2,2,256]{3,2,1,0:T(2,128)S(1)} all-gather(f32[1,2,2,256]{3,2,1,0:T(2,128)S(1)} %slice_add_fusion.61), channel_id=1, replica_groups=mesh['gx'=2,'gy'=16] {'gy'}, dimensions={0}, use_global_device_ids=true | all-gather | bytes 69632 | tf_op jit(solution)/shard_map/while/body/eval_jaxpr/all_gather | solution.py:9
  55.6 36.9 %all_gather.89 = f32[16,8,2,256]{3,1,2,0:T(8,128)S(1)} all-gather(f32[1,8,2,256]{3,1,2,0:T(8,128)S(1)} %slice_add_fusion.62), channel_id=1, replica_groups=mesh['gx'=2,'gy'=16] {'gy'}, dimensions={0}, use_global_device_ids=true | all-gather | bytes 278528 | tf_op jit(solution)/shard_map/while/body/eval_jaxpr/all_gather | solution.py:9
  92.5 2.7 while.180
  98.3 38.0 %all_gather.90 = f32[16,2,2,256]{3,2,1,0:T(2,128)S(1)} all-gather(f32[1,2,2,256]{3,2,1,0:T(2,128)S(1)} %slice_add_fusion.66), channel_id=1, replica_groups=mesh['gx'=2,'gy'=16] {'gy'}, dimensions={0}, use_global_device_ids=true | all-gather | bytes 69632 | tf_op jit(solution)/shard_map/while/body/eval_jaxpr/all_gather | solution.py:9
  136.3 36.8 %all_gather.91 = f32[16,8,2,256]{3,1,2,0:T(8,128)S(1)} all-gather(f32[1,8,2,256]{3,1,2,0:T(8,128)S(1)} %slice_add_fusion.67), channel_id=1, replica_groups=mesh['gx'=2,'gy'=16] {'gy'}, dimensions={0}, use_global_device_ids=true | all-gather | bytes 278528 | tf_op jit(solution)/shard_map/while/body/eval_jaxpr/all_gather | solution.py:9
  173.1 2.7 while.181
  175.9 1.3 collective-permute-start.1
  185.5 37.8 %all_gather.88 = f32[16,2,2,256]{3,2,1,0:T(2,128)S(1)} all-gather(f32[1,2,2,256]{3,2,1,0:T(2,128)S(1)} %slice_add_fusion.61), channel_id=1, replica_groups=mesh['gx'=2,'gy'=16] {'gy'}, dimensions={0}, use_global_device_ids=true | all-gather | bytes 69632 | tf_op jit(solution)/shard_map/while/body/eval_jaxpr/all_gather | solution.py:9
  223.7 37.0 %all_gather.89 = f32[16,8,2,256]{3,1,2,0:T(8,128)S(1)} all-gather(f32[1,8,2,256]{3,1,2,0:T(8,128)S(1)} %slice_add_fusion.62), channel_id=1, replica_groups=mesh['gx'=2,'gy'=16] {'gy'}, dimensions={0}, use_global_device_ids=true | all-gather | bytes 278528 | tf_op jit(solution)/shard_map/while/body/eval_jaxpr/all_gather | solution.py:9
  260.7 2.7 while.180
  266.5 37.7 %all_gather.90 = f32[16,2,2,256]{3,2,1,0:T(2,128)S(1)} all-gather(f32[1,2,2,256]{3,2,1,0:T(2,128)S(1)} %slice_add_fusion.66), channel_id=1, replica_groups=mesh['gx'=2,'gy'=16] {'gy'}, dimensions={0}, use_global_device_ids=true | all-gather | bytes 69632 | tf_op jit(solution)/shard_map/while/body/eval_jaxpr/all_gather | solution.py:9
  304.2 36.9 %all_gather.91 = f32[16,8,2,256]{3,1,2,0:T(8,128)S(1)} all-gather(f32[1,8,2,256]{3,1,2,0:T(8,128)S(1)} %slice_add_fusion.67), channel_id=1, replica_groups=mesh['gx'=2,'gy'=16] {'gy'}, dimensions={0}, use_global_device_ids=true | all-gather | bytes 278528 | tf_op jit(solution)/shard_map/while/body/eval_jaxpr/all_gather | solution.py:9
  341.1 2.7 while.181
  343.9 1.3 collective-permute-start.1
  347.3 338.0 %while.179 = (s32[]{:T(128)}, f32[1,16,8,2,256]{4,2,3,1,0:T(8,128)}, f32[16,8,2,256]{3,1,2,0:T(8,128)S(1)}, f32[1,16,8,2,256]{4,2,3,1,0:T(8,128)S(1)}, f32[1,16,...) while((s32[]{:T(128)}, f32[1,16,8,2,256]{4,2,3,1,0:T(8,128)}, ...), condition=%wide.region_11.12_spmd, body=%wide.region_6.11_spmd.sunk | while | flops 2625554 | bytes 27898876 | solution.py:128
  354.4 37.8 %all_gather.92 = f32[16,2,2,256]{3,2,1,0:T(2,128)S(1)} all-gather(f32[1,2,2,256]{3,2,1,0:T(2,128)S(1)} %slice_add_fusion.73), channel_id=1, replica_groups=mesh['gx'=2,'gy'=16] {'gy'}, dimensions={0}, use_global_device_ids=true | all-gather | bytes 69632 | tf_op jit(solution)/shard_map/while/body/eval_jaxpr/all_gather | solution.py:9
  392.6 37.0 %all_gather.93 = f32[16,8,2,256]{3,1,2,0:T(8,128)S(1)} all-gather(f32[1,8,2,256]{3,1,2,0:T(8,128)S(1)} %slice_add_fusion.74), channel_id=1, replica_groups=mesh['gx'=2,'gy'=16] {'gy'}, dimensions={0}, use_global_device_ids=true | all-gather | bytes 278528 | tf_op jit(solution)/shard_map/while/body/eval_jaxpr/all_gather | solution.py:9
  429.6 2.7 while.182
  435.4 37.7 %all_gather.94 = f32[16,2,2,256]{3,2,1,0:T(2,128)S(1)} all-gather(f32[1,2,2,256]{3,2,1,0:T(2,128)S(1)} %slice_add_fusion.78), channel_id=1, replica_groups=mesh['gx'=2,'gy'=16] {'gy'}, dimensions={0}, use_global_device_ids=true | all-gather | bytes 69632 | tf_op jit(solution)/shard_map/while/body/eval_jaxpr/all_gather | solution.py:9
  473.1 36.9 %all_gather.95 = f32[16,8,2,256]{3,1,2,0:T(8,128)S(1)} all-gather(f32[1,8,2,256]{3,1,2,0:T(8,128)S(1)} %slice_add_fusion.79), channel_id=1, replica_groups=mesh['gx'=2,'gy'=16] {'gy'}, dimensions={0}, use_global_device_ids=true | all-gather | bytes 278528 | tf_op jit(solution)/shard_map/while/body/eval_jaxpr/all_gather | solution.py:9
  510.0 2.7 while.183
  512.9 1.3 collective-permute-start
  514.2 2.1 collective-permute-done
  523.4 37.8 %all_gather.92 = f32[16,2,2,256]{3,2,1,0:T(2,128)S(1)} all-gather(f32[1,2,2,256]{3,2,1,0:T(2,128)S(1)} %slice_add_fusion.73), channel_id=1, replica_groups=mesh['gx'=2,'gy'=16] {'gy'}, dimensions={0}, use_global_device_ids=true | all-gather | bytes 69632 | tf_op jit(solution)/shard_map/while/body/eval_jaxpr/all_gather | solution.py:9
  561.7 37.0 %all_gather.93 = f32[16,8,2,256]{3,1,2,0:T(8,128)S(1)} all-gather(f32[1,8,2,256]{3,1,2,0:T(8,128)S(1)} %slice_add_fusion.74), channel_id=1, replica_groups=mesh['gx'=2,'gy'=16] {'gy'}, dimensions={0}, use_global_device_ids=true | all-gather | bytes 278528 | tf_op jit(solution)/shard_map/while/body/eval_jaxpr/all_gather | solution.py:9
  598.6 2.7 while.182
  604.4 37.7 %all_gather.94 = f32[16,2,2,256]{3,2,1,0:T(2,128)S(1)} all-gather(f32[1,2,2,256]{3,2,1,0:T(2,128)S(1)} %slice_add_fusion.78), channel_id=1, replica_groups=mesh['gx'=2,'gy'=16] {'gy'}, dimensions={0}, use_global_device_ids=true | all-gather | bytes 69632 | tf_op jit(solution)/shard_map/while/body/eval_jaxpr/all_gather | solution.py:9
  642.1 36.9 %all_gather.95 = f32[16,8,2,256]{3,1,2,0:T(8,128)S(1)} all-gather(f32[1,8,2,256]{3,1,2,0:T(8,128)S(1)} %slice_add_fusion.79), channel_id=1, replica_groups=mesh['gx'=2,'gy'=16] {'gy'}, dimensions={0}, use_global_device_ids=true | all-gather | bytes 278528 | tf_op jit(solution)/shard_map/while/body/eval_jaxpr/all_gather | solution.py:9
  679.0 2.7 while.183
  683.2 2.1 collective-permute-done
  685.3 1.8 copy.38
  (1957 shorter events, 57.9 us)
Async XLA Ops:
  0.0 0.9 copy-start.10
  0.9 0.8 copy-start.11
  1.8 0.8 copy-start.9
  2.7 0.8 copy-start.12
  2.7 0.9 copy-start.13
  3.6 0.9 copy-start.8
  6.7 0.7 slice-start.2
  8.4 0.6 copy-start.4
  9.5 0.7 slice-start.3
  95.3 0.7 copy-start
  97.0 0.7 slice-start
  175.9 2.4 collective-permute-start.1
  179.8 0.7 slice-start.2
  182.6 0.7 slice-start.3
  263.5 0.7 copy-start
  265.2 0.7 slice-start
  343.9 2.4 collective-permute-start.1
  346.4 0.9 copy-start.2
  348.7 0.7 slice-start.4
  351.6 0.7 slice-start.5
  432.4 0.7 copy-start.1
  434.1 0.7 slice-start.1
  512.9 3.4 copy-start.7
  512.9 3.4 collective-permute-start
  516.5 0.6 copy-start.5
  517.7 0.7 slice-start.4
  519.4 0.6 copy-start.6
  520.6 0.7 slice-start.5
  601.4 0.7 copy-start.1
  603.1 0.7 slice-start.1
  681.9 3.4 copy-start.7
  681.9 3.4 collective-permute-start
  (5 other events, 3.1 us)
where the time goes:
time: 688 us; the launch traced here: 687 us
  blocking collectives  603 us (88%)
  local copies, waits for them, and re-layouts  45 us (7%)
  loops' own time  16.5 us (2%)
  other arithmetic  12.6 us (2%)
    all_gather x16, blocking collectives, entering(): everything = jax.tree.map(lambda part: lax.all_gather(part, axis), x)  603 us
  transfers between devices with their start and end apart: 4, of which 4 were waited for; matrix products, arithmetic and copies ran while one was open for 0% of the time, Pallas kernels for 0%

commit v1 on v0

v1 whole, which is shorter than its diff:
```python
import functools

import jax
import jax.numpy as jnp
from jax import lax
from jax.experimental import pallas as pl
from jax.experimental.pallas import tpu as pltpu
from jax.sharding import PartitionSpec as P

CHAINS = ((0, 0), (1, 0), (0, 1), (1, 1), (0, 2), (1, 2))
T1, U1, T2, U2, T3, U3 = range(6)
UNITS = 4
VMEM = pl.BlockSpec(memory_space=pltpu.VMEM)
ANY = pl.BlockSpec(memory_space=pl.ANY)
HBM = pl.BlockSpec(memory_space=pltpu.HBM)


def spot(chain):
    direction, number = CHAINS[chain]
    return 3 * direction + number


def feeds(chain):
    return range(min(chain + 1, UNITS))


def spread(ref, row, count):
    return ref[pl.ds(row, count, stride=0), :]


def call(kernel, name, outs, ins, scratch=(), specs=None, out_specs=None):
    return pl.pallas_call(
        kernel,
        name=name,
        out_shape=[jax.ShapeDtypeStruct(s, jnp.float32) for s in outs],
        in_specs=specs or [VMEM] * len(ins),
        out_specs=out_specs or [VMEM] * len(outs),
        scratch_shapes=list(scratch),
        compiler_params=pltpu.CompilerParams(vmem_limit_bytes=8 << 20),
    )(*ins)


def pack_kernel(half, vectors, krylov, inverse, back, front, left, right, keep, send, sems):
    core = lax.axis_index("gx")
    base = (0, vectors, vectors + 2, vectors + 4, vectors + 6)

    def copies(ref, position, target, number):
        lanes = pl.ds(pl.multiple_of(position * half, half), half)
        size = ref.shape[2]
        return pltpu.make_async_copy(
            ref.at[0, :, :, :, lanes],
            target.at[:, pl.ds(base[number], size)],
            sems.at[number, 0 if target is keep else 1],
        )

    fixed = (krylov, inverse, left, right)
    plan = [
        copies(ref, position, target, number)
        for target, position in ((send, 1 - core), (keep, core))
        for number, ref in enumerate(fixed)
    ]
    for copy in plan:
        copy.start()
    for own, ref in ((0, front), (1, back)):

        @pl.when(core == own)
        def _():
            pair = [copies(ref, 1 - core, send, 4), copies(ref, core, keep, 4)]
            for copy in pair:
                copy.start()
            for copy in pair:
                copy.wait()

    for copy in plan:
        copy.wait()


def local_kernel(lines, vectors, keep, recv, edge, first, second, low, data, maps):
    core = lax.axis_index("gx")
    pitch = 2 * vectors + 16
    rows = lines * pitch
    width = vectors + 2 * UNITS
    mine, other = keep[...], recv[...]
    data[pl.ds(0, rows), :] = jnp.where(core == 0, mine, other)
    data[pl.ds(rows, rows), :] = jnp.where(core == 0, other, mine)

    def block(plane, number):
        start = plane * rows + 2 * vectors + 4 * number
        return [[data[pl.ds(start + 2 * a + b, lines, stride=pitch), :] for b in (0, 1)] for a in (0, 1)]

    def keep_map(number, left, right):
        for a in (0, 1):
            for b in (0, 1):
                value = -(left[a][0] * right[0][b] + left[a][1] * right[1][b])
                maps[pl.ds((4 * number + 2 * a + b) * lines, lines), :] = value

    for plane in (0, 1):
        inverse = block(plane, 0)
        keep_map(2 * plane, inverse, block(plane, 1))
        keep_map(2 * plane + 1, inverse, block(plane, 2))
        keep_map(4 + plane, inverse, block(plane, 3))

    def product(ref, place, state):
        out = []
        for a in (0, 1):
            left, right = (spread(ref, place(a, b), 8) for b in (0, 1))
            out.append([left * x + right * y for x, y in zip(state[0], state[1])])
        return out

    def mapped(number, line, state):
        return product(maps, lambda a, b: (4 * number + 2 * a + b) * lines + line, state)

    def add(x, y):
        return [[p + q for p, q in zip(s, t)] for s, t in zip(x, y)]

    row = lax.broadcasted_iota(jnp.int32, (8, 128), 0)
    none = jnp.zeros((8, 128), jnp.float32)

    def unit(chain):
        one = [jnp.where(row == 2 * chain + a, 1.0, 0.0) for a in (0, 1)] if chain < UNITS else [none, none]
        return [[none, one[a]] for a in (0, 1)]

    def scaled(plane, line):
        start = plane * rows + line * pitch
        source = [[data[pl.ds(start + a, vectors, stride=2), :]] for a in (0, 1)]
        got = product(data, lambda a, b: start + 2 * vectors + 2 * a + b, source)
        return [[s[0], none] for s in got]

    def leave(chain, state):
        for a in (0, 1):
            for half in (0, 1):
                edge[pl.ds((2 * spot(chain) + a) * width + half * 8, 8), :] = state[a][half]

    def solve(plane, chain, source):
        state, states = unit(chain), []
        for line in range(lines):
            state = add(source(line), mapped(2 * plane, line, state))
            states.append(state)
        leave(chain, state)
        state, result = unit(chain + 1), [None] * lines
        for line in reversed(range(lines)):
            state = add(states[line], mapped(2 * plane + 1, line, state))
            result[line] = state
        leave(chain + 1, state)
        return result

    swept_low = solve(0, T1, lambda line: scaled(0, line))
    for line in range(lines):
        for a in (0, 1):
            low[pl.ds((2 * line + a) * 8, 8), :] = swept_low[line][a][1]
    swept_high = solve(1, T2, lambda line: add(scaled(1, line), mapped(5, line, swept_low[line])))
    fixed = solve(0, T3, lambda line: mapped(4, line, swept_high[line]))
    for line in range(lines):
        total = add(swept_low[line], fixed[line])
        for a in (0, 1):
            for half in (0, 1):
                place = pl.ds((2 * line + a) * width + half * 8, 8)
                first[place, :] = total[a][half]
                second[place, :] = swept_high[line][a][half]


def response(ref, width, to, frm, state, start=0):
    if frm >= UNITS:
        to, frm = to - UNITS, frm - UNITS
    out = []
    for a in (0, 1):
        row = (2 * (spot(to) - start) + a) * width + width - 2 * UNITS + 2 * frm
        left, right = spread(ref, row, 8), spread(ref, row + 1, 8)
        out.append([left * x + right * y for x, y in zip(state[0], state[1])])
    return out


def total(first, *others):
    for other in others:
        first = [[p + q for p, q in zip(s, t)] for s, t in zip(first, other)]
    return first


def merge_kernel(bit, width, last, mine, other, edge, mids, lower, upper):
    is_low = jnp.bitwise_and(lax.axis_index("gy"), bit) == 0
    x, y = mine[...], other[...]
    lower[...] = jnp.where(is_low, x, y)
    upper[...] = jnp.where(is_low, y, x)
    row = lax.broadcasted_iota(jnp.int32, (8, 128), 0)
    up = jnp.bitwise_and(row, 2) == 0

    def base(ref, chain, keep_up):
        out = []
        for a in (0, 1):
            start = (2 * spot(chain) + a) * width
            units = ref[pl.ds(start + 8, 8), :]
            out.append([ref[pl.ds(start, 8), :], jnp.where(up if keep_up else ~up, units, 0.0)])
        return out

    low = functools.partial(response, lower, width)
    high = functools.partial(response, upper, width)
    m = [None] * 6
    m[T1] = base(lower, T1, True)
    m[U1] = total(base(upper, U1, False), high(U1, T1, m[T1]))
    m[T2] = total(base(lower, T2, True), low(T2, U1, m[U1]))
    m[U2] = total(base(upper, U2, False), high(U2, T1, m[T1]), high(U2, T2, m[T2]))
    m[T3] = total(base(lower, T3, True), low(T3, U1, m[U1]), low(T3, U2, m[U2]))
    m[U3] = total(base(upper, U3, False), high(U3, T1, m[T1]), high(U3, T2, m[T2]), high(U3, T3, m[T3]))
    e = [None] * 6
    for chain in range(6):
        ref, of = (upper, high) if CHAINS[chain][0] == 0 else (lower, low)
        through = [c for c in range(chain + 1) if CHAINS[c][0] == CHAINS[chain][0]]
        e[chain] = total(base(ref, chain, CHAINS[chain][0] == 1), *(of(chain, c, m[c]) for c in through))
    next_low = jnp.bitwise_and(lax.axis_index("gy"), 2 * bit) == 0
    for chain in range(6):
        for a in (0, 1):
            for half in (0, 1):
                place = (2 * spot(chain) + a) * width + 8 * half
                mids[pl.ds(place, 8), :] = m[chain][a][half]
                if not last:
                    edge[pl.ds(place, 8), :] = e[chain][a][half]
                elif chain % 2 == 0:
                    edge[pl.ds(place, 8), :] = jnp.where(next_low, e[chain][a][half], e[chain + 1][a][half])


def finish_kernel(lines, levels, width, mine, other, *refs):
    mids, (first, second, low, kept, sent, ups, downs) = refs[: levels - 1], refs[levels - 1 :]
    core, place = lax.axis_index("gx"), lax.axis_index("gy")
    is_low = jnp.bitwise_and(place, 1 << (levels - 1)) == 0
    x, y = mine[...], other[...]
    ups[...] = jnp.where(is_low, x, y)
    downs[...] = jnp.where(is_low, y, x)

    def base(ref, chain, start):
        return [[ref[pl.ds((2 * (spot(chain) - start) + a) * width, 8), :]] for a in (0, 1)]

    def up(to, frm, state):
        return response(ups, width, to, frm, state)

    def down(to, frm, state):
        return response(downs, width, to, frm, state, 3)

    m = [None] * 6
    m[T1] = base(ups, T1, 0)
    m[U1] = total(base(downs, U1, 3), down(U1, T1, m[T1]))
    m[T2] = total(base(ups, T2, 0), up(T2, U1, m[U1]))
    m[U2] = total(base(downs, U2, 3), down(U2, T1, m[T1]), down(U2, T2, m[T2]))
    m[T3] = total(base(ups, T3, 0), up(T3, U1, m[U1]), up(T3, U2, m[U2]))
    m[U3] = total(base(downs, U3, 3), down(U3, T1, m[T1]), down(U3, T2, m[T2]), down(U3, T3, m[T3]))

    def select(condition, x, y):
        return [[jnp.where(condition, p, q) for p, q in zip(s, t)] for s, t in zip(x, y)]

    none = [[jnp.zeros((8, 128), jnp.float32)], [jnp.zeros((8, 128), jnp.float32)]]
    enters = [none] * 6
    for level in reversed(range(levels)):
        if level < levels - 1:
            ref = mids[level]
            m = []
            for chain in range(6):
                terms = [response(ref, width, chain, c, enters[c]) for c in feeds(chain)]
                if chain >= UNITS:
                    terms += [response(ref, width, chain, c, enters[c]) for c in range(UNITS, chain + 1)]
                m.append(total(base(ref, chain, 0), *terms))
        is_low = jnp.bitwise_and(place, 1 << level) == 0
        enters = [
            select(is_low, enters[c], m[c]) if CHAINS[c][0] == 0 else select(is_low, m[c], enters[c])
            for c in range(6)
        ]

    def columns(ref, start, chains):
        value = None
        for place_of, chain in chains:
            for b in (0, 1):
                term = spread(ref, start + 2 * place_of + b, 8) * enters[chain][b][0]
                value = term if value is None else value + term
        return value

    for line in range(lines):
        for a in (0, 1):
            start = (2 * line + a) * width
            units = [(c, c) for c in range(UNITS)]
            high = second[pl.ds(start, 8), :] + columns(second, start + 8, units)
            own = first[pl.ds(start, 8), :] + columns(first, start + 8, units)
            own = own + columns(low, (2 * line + a) * 8, [(T1, T3), (U1, U3)])
            target = pl.ds(line * 16 + a, 8, stride=2)
            kept[target, :] = jnp.where(core == 0, own, high)
            sent[target, :] = jnp.where(core == 0, high, own)


def unpack_kernel(half, kept, got, out, sems):
    core = lax.axis_index("gx")
    plan = []
    for number, (ref, position) in enumerate(((kept, core), (got, 1 - core))):
        lanes = pl.ds(pl.multiple_of(position * half, half), half)
        plan.append(pltpu.make_async_copy(ref, out.at[0, :, :, :, lanes], sems.at[number]))
    for copy in plan:
        copy.start()
    for copy in plan:
        copy.wait()


def per_device(krylov, inverse, back, front, left, right):
    _, lines, vectors, _, cells = krylov.shape
    count = lax.axis_size("gy")
    levels = count.bit_length() - 1
    half = cells // 2
    width = vectors + 2 * UNITS
    assert lax.axis_size("gx") == 2 and count == 1 << levels and levels > 1
    assert vectors == 8 and half == 128
    swap = [(0, 1), (1, 0)]

    slots = vectors + 8
    keep, send = call(
        functools.partial(pack_kernel, half, vectors),
        "pack",
        [(lines, slots, 2, half)] * 2,
        [pltpu.with_memory_space_constraint(x, pltpu.HBM) for x in (krylov, inverse, back, front, left, right)],
        [pltpu.SemaphoreType.DMA((5, 2))],
        specs=[HBM] * 6,
    )
    recv = lax.ppermute(send.reshape(-1, half), "gx", swap)
    keep = keep.reshape(-1, half)
    edge, first, second, low = call(
        functools.partial(local_kernel, lines, vectors),
        "local",
        [(12 * width, half), (2 * lines * width, half), (2 * lines * width, half), (2 * lines * 8, half)],
        (keep, recv),
        [pltpu.VMEM((2 * keep.shape[0], half), jnp.float32), pltpu.VMEM((24 * lines, half), jnp.float32)],
    )
    mids = []
    for level in range(levels - 1):
        got = lax.ppermute(edge, "gy", [(j, j ^ (1 << level)) for j in range(count)])
        last = level == levels - 2
        edge, mid = call(
            functools.partial(merge_kernel, 1 << level, width, last),
            f"merge{level}",
            [((6 if last else 12) * width, half), (12 * width, half)],
            (edge, got),
            [pltpu.VMEM((12 * width, half), jnp.float32)] * 2,
        )
        mids.append(mid)
    got = lax.ppermute(edge, "gy", [(j, j ^ (count // 2)) for j in range(count)])
    kept, sent = call(
        functools.partial(finish_kernel, lines, levels, width),
        "finish",
        [(lines * 16, half)] * 2,
        (edge, got, *mids, first, second, low),
        [pltpu.VMEM((6 * width, half), jnp.float32)] * 2,
    )
    got = lax.ppermute(sent, "gx", swap)
    (out,) = call(
        functools.partial(unpack_kernel, half),
        "unpack",
        [krylov.shape],
        [x.reshape(lines, vectors, 2, half) for x in (kept, got)],
        [pltpu.SemaphoreType.DMA((2,))],
        specs=[ANY] * 2,
        out_specs=[HBM],
    )
    return out


def solution(mesh):
    spec = P("gx", "gy", None, None, None)
    return jax.shard_map(
        per_device, mesh=mesh, in_specs=(spec,) * 6, out_specs=spec, check_vma=False
    )
```

time: 688 us -> 26.9 us (0.04)
  blocking collectives: 603 us -> 0 us
  local copies, waits for them, and re-layouts: 45 us -> 0 us
  loops' own time: 16.5 us -> 0 us
  other arithmetic: 12.6 us -> 0 us
  waiting for transfers between devices: 5.01 us -> 13.3 us
    all_gather x16 -> x0, blocking collectives: 603 us -> none  [entering(): everything = jax.tree.map(lambda part: lax.all_gather(part, axis), x)]
    another operation x10 -> x0, loops' own time: 16.5 us -> none  [the longest x8 9.4 us: entering(): return lax.fori_loop(0, size, step, start)]
    slice x533 -> x0, local copies, waits for them, and re-layouts: 14.6 us -> none  [the longest x64 5.69 us: solve_plane(): lax.associative_scan(compose, (backward_maps, forward_state), reverse=True)]
    while x385 -> x0, local copies, waits for them, and re-layouts: 12.2 us -> none
    pad x96 -> x0, local copies, waits for them, and re-layouts: 10.6 us -> none  [the longest x48 5.3 us: solve_plane(): matrices, offsets = lax.associative_scan(compose, (forward_maps, scaled))]
    ppermute x4 -> x6, waiting for transfers between devices: 5.01 us -> 13.3 us  [the longest x3 8.73 us: per_device(): got = lax.ppermute(edge, 'gy', [(j, j ^ 1 << level) for j in range(count)])]
  transfers between devices with their start and end apart: 4 -> 6, of which waited for: 4 -> 6; matrix products, arithmetic and copies ran while one was open for 0% -> 0% of each run, Pallas kernels for 0% -> 0%
where the time goes in v1:
time: 26.9 us; the launch traced here: 26.8 us
  waiting for transfers between devices  13.3 us (49%)
  starting transfers between devices  10.6 us (39%)
  Pallas kernels  2.88 us (11%)
    ppermute x3, waiting for transfers between devices, per_device(): got = lax.ppermute(edge, 'gy', [(j, j ^ 1 << level) for j in range(count)])  8.73 us
    ppermute x3, starting transfers between devices, per_device(): got = lax.ppermute(edge, 'gy', [(j, j ^ 1 << level) for j in range(count)])  6.64 us
    ppermute x1, starting transfers between devices, per_device(): got = lax.ppermute(edge, 'gy', [(j, j ^ count // 2) for j in range(count)])  3.29 us
    pallas_call x7, Pallas kernels, call(): pl.pallas_call(kernel, name=name, out_shape=[jax.ShapeDtypeStruct(s, jnp....  2.88 us
    ppermute x1, waiting for transfers between devices, per_device(): got = lax.ppermute(edge, 'gy', [(j, j ^ count // 2) for j in range(count)])  2.07 us
    ppermute x1, waiting for transfers between devices, per_device(): got = lax.ppermute(sent, 'gx', swap)  1.33 us
    ppermute x1, waiting for transfers between devices, per_device(): recv = lax.ppermute(send.reshape(-1, half), 'gx', swap)  1.16 us
    ppermute x1, starting transfers between devices, per_device(): recv = lax.ppermute(send.reshape(-1, half), 'gx', swap)  0.56 us
  transfers between devices with their start and end apart: 6, of which 6 were waited for; matrix products, arithmetic and copies ran while one was open for 0% of the time, Pallas kernels for 0%

profile of v1, /device:TPU:0, one launch (start us, length us, event | category | flops | bytes accessed | tf_op | source)
XLA Modules:
  0.0 26.8 jit_solution(4365593502200792800)
XLA Ops:
  0.0 1.1 %pack.1 = (f32[16,16,2,128]{3,2,1,0:T(2,128)S(1)}, f32[16,16,2,128]{3,2,1,0:T(2,128)S(1)}) custom-call(f32[1,16,8,2,256]{4,3,2,1,0:T(2,128)} %krylov.1, f32[1,16,2,2,256]{4,3,2,1,0:T(2,128)} %inverse.1, f32[1,16,2,2,256]{4,3,2,1,0:T(2,128)} %back.1, f32[1,16,2,2,256]{4,3,2,1,0:T(2,128)} %front.1, f32[1,16,2,2,256]{4,3,2,1,0:T(2,128)} %left.1, ...), custom_call_target="tpu_custom_call" | custom-call | tf_op jit(solution)/shard_map/pack/pallas_call | solution.py:32
  1.1 0.6 %collective-permute-start = (f32[512,128]{1,0:T(8,128)S(1)}, f32[512,128]{1,0:T(8,128)S(1)}, u32[]{:S(2)}, u32[]{:S(2)}) collective-permute-start(f32[512,128]{1,0:T(8,128)S(1)} %bitcast.7), channel_id=1, source_target_pairs={{0,16},{16,0},{1,17},{17,1},{2,18},{18,2},{3,19},{19,3},{4,20},{20... | collective-permute-start | bytes 786440 | tf_op jit(solution)/shard_map/ppermute | solution.py:317
  1.7 1.2 %collective-permute-done.recv = f32[512,128]{1,0:T(8,128)S(1)} collective-permute-done((f32[512,128]{1,0:T(8,128)S(1)}, f32[512,128]{1,0:T(8,128)S(1)}, u32[]{:S(2)}, u32[]{:S(2)}) %collective-permute-start) | collective-permute-done | bytes 262176 | tf_op jit(solution)/shard_map/ppermute | solution.py:317
  2.8 0.5 %local.1 = (f32[192,128]{1,0:T(8,128)S(1)}, f32[512,128]{1,0:T(8,128)S(1)}, f32[512,128]{1,0:T(8,128)S(1)}, f32[256,128]{1,0:T(8,128)S(1)}) custom-call(f32[512,128]{1,0:T(8,128)S(1)} %bitcast.4, f32[512,128]{1,0:T(8,128)S(1)} %collective-permute-done.recv), custom_call_target="tpu_custom_call" | custom-call | tf_op jit(solution)/shard_map/local/pallas_call | solution.py:32
  3.4 2.9 %collective-permute-start.1 = (f32[192,128]{1,0:T(8,128)S(1)}, f32[192,128]{1,0:T(8,128)S(1)}, u32[]{:S(2)}, u32[]{:S(2)}) collective-permute-start(f32[192,128]{1,0:T(8,128)S(1)} %get-tuple-element.21.mine), channel_id=1, source_target_pairs={{0,1},{1,0},{2,3},{3,2},{4,5},{5,4},{6,7},{7,6},{8,9},{9,8},{10,11... | collective-permute-start | bytes 294920 | tf_op jit(solution)/shard_map/ppermute | solution.py:328
  6.3 3.1 %collective-permute-done.1.other = f32[192,128]{1,0:T(8,128)S(1)} collective-permute-done((f32[192,128]{1,0:T(8,128)S(1)}, f32[192,128]{1,0:T(8,128)S(1)}, u32[]{:S(2)}, u32[]{:S(2)}) %collective-permute-start.1) | collective-permute-done | bytes 98336 | tf_op jit(solution)/shard_map/ppermute | solution.py:328
  9.4 0.1 merge0.1
  9.5 1.8 %collective-permute-start.2 = (f32[192,128]{1,0:T(8,128)S(1)}, f32[192,128]{1,0:T(8,128)S(1)}, u32[]{:S(2)}, u32[]{:S(2)}) collective-permute-start(f32[192,128]{1,0:T(8,128)S(1)} %get-tuple-element.22.mine), channel_id=1, source_target_pairs={{0,2},{1,3},{2,0},{3,1},{4,6},{5,7},{6,4},{7,5},{8,10},{9,11},{10,... | collective-permute-start | bytes 294920 | tf_op jit(solution)/shard_map/ppermute | solution.py:328
  11.3 2.8 %collective-permute-done.2.other = f32[192,128]{1,0:T(8,128)S(1)} collective-permute-done((f32[192,128]{1,0:T(8,128)S(1)}, f32[192,128]{1,0:T(8,128)S(1)}, u32[]{:S(2)}, u32[]{:S(2)}) %collective-permute-start.2) | collective-permute-done | bytes 98336 | tf_op jit(solution)/shard_map/ppermute | solution.py:328
  14.2 0.1 merge1.1
  14.2 1.9 %collective-permute-start.3 = (f32[192,128]{1,0:T(8,128)S(1)}, f32[192,128]{1,0:T(8,128)S(1)}, u32[]{:S(2)}, u32[]{:S(2)}) collective-permute-start(f32[192,128]{1,0:T(8,128)S(1)} %get-tuple-element.23.mine), channel_id=1, source_target_pairs={{0,4},{1,5},{2,6},{3,7},{4,0},{5,1},{6,2},{7,3},{8,12},{9,13},{10,... | collective-permute-start | bytes 294920 | tf_op jit(solution)/shard_map/ppermute | solution.py:328
  16.1 2.8 %collective-permute-done.3.other = f32[192,128]{1,0:T(8,128)S(1)} collective-permute-done((f32[192,128]{1,0:T(8,128)S(1)}, f32[192,128]{1,0:T(8,128)S(1)}, u32[]{:S(2)}, u32[]{:S(2)}) %collective-permute-start.3) | collective-permute-done | bytes 98336 | tf_op jit(solution)/shard_map/ppermute | solution.py:328
  18.9 0.1 merge2.1
  19.0 3.3 %collective-permute-start.4 = (f32[96,128]{1,0:T(8,128)S(1)}, f32[96,128]{1,0:T(8,128)S(1)}, u32[]{:S(2)}, u32[]{:S(2)}) collective-permute-start(f32[96,128]{1,0:T(8,128)S(1)} %get-tuple-element.24.mine), channel_id=1, source_target_pairs={{0,8},{1,9},{2,10},{3,11},{4,12},{5,13},{6,14},{7,15},{8,0},{9,1},... | collective-permute-start | bytes 147464 | tf_op jit(solution)/shard_map/ppermute | solution.py:338
  22.3 2.1 %collective-permute-done.4.other = f32[96,128]{1,0:T(8,128)S(1)} collective-permute-done((f32[96,128]{1,0:T(8,128)S(1)}, f32[96,128]{1,0:T(8,128)S(1)}, u32[]{:S(2)}, u32[]{:S(2)}) %collective-permute-start.4) | collective-permute-done | bytes 49184 | tf_op jit(solution)/shard_map/ppermute | solution.py:338
  24.4 0.3 %finish.1 = (f32[256,128]{1,0:T(8,128)S(1)}, f32[256,128]{1,0:T(8,128)S(1)}) custom-call(f32[96,128]{1,0:T(8,128)S(1)} %get-tuple-element.24.mine, f32[96,128]{1,0:T(8,128)S(1)} %collective-permute-done.4.other, f32[192,128]{1,0:T(8,128)S(1)} %get-tuple-element.25.refs_0_, f32[192,128]{1,0:T(8,128)S(1)} %get-tuple-element.26.refs_1_, ...), custom_call_target="tpu_custom_call" | custom-call | tf_op jit(solution)/shard_map/finish/pallas_call | solution.py:32
  24.6 0.1 collective-permute-start.5
  24.7 1.3 %collective-permute-done.5 = f32[256,128]{1,0:T(8,128)S(1)} collective-permute-done((f32[256,128]{1,0:T(8,128)S(1)}, f32[256,128]{1,0:T(8,128)S(1)}, u32[]{:S(2)}, u32[]{:S(2)}) %collective-permute-start.5) | collective-permute-done | bytes 131104 | tf_op jit(solution)/shard_map/ppermute | solution.py:346
  26.1 0.7 %unpack.1 = f32[1,16,8,2,256]{4,3,2,1,0:T(2,128)} custom-call(f32[16,8,2,128]{3,2,1,0:T(2,128)S(1)} %bitcast.5, f32[16,8,2,128]{3,2,1,0:T(2,128)S(1)} %bitcast.6), custom_call_target="tpu_custom_call" | custom-call | tf_op jit(solution)/shard_map/unpack/pallas_call | solution.py:32
Async XLA Ops:
  1.1 1.7 %collective-permute-start = (f32[512,128]{1,0:T(8,128)S(1)}, f32[512,128]{1,0:T(8,128)S(1)}, u32[]{:S(2)}, u32[]{:S(2)}) collective-permute-start(f32[512,128]{1,0:T(8,128)S(1)} %bitcast.7), channel_id=1, source_target_pairs={{0,16},{16,0},{1,17},{17,1},{2,18},{18,2},{3,19},{19,3},{4,20},{20... | collective-permute-start | bytes 786440 | tf_op jit(solution)/shard_map/ppermute | solution.py:317
  3.4 6.0 %collective-permute-start.1 = (f32[192,128]{1,0:T(8,128)S(1)}, f32[192,128]{1,0:T(8,128)S(1)}, u32[]{:S(2)}, u32[]{:S(2)}) collective-permute-start(f32[192,128]{1,0:T(8,128)S(1)} %get-tuple-element.21.mine), channel_id=1, source_target_pairs={{0,1},{1,0},{2,3},{3,2},{4,5},{5,4},{6,7},{7,6},{8,9},{9,8},{10,11... | collective-permute-start | bytes 294920 | tf_op jit(solution)/shard_map/ppermute | solution.py:328
  9.5 4.7 %collective-permute-start.2 = (f32[192,128]{1,0:T(8,128)S(1)}, f32[192,128]{1,0:T(8,128)S(1)}, u32[]{:S(2)}, u32[]{:S(2)}) collective-permute-start(f32[192,128]{1,0:T(8,128)S(1)} %get-tuple-element.22.mine), channel_id=1, source_target_pairs={{0,2},{1,3},{2,0},{3,1},{4,6},{5,7},{6,4},{7,5},{8,10},{9,11},{10,... | collective-permute-start | bytes 294920 | tf_op jit(solution)/shard_map/ppermute | solution.py:328
  14.2 4.7 %collective-permute-start.3 = (f32[192,128]{1,0:T(8,128)S(1)}, f32[192,128]{1,0:T(8,128)S(1)}, u32[]{:S(2)}, u32[]{:S(2)}) collective-permute-start(f32[192,128]{1,0:T(8,128)S(1)} %get-tuple-element.23.mine), channel_id=1, source_target_pairs={{0,4},{1,5},{2,6},{3,7},{4,0},{5,1},{6,2},{7,3},{8,12},{9,13},{10,... | collective-permute-start | bytes 294920 | tf_op jit(solution)/shard_map/ppermute | solution.py:328
  19.0 5.4 %collective-permute-start.4 = (f32[96,128]{1,0:T(8,128)S(1)}, f32[96,128]{1,0:T(8,128)S(1)}, u32[]{:S(2)}, u32[]{:S(2)}) collective-permute-start(f32[96,128]{1,0:T(8,128)S(1)} %get-tuple-element.24.mine), channel_id=1, source_target_pairs={{0,8},{1,9},{2,10},{3,11},{4,12},{5,13},{6,14},{7,15},{8,0},{9,1},... | collective-permute-start | bytes 147464 | tf_op jit(solution)/shard_map/ppermute | solution.py:338
  24.6 1.4 %collective-permute-start.5 = (f32[256,128]{1,0:T(8,128)S(1)}, f32[256,128]{1,0:T(8,128)S(1)}, u32[]{:S(2)}, u32[]{:S(2)}) collective-permute-start(f32[256,128]{1,0:T(8,128)S(1)} %get-tuple-element.32), channel_id=1, source_target_pairs={{0,16},{16,0},{1,17},{17,1},{2,18},{18,2},{3,19},{19,3},{4,20},{20... | collective-permute-start | bytes 393224 | tf_op jit(solution)/shard_map/ppermute | solution.py:346

commit v2 on v1

--- a/solution.py
+++ b/solution.py
@@ -22,6 +22,43 @@
 
 def feeds(chain):
     return range(min(chain + 1, UNITS))
+
+
+UNIT_START = {U1: (0, 4), T2: (8, 8), T1: (14, 8), U2: (24, 8), T3: (40, 8), U3: (56, 8)}
+VECTOR_ROWS = 96
+ROWS = VECTOR_ROWS + 72
+UP_ROWS = {(T2, U1): (0, 2), (T3, U1): (4, 4), (T3, U2): (6, 4)}
+DOWN_ROWS = {(U1, T1): (0, 2), (U2, T1): (4, 4), (U2, T2): (6, 4), (U3, T1): (12, 4), (U3, T2): (14, 4)}
+LAST_UNITS = 24
+LAST_ROWS = VECTOR_ROWS // 2 + LAST_UNITS
+
+
+def vector_row(chain, a):
+    return (2 * spot(chain) + a) * 8
+
+
+def unit_row(chain, a):
+    start, step = UNIT_START[chain]
+    return VECTOR_ROWS + start + step * a
+
+
+def unit_count(chain):
+    return 2 * len(feeds(chain))
+
+
+def half_of():
+    top = lax.axis_size("gy") // 2
+    flip = jnp.where(jnp.bitwise_and(lax.axis_index("gy"), top) == 0, 0, 1)
+    return jnp.bitwise_xor(lax.axis_index("gx"), flip)
+
+
+def keep_record(ref, values):
+    for chain in range(6):
+        for a in (0, 1):
+            carries, units = values[chain][a]
+            ref[pl.ds(vector_row(chain, a), 8), :] = carries
+            count = unit_count(chain)
+            ref[pl.ds(unit_row(chain, a), count), :] = units[:count]
 
 
 def spread(ref, row, count):
@@ -41,7 +78,7 @@
 
 
 def pack_kernel(half, vectors, krylov, inverse, back, front, left, right, keep, send, sems):
-    core = lax.axis_index("gx")
+    core, part = lax.axis_index("gx"), half_of()
     base = (0, vectors, vectors + 2, vectors + 4, vectors + 6)
 
     def copies(ref, position, target, number):
@@ -56,7 +93,7 @@
     fixed = (krylov, inverse, left, right)
     plan = [
         copies(ref, position, target, number)
-        for target, position in ((send, 1 - core), (keep, core))
+        for target, position in ((send, 1 - part), (keep, part))
         for number, ref in enumerate(fixed)
     ]
     for copy in plan:
@@ -65,7 +102,7 @@
 
         @pl.when(core == own)
         def _():
-            pair = [copies(ref, 1 - core, send, 4), copies(ref, core, keep, 4)]
+            pair = [copies(ref, 1 - part, send, 4), copies(ref, part, keep, 4)]
             for copy in pair:
                 copy.start()
             for copy in pair:
@@ -126,22 +163,19 @@
         got = product(data, lambda a, b: start + 2 * vectors + 2 * a + b, source)
         return [[s[0], none] for s in got]
 
-    def leave(chain, state):
-        for a in (0, 1):
-            for half in (0, 1):
-                edge[pl.ds((2 * spot(chain) + a) * width + half * 8, 8), :] = state[a][half]
+    leaving = [None] * 6
 
     def solve(plane, chain, source):
         state, states = unit(chain), []
         for line in range(lines):
             state = add(source(line), mapped(2 * plane, line, state))
             states.append(state)
-        leave(chain, state)
+        leaving[chain] = state
         state, result = unit(chain + 1), [None] * lines
         for line in reversed(range(lines)):
             state = add(states[line], mapped(2 * plane + 1, line, state))
             result[line] = state
-        leave(chain + 1, state)
+        leaving[chain + 1] = state
         return result
 
     swept_low = solve(0, T1, lambda line: scaled(0, line))
@@ -150,6 +184,7 @@
             low[pl.ds((2 * line + a) * 8, 8), :] = swept_low[line][a][1]
     swept_high = solve(1, T2, lambda line: add(scaled(1, line), mapped(5, line, swept_low[line])))
     fixed = solve(0, T3, lambda line: mapped(4, line, swept_high[line]))
+    keep_record(edge, leaving)
     for line in range(lines):
         total = add(swept_low[line], fixed[line])
         for a in (0, 1):
@@ -159,15 +194,19 @@
                 second[place, :] = swept_high[line][a][half]
 
 
-def response(ref, width, to, frm, state, start=0):
+def times(ref, row, step, state):
+    out = []
+    for a in (0, 1):
+        left, right = spread(ref, row + step * a, 8), spread(ref, row + step * a + 1, 8)
+        out.append([left * x + right * y for x, y in zip(state[0], state[1])])
+    return out
+
+
+def response(ref, to, frm, state):
     if frm >= UNITS:
         to, frm = to - UNITS, frm - UNITS
-    out = []
-    for a in (0, 1):
-        row = (2 * (spot(to) - start) + a) * width + width - 2 * UNITS + 2 * frm
-        left, right = spread(ref, row, 8), spread(ref, row + 1, 8)
-        out.append([left * x + right * y for x, y in zip(state[0], state[1])])
-    return out
+    start, step = UNIT_START[to]
+    return times(ref, VECTOR_ROWS + start + 2 * frm, step, state)
 
 
 def total(first, *others):
@@ -176,7 +215,7 @@
     return first
 
 
-def merge_kernel(bit, width, last, mine, other, edge, mids, lower, upper):
+def merge_kernel(bit, last, mine, other, edge, mids, lower, upper, *pair):
     is_low = jnp.bitwise_and(lax.axis_index("gy"), bit) == 0
     x, y = mine[...], other[...]
     lower[...] = jnp.where(is_low, x, y)
@@ -185,15 +224,15 @@
     up = jnp.bitwise_and(row, 2) == 0
 
     def base(ref, chain, keep_up):
+        wanted = (up if keep_up else ~up) & (row < unit_count(chain))
         out = []
         for a in (0, 1):
-            start = (2 * spot(chain) + a) * width
-            units = ref[pl.ds(start + 8, 8), :]
-            out.append([ref[pl.ds(start, 8), :], jnp.where(up if keep_up else ~up, units, 0.0)])
+            units = ref[pl.ds(unit_row(chain, a), 8), :]
+            out.append([ref[pl.ds(vector_row(chain, a), 8), :], jnp.where(wanted, units, 0.0)])
         return out
 
-    low = functools.partial(response, lower, width)
-    high = functools.partial(response, upper, width)
+    low = functools.partial(response, lower)
+    high = functools.partial(response, upper)
     m = [None] * 6
     m[T1] = base(lower, T1, True)
     m[U1] = total(base(upper, U1, False), high(U1, T1, m[T1]))
@@ -206,19 +245,25 @@
         ref, of = (upper, high) if CHAINS[chain][0] == 0 else (lower, low)
         through = [c for c in range(chain + 1) if CHAINS[c][0] == CHAINS[chain][0]]
         e[chain] = total(base(ref, chain, CHAINS[chain][0] == 1), *(of(chain, c, m[c]) for c in through))
+    keep_record(mids, m)
+    if not last:
+        keep_record(edge, e)
+        return
     next_low = jnp.bitwise_and(lax.axis_index("gy"), 2 * bit) == 0
-    for chain in range(6):
-        for a in (0, 1):
-            for half in (0, 1):
-                place = (2 * spot(chain) + a) * width + 8 * half
-                mids[pl.ds(place, 8), :] = m[chain][a][half]
-                if not last:
-                    edge[pl.ds(place, 8), :] = e[chain][a][half]
-                elif chain % 2 == 0:
-                    edge[pl.ds(place, 8), :] = jnp.where(next_low, e[chain][a][half], e[chain + 1][a][half])
-
-
-def finish_kernel(lines, levels, width, mine, other, *refs):
+    for chain in (T1, T2, T3):
+        for a in (0, 1):
+            place = pl.ds(vector_row(chain, a), 8)
+            edge[place, :] = jnp.where(next_low, e[chain][a][0], e[chain + 1][a][0])
+    for ref, table in zip(pair, (UP_ROWS, DOWN_ROWS)):
+        ref[...] = jnp.zeros_like(ref)
+        for (to, frm), (start, step) in table.items():
+            for a in (0, 1):
+                ref[pl.ds(start + step * a, 2), :] = e[to][a][1][2 * frm : 2 * frm + 2]
+    units = pl.ds(VECTOR_ROWS // 2, LAST_UNITS)
+    edge[units, :] = jnp.where(next_low, pair[0][...], pair[1][...])
+
+
+def finish_kernel(lines, levels, mine, other, *refs):
     mids, (first, second, low, kept, sent, ups, downs) = refs[: levels - 1], refs[levels - 1 :]
     core, place = lax.axis_index("gx"), lax.axis_index("gy")
     is_low = jnp.bitwise_and(place, 1 << (levels - 1)) == 0
@@ -226,22 +271,29 @@
     ups[...] = jnp.where(is_low, x, y)
     downs[...] = jnp.where(is_low, y, x)
 
-    def base(ref, chain, start):
-        return [[ref[pl.ds((2 * (spot(chain) - start) + a) * width, 8), :]] for a in (0, 1)]
+    width = 8 + 2 * UNITS
+
+    def base(ref, chain, first_chain):
+        skip = vector_row(first_chain, 0)
+        return [[ref[pl.ds(vector_row(chain, a) - skip, 8), :]] for a in (0, 1)]
 
     def up(to, frm, state):
-        return response(ups, width, to, frm, state)
+        start, step = UP_ROWS[to, frm]
+        return times(ups, VECTOR_ROWS // 2 + start, step, state)
 
     def down(to, frm, state):
-        return response(downs, width, to, frm, state, 3)
+        if frm >= UNITS:
+            to, frm = to - UNITS, frm - UNITS
+        start, step = DOWN_ROWS[to, frm]
+        return times(downs, VECTOR_ROWS // 2 + start, step, state)
 
     m = [None] * 6
-    m[T1] = base(ups, T1, 0)
-    m[U1] = total(base(downs, U1, 3), down(U1, T1, m[T1]))
-    m[T2] = total(base(ups, T2, 0), up(T2, U1, m[U1]))
-    m[U2] = total(base(downs, U2, 3), down(U2, T1, m[T1]), down(U2, T2, m[T2]))
-    m[T3] = total(base(ups, T3, 0), up(T3, U1, m[U1]), up(T3, U2, m[U2]))
-    m[U3] = total(base(downs, U3, 3), down(U3, T1, m[T1]), down(U3, T2, m[T2]), down(U3, T3, m[T3]))
+    m[T1] = base(ups, T1, T1)
+    m[U1] = total(base(downs, U1, U1), down(U1, T1, m[T1]))
+    m[T2] = total(base(ups, T2, T1), up(T2, U1, m[U1]))
+    m[U2] = total(base(downs, U2, U1), down(U2, T1, m[T1]), down(U2, T2, m[T2]))
+    m[T3] = total(base(ups, T3, T1), up(T3, U1, m[U1]), up(T3, U2, m[U2]))
+    m[U3] = total(base(downs, U3, U1), down(U3, T1, m[T1]), down(U3, T2, m[T2]), down(U3, T3, m[T3]))
 
     def select(condition, x, y):
         return [[jnp.where(condition, p, q) for p, q in zip(s, t)] for s, t in zip(x, y)]
@@ -253,10 +305,10 @@
             ref = mids[level]
             m = []
             for chain in range(6):
-                terms = [response(ref, width, chain, c, enters[c]) for c in feeds(chain)]
+                terms = [response(ref, chain, c, enters[c]) for c in feeds(chain)]
                 if chain >= UNITS:
-                    terms += [response(ref, width, chain, c, enters[c]) for c in range(UNITS, chain + 1)]
-                m.append(total(base(ref, chain, 0), *terms))
+                    terms += [response(ref, chain, c, enters[c]) for c in range(UNITS, chain + 1)]
+                m.append(total(base(ref, chain, T1), *terms))
         is_low = jnp.bitwise_and(place, 1 << level) == 0
         enters = [
             select(is_low, enters[c], m[c]) if CHAINS[c][0] == 0 else select(is_low, m[c], enters[c])
@@ -284,9 +336,9 @@
 
 
 def unpack_kernel(half, kept, got, out, sems):
-    core = lax.axis_index("gx")
+    part = half_of()
     plan = []
-    for number, (ref, position) in enumerate(((kept, core), (got, 1 - core))):
+    for number, (ref, position) in enumerate(((kept, part), (got, 1 - part))):
         lanes = pl.ds(pl.multiple_of(position * half, half), half)
         plan.append(pltpu.make_async_copy(ref, out.at[0, :, :, :, lanes], sems.at[number]))
     for copy in plan:
@@ -319,7 +371,7 @@
     edge, first, second, low = call(
         functools.partial(local_kernel, lines, vectors),
         "local",
-        [(12 * width, half), (2 * lines * width, half), (2 * lines * width, half), (2 * lines * 8, half)],
+        [(ROWS, half), (2 * lines * width, half), (2 * lines * width, half), (2 * lines * 8, half)],
         (keep, recv),
         [pltpu.VMEM((2 * keep.shape[0], half), jnp.float32), pltpu.VMEM((24 * lines, half), jnp.float32)],
     )
@@ -328,20 +380,21 @@
         got = lax.ppermute(edge, "gy", [(j, j ^ (1 << level)) for j in range(count)])
         last = level == levels - 2
         edge, mid = call(
-            functools.partial(merge_kernel, 1 << level, width, last),
+            functools.partial(merge_kernel, 1 << level, last),
             f"merge{level}",
-            [((6 if last else 12) * width, half), (12 * width, half)],
+            [(LAST_ROWS if last else ROWS, half), (ROWS, half)],
             (edge, got),
-            [pltpu.VMEM((12 * width, half), jnp.float32)] * 2,
+            [pltpu.VMEM((ROWS, half), jnp.float32)] * 2 + [pltpu.VMEM((LAST_UNITS, half), jnp.float32)] * (2 * last),
         )
         mids.append(mid)
-    got = lax.ppermute(edge, "gy", [(j, j ^ (count // 2)) for j in range(count)])
+    across = [(core * count + j, (1 - core) * count + (j ^ (count // 2))) for core in (0, 1) for j in range(count)]
+    got = lax.ppermute(edge, ("gx", "gy"), across)
     kept, sent = call(
-        functools.partial(finish_kernel, lines, levels, width),
+        functools.partial(finish_kernel, lines, levels),
         "finish",
         [(lines * 16, half)] * 2,
         (edge, got, *mids, first, second, low),
-        [pltpu.VMEM((6 * width, half), jnp.float32)] * 2,
+        [pltpu.VMEM((LAST_ROWS, half), jnp.float32)] * 2,
     )
     got = lax.ppermute(sent, "gx", swap)
     (out,) = call(

time: 26.9 us -> 25.4 us (0.944)
  starting transfers between devices: 10.6 us -> 7.64 us
  waiting for transfers between devices: 13.3 us -> 14.7 us
    ppermute x1, starting transfers between devices: 3.29 us -> 0.07 us  [per_device(): got = lax.ppermute(edge, ('gx', 'gy'), across)]
    ppermute x1, waiting for transfers between devices: 2.07 us -> 4.27 us  [per_device(): got = lax.ppermute(edge, ('gx', 'gy'), across)]
    ppermute x3, waiting for transfers between devices: 8.73 us -> 8.21 us  [per_device(): got = lax.ppermute(edge, 'gy', [(j, j ^ 1 << level) for j in range(count)])]
    ppermute x1, starting transfers between devices: 0.07 us -> 0.38 us  [per_device(): got = lax.ppermute(sent, 'gx', swap)]
    ppermute x1, waiting for transfers between devices: 1.33 us -> 1.03 us  [per_device(): got = lax.ppermute(sent, 'gx', swap)]
where the time goes in v2:
time: 25.4 us; the launch traced here: 25.2 us
  waiting for transfers between devices  14.7 us (58%)
  starting transfers between devices  7.64 us (30%)
  Pallas kernels  2.89 us (11%)
    ppermute x3, waiting for transfers between devices, per_device(): got = lax.ppermute(edge, 'gy', [(j, j ^ 1 << level) for j in range(count)])  8.21 us
    ppermute x3, starting transfers between devices, per_device(): got = lax.ppermute(edge, 'gy', [(j, j ^ 1 << level) for j in range(count)])  6.64 us
    ppermute x1, waiting for transfers between devices, per_device(): got = lax.ppermute(edge, ('gx', 'gy'), across)  4.27 us
    pallas_call x7, Pallas kernels, call(): pl.pallas_call(kernel, name=name, out_shape=[jax.ShapeDtypeStruct(s, jnp....  2.89 us
    ppermute x1, waiting for transfers between devices, per_device(): recv = lax.ppermute(send.reshape(-1, half), 'gx', swap)  1.16 us
    ppermute x1, waiting for transfers between devices, per_device(): got = lax.ppermute(sent, 'gx', swap)  1.03 us
    ppermute x1, starting transfers between devices, per_device(): recv = lax.ppermute(send.reshape(-1, half), 'gx', swap)  0.56 us
  transfers between devices with their start and end apart: 6, of which 6 were waited for; matrix products, arithmetic and copies ran while one was open for 0% of the time, Pallas kernels for 0%

profile of v2, /device:TPU:0, one launch (start us, length us, event | category | flops | bytes accessed | tf_op | source)
XLA Modules:
  0.0 25.2 jit_solution(5579260419263819389)
XLA Ops:
  0.0 1.1 %pack.1 = (f32[16,16,2,128]{3,2,1,0:T(2,128)S(1)}, f32[16,16,2,128]{3,2,1,0:T(2,128)S(1)}) custom-call(f32[1,16,8,2,256]{4,3,2,1,0:T(2,128)} %krylov.1, f32[1,16,2,2,256]{4,3,2,1,0:T(2,128)} %inverse.1, f32[1,16,2,2,256]{4,3,2,1,0:T(2,128)} %back.1, f32[1,16,2,2,256]{4,3,2,1,0:T(2,128)} %front.1, f32[1,16,2,2,256]{4,3,2,1,0:T(2,128)} %left.1, ...), custom_call_target="tpu_custom_call" | custom-call | tf_op jit(solution)/shard_map/pack/pallas_call | solution.py:69
  1.1 0.6 %collective-permute-start = (f32[512,128]{1,0:T(8,128)S(1)}, f32[512,128]{1,0:T(8,128)S(1)}, u32[]{:S(2)}, u32[]{:S(2)}) collective-permute-start(f32[512,128]{1,0:T(8,128)S(1)} %bitcast.7), channel_id=1, source_target_pairs={{0,16},{16,0},{1,17},{17,1},{2,18},{18,2},{3,19},{19,3},{4,20},{20... | collective-permute-start | bytes 786440 | tf_op jit(solution)/shard_map/ppermute | solution.py:369
  1.7 1.2 %collective-permute-done.recv = f32[512,128]{1,0:T(8,128)S(1)} collective-permute-done((f32[512,128]{1,0:T(8,128)S(1)}, f32[512,128]{1,0:T(8,128)S(1)}, u32[]{:S(2)}, u32[]{:S(2)}) %collective-permute-start) | collective-permute-done | bytes 262176 | tf_op jit(solution)/shard_map/ppermute | solution.py:369
  2.8 0.5 %local.1 = (f32[168,128]{1,0:T(8,128)S(1)}, f32[512,128]{1,0:T(8,128)S(1)}, f32[512,128]{1,0:T(8,128)S(1)}, f32[256,128]{1,0:T(8,128)S(1)}) custom-call(f32[512,128]{1,0:T(8,128)S(1)} %bitcast.4, f32[512,128]{1,0:T(8,128)S(1)} %collective-permute-done.recv), custom_call_target="tpu_custom_call" | custom-call | tf_op jit(solution)/shard_map/local/pallas_call | solution.py:69
  3.4 2.9 %collective-permute-start.1 = (f32[168,128]{1,0:T(8,128)S(1)}, f32[168,128]{1,0:T(8,128)S(1)}, u32[]{:S(2)}, u32[]{:S(2)}) collective-permute-start(f32[168,128]{1,0:T(8,128)S(1)} %get-tuple-element.21.mine), channel_id=1, source_target_pairs={{0,1},{1,0},{2,3},{3,2},{4,5},{5,4},{6,7},{7,6},{8,9},{9,8},{10,11... | collective-permute-start | bytes 258056 | tf_op jit(solution)/shard_map/ppermute | solution.py:380
  6.3 2.8 %collective-permute-done.1.other = f32[168,128]{1,0:T(8,128)S(1)} collective-permute-done((f32[168,128]{1,0:T(8,128)S(1)}, f32[168,128]{1,0:T(8,128)S(1)}, u32[]{:S(2)}, u32[]{:S(2)}) %collective-permute-start.1) | collective-permute-done | bytes 86048 | tf_op jit(solution)/shard_map/ppermute | solution.py:380
  9.1 0.1 merge0.1
  9.2 1.8 %collective-permute-start.2 = (f32[168,128]{1,0:T(8,128)S(1)}, f32[168,128]{1,0:T(8,128)S(1)}, u32[]{:S(2)}, u32[]{:S(2)}) collective-permute-start(f32[168,128]{1,0:T(8,128)S(1)} %get-tuple-element.22.mine), channel_id=1, source_target_pairs={{0,2},{1,3},{2,0},{3,1},{4,6},{5,7},{6,4},{7,5},{8,10},{9,11},{10,... | collective-permute-start | bytes 258056 | tf_op jit(solution)/shard_map/ppermute | solution.py:380
  11.0 2.7 %collective-permute-done.2.other = f32[168,128]{1,0:T(8,128)S(1)} collective-permute-done((f32[168,128]{1,0:T(8,128)S(1)}, f32[168,128]{1,0:T(8,128)S(1)}, u32[]{:S(2)}, u32[]{:S(2)}) %collective-permute-start.2) | collective-permute-done | bytes 86048 | tf_op jit(solution)/shard_map/ppermute | solution.py:380
  13.8 0.1 merge1.1
  13.8 1.9 %collective-permute-start.3 = (f32[168,128]{1,0:T(8,128)S(1)}, f32[168,128]{1,0:T(8,128)S(1)}, u32[]{:S(2)}, u32[]{:S(2)}) collective-permute-start(f32[168,128]{1,0:T(8,128)S(1)} %get-tuple-element.23.mine), channel_id=1, source_target_pairs={{0,4},{1,5},{2,6},{3,7},{4,0},{5,1},{6,2},{7,3},{8,12},{9,13},{10,... | collective-permute-start | bytes 258056 | tf_op jit(solution)/shard_map/ppermute | solution.py:380
  15.7 2.7 %collective-permute-done.3.other = f32[168,128]{1,0:T(8,128)S(1)} collective-permute-done((f32[168,128]{1,0:T(8,128)S(1)}, f32[168,128]{1,0:T(8,128)S(1)}, u32[]{:S(2)}, u32[]{:S(2)}) %collective-permute-start.3) | collective-permute-done | bytes 86048 | tf_op jit(solution)/shard_map/ppermute | solution.py:380
  18.4 0.1 merge2.1
  18.5 0.1 collective-permute-start.4
  18.6 4.3 %collective-permute-done.4.other = f32[72,128]{1,0:T(8,128)S(1)} collective-permute-done((f32[72,128]{1,0:T(8,128)S(1)}, f32[72,128]{1,0:T(8,128)S(1)}, u32[]{:S(2)}, u32[]{:S(2)}) %collective-permute-start.4) | collective-permute-done | bytes 36896 | tf_op jit(solution)/shard_map/ppermute | solution.py:391
  22.8 0.3 %finish.1 = (f32[256,128]{1,0:T(8,128)S(1)}, f32[256,128]{1,0:T(8,128)S(1)}) custom-call(f32[72,128]{1,0:T(8,128)S(1)} %get-tuple-element.24.mine, f32[72,128]{1,0:T(8,128)S(1)} %collective-permute-done.4.other, f32[168,128]{1,0:T(8,128)S(1)} %get-tuple-element.25.refs_0_, f32[168,128]{1,0:T(8,128)S(1)} %get-tuple-element.26.refs_1_, ...), custom_call_target="tpu_custom_call" | custom-call | tf_op jit(solution)/shard_map/finish/pallas_call | solution.py:69
  23.1 0.4 %collective-permute-start.5 = (f32[256,128]{1,0:T(8,128)S(1)}, f32[256,128]{1,0:T(8,128)S(1)}, u32[]{:S(2)}, u32[]{:S(2)}) collective-permute-start(f32[256,128]{1,0:T(8,128)S(1)} %get-tuple-element.32), channel_id=1, source_target_pairs={{0,16},{16,0},{1,17},{17,1},{2,18},{18,2},{3,19},{19,3},{4,20},{20... | collective-permute-start | bytes 393224 | tf_op jit(solution)/shard_map/ppermute | solution.py:399
  23.5 1.0 %collective-permute-done.5 = f32[256,128]{1,0:T(8,128)S(1)} collective-permute-done((f32[256,128]{1,0:T(8,128)S(1)}, f32[256,128]{1,0:T(8,128)S(1)}, u32[]{:S(2)}, u32[]{:S(2)}) %collective-permute-start.5) | collective-permute-done | bytes 131104 | tf_op jit(solution)/shard_map/ppermute | solution.py:399
  24.5 0.7 %unpack.1 = f32[1,16,8,2,256]{4,3,2,1,0:T(2,128)} custom-call(f32[16,8,2,128]{3,2,1,0:T(2,128)S(1)} %bitcast.5, f32[16,8,2,128]{3,2,1,0:T(2,128)S(1)} %bitcast.6), custom_call_target="tpu_custom_call" | custom-call | tf_op jit(solution)/shard_map/unpack/pallas_call | solution.py:69
Async XLA Ops:
  1.1 1.7 %collective-permute-start = (f32[512,128]{1,0:T(8,128)S(1)}, f32[512,128]{1,0:T(8,128)S(1)}, u32[]{:S(2)}, u32[]{:S(2)}) collective-permute-start(f32[512,128]{1,0:T(8,128)S(1)} %bitcast.7), channel_id=1, source_target_pairs={{0,16},{16,0},{1,17},{17,1},{2,18},{18,2},{3,19},{19,3},{4,20},{20... | collective-permute-start | bytes 786440 | tf_op jit(solution)/shard_map/ppermute | solution.py:369
  3.4 5.7 %collective-permute-start.1 = (f32[168,128]{1,0:T(8,128)S(1)}, f32[168,128]{1,0:T(8,128)S(1)}, u32[]{:S(2)}, u32[]{:S(2)}) collective-permute-start(f32[168,128]{1,0:T(8,128)S(1)} %get-tuple-element.21.mine), channel_id=1, source_target_pairs={{0,1},{1,0},{2,3},{3,2},{4,5},{5,4},{6,7},{7,6},{8,9},{9,8},{10,11... | collective-permute-start | bytes 258056 | tf_op jit(solution)/shard_map/ppermute | solution.py:380
  9.2 4.6 %collective-permute-start.2 = (f32[168,128]{1,0:T(8,128)S(1)}, f32[168,128]{1,0:T(8,128)S(1)}, u32[]{:S(2)}, u32[]{:S(2)}) collective-permute-start(f32[168,128]{1,0:T(8,128)S(1)} %get-tuple-element.22.mine), channel_id=1, source_target_pairs={{0,2},{1,3},{2,0},{3,1},{4,6},{5,7},{6,4},{7,5},{8,10},{9,11},{10,... | collective-permute-start | bytes 258056 | tf_op jit(solution)/shard_map/ppermute | solution.py:380
  13.8 4.6 %collective-permute-start.3 = (f32[168,128]{1,0:T(8,128)S(1)}, f32[168,128]{1,0:T(8,128)S(1)}, u32[]{:S(2)}, u32[]{:S(2)}) collective-permute-start(f32[168,128]{1,0:T(8,128)S(1)} %get-tuple-element.23.mine), channel_id=1, source_target_pairs={{0,4},{1,5},{2,6},{3,7},{4,0},{5,1},{6,2},{7,3},{8,12},{9,13},{10,... | collective-permute-start | bytes 258056 | tf_op jit(solution)/shard_map/ppermute | solution.py:380
  18.5 4.3 %collective-permute-start.4 = (f32[72,128]{1,0:T(8,128)S(1)}, f32[72,128]{1,0:T(8,128)S(1)}, u32[]{:S(2)}, u32[]{:S(2)}) collective-permute-start(f32[72,128]{1,0:T(8,128)S(1)} %get-tuple-element.24.mine), channel_id=1, source_target_pairs={{0,24},{1,25},{2,26},{3,27},{4,28},{5,29},{6,30},{7,31},{8,16},{9,... | collective-permute-start | bytes 110600 | tf_op jit(solution)/shard_map/ppermute | solution.py:391
  23.1 1.4 %collective-permute-start.5 = (f32[256,128]{1,0:T(8,128)S(1)}, f32[256,128]{1,0:T(8,128)S(1)}, u32[]{:S(2)}, u32[]{:S(2)}) collective-permute-start(f32[256,128]{1,0:T(8,128)S(1)} %get-tuple-element.32), channel_id=1, source_target_pairs={{0,16},{16,0},{1,17},{17,1},{2,18},{18,2},{3,19},{19,3},{4,20},{20... | collective-permute-start | bytes 393224 | tf_op jit(solution)/shard_map/ppermute | solution.py:399

commit v3 on v2

--- a/solution.py
+++ b/solution.py
@@ -65,7 +65,7 @@
     return ref[pl.ds(row, count, stride=0), :]
 
 
-def call(kernel, name, outs, ins, scratch=(), specs=None, out_specs=None):
+def call(kernel, name, outs, ins, scratch=(), specs=None, out_specs=None, aliases={}):
     return pl.pallas_call(
         kernel,
         name=name,
@@ -73,43 +73,34 @@
         in_specs=specs or [VMEM] * len(ins),
         out_specs=out_specs or [VMEM] * len(outs),
         scratch_shapes=list(scratch),
+        input_output_aliases=aliases,
         compiler_params=pltpu.CompilerParams(vmem_limit_bytes=8 << 20),
     )(*ins)
 
 
-def pack_kernel(half, vectors, krylov, inverse, back, front, left, right, keep, send, sems):
+def pack_kernel(half, vectors, away, krylov, inverse, back, front, left, right, out, sems):
     core, part = lax.axis_index("gx"), half_of()
+    position = 1 - part if away else part
+    lanes = pl.ds(pl.multiple_of(position * half, half), half)
     base = (0, vectors, vectors + 2, vectors + 4, vectors + 6)
 
-    def copies(ref, position, target, number):
-        lanes = pl.ds(pl.multiple_of(position * half, half), half)
-        size = ref.shape[2]
-        return pltpu.make_async_copy(
-            ref.at[0, :, :, :, lanes],
-            target.at[:, pl.ds(base[number], size)],
-            sems.at[number, 0 if target is keep else 1],
-        )
-
-    fixed = (krylov, inverse, left, right)
-    plan = [
-        copies(ref, position, target, number)
-        for target, position in ((send, 1 - part), (keep, part))
-        for number, ref in enumerate(fixed)
-    ]
-    for copy in plan:
-        copy.start()
+    def copy(ref, number):
+        target = out.at[:, pl.ds(base[number], ref.shape[2])]
+        return pltpu.make_async_copy(ref.at[0, :, :, :, lanes], target, sems.at[number])
+
+    plan = [copy(ref, number) for number, ref in enumerate((krylov, inverse, left, right))]
+    for one in plan:
+        one.start()
     for own, ref in ((0, front), (1, back)):
 
         @pl.when(core == own)
         def _():
-            pair = [copies(ref, 1 - part, send, 4), copies(ref, part, keep, 4)]
-            for copy in pair:
-                copy.start()
-            for copy in pair:
-                copy.wait()
-
-    for copy in plan:
-        copy.wait()
+            one = copy(ref, 4)
+            one.start()
+            one.wait()
+
+    for one in plan:
+        one.wait()
 
 
 def local_kernel(lines, vectors, keep, recv, edge, first, second, low, data, maps):
@@ -263,15 +254,40 @@
     edge[units, :] = jnp.where(next_low, pair[0][...], pair[1][...])
 
 
+def write_plane(lines, own, enters, first, second, low, target):
+    width = 8 + 2 * UNITS
+
+    def columns(ref, start, chains):
+        value = None
+        for place, chain in chains:
+            for b in (0, 1):
+                term = spread(ref, start + 2 * place + b, 8) * enters[chain][b][0]
+                value = term if value is None else value + term
+        return value
+
+    core = lax.axis_index("gx")
+    units = [(c, c) for c in range(UNITS)]
+    for plane in (0, 1):
+
+        @pl.when(core == (plane if own else 1 - plane))
+        def _():
+            source = second if plane else first
+            for line in range(lines):
+                for a in (0, 1):
+                    start = (2 * line + a) * width
+                    value = source[pl.ds(start, 8), :] + columns(source, start + 8, units)
+                    if plane == 0:
+                        value = value + columns(low, (2 * line + a) * 8, [(T1, T3), (U1, U3)])
+                    target[pl.ds(line * 16 + a, 8, stride=2), :] = value
+
+
 def finish_kernel(lines, levels, mine, other, *refs):
-    mids, (first, second, low, kept, sent, ups, downs) = refs[: levels - 1], refs[levels - 1 :]
-    core, place = lax.axis_index("gx"), lax.axis_index("gy")
+    mids, (first, second, low, sent, entry, ups, downs) = refs[: levels - 1], refs[levels - 1 :]
+    place = lax.axis_index("gy")
     is_low = jnp.bitwise_and(place, 1 << (levels - 1)) == 0
     x, y = mine[...], other[...]
     ups[...] = jnp.where(is_low, x, y)
     downs[...] = jnp.where(is_low, y, x)
-
-    width = 8 + 2 * UNITS
 
     def base(ref, chain, first_chain):
         skip = vector_row(first_chain, 0)
@@ -315,36 +331,32 @@
             for c in range(6)
         ]
 
-    def columns(ref, start, chains):
-        value = None
-        for place_of, chain in chains:
-            for b in (0, 1):
-                term = spread(ref, start + 2 * place_of + b, 8) * enters[chain][b][0]
-                value = term if value is None else value + term
-        return value
-
-    for line in range(lines):
-        for a in (0, 1):
-            start = (2 * line + a) * width
-            units = [(c, c) for c in range(UNITS)]
-            high = second[pl.ds(start, 8), :] + columns(second, start + 8, units)
-            own = first[pl.ds(start, 8), :] + columns(first, start + 8, units)
-            own = own + columns(low, (2 * line + a) * 8, [(T1, T3), (U1, U3)])
-            target = pl.ds(line * 16 + a, 8, stride=2)
-            kept[target, :] = jnp.where(core == 0, own, high)
-            sent[target, :] = jnp.where(core == 0, high, own)
-
-
-def unpack_kernel(half, kept, got, out, sems):
-    part = half_of()
-    plan = []
-    for number, (ref, position) in enumerate(((kept, part), (got, 1 - part))):
-        lanes = pl.ds(pl.multiple_of(position * half, half), half)
-        plan.append(pltpu.make_async_copy(ref, out.at[0, :, :, :, lanes], sems.at[number]))
-    for copy in plan:
-        copy.start()
-    for copy in plan:
-        copy.wait()
+    write_plane(lines, False, enters, first, second, low, sent)
+    for chain in range(6):
+        for a in (0, 1):
+            entry[pl.ds(vector_row(chain, a), 8), :] = enters[chain][a][0]
+
+
+def part_copy(half, position, value, out, sem):
+    lanes = pl.ds(pl.multiple_of(position * half, half), half)
+    return pltpu.make_async_copy(value, out.at[0, :, :, :, lanes], sem)
+
+
+def own_kernel(lines, entry, first, second, low, kept):
+    enters = [[[entry[pl.ds(vector_row(chain, a), 8), :]] for a in (0, 1)] for chain in range(6)]
+    write_plane(lines, True, enters, first, second, low, kept)
+
+
+def store_kernel(half, kept, out, sem):
+    one = part_copy(half, half_of(), kept, out, sem.at[0])
+    one.start()
+    one.wait()
+
+
+def last_kernel(half, got, before, out, sem):
+    one = part_copy(half, 1 - half_of(), got, out, sem.at[0])
+    one.start()
+    one.wait()
 
 
 def per_device(krylov, inverse, back, front, left, right):
@@ -357,17 +369,21 @@
     assert vectors == 8 and half == 128
     swap = [(0, 1), (1, 0)]
 
-    slots = vectors + 8
-    keep, send = call(
-        functools.partial(pack_kernel, half, vectors),
-        "pack",
-        [(lines, slots, 2, half)] * 2,
-        [pltpu.with_memory_space_constraint(x, pltpu.HBM) for x in (krylov, inverse, back, front, left, right)],
-        [pltpu.SemaphoreType.DMA((5, 2))],
-        specs=[HBM] * 6,
-    )
-    recv = lax.ppermute(send.reshape(-1, half), "gx", swap)
-    keep = keep.reshape(-1, half)
+    arguments = [pltpu.with_memory_space_constraint(x, pltpu.HBM) for x in (krylov, inverse, back, front, left, right)]
+
+    def pack(away):
+        (out,) = call(
+            functools.partial(pack_kernel, half, vectors, away),
+            "pack_away" if away else "pack_own",
+            [(lines, vectors + 8, 2, half)],
+            arguments,
+            [pltpu.SemaphoreType.DMA((5,))],
+            specs=[HBM] * 6,
+        )
+        return out.reshape(-1, half)
+
+    recv = lax.ppermute(pack(True), "gx", swap)
+    keep = pack(False)
     edge, first, second, low = call(
         functools.partial(local_kernel, lines, vectors),
         "local",
@@ -389,22 +405,35 @@
         mids.append(mid)
     across = [(core * count + j, (1 - core) * count + (j ^ (count // 2))) for core in (0, 1) for j in range(count)]
     got = lax.ppermute(edge, ("gx", "gy"), across)
-    kept, sent = call(
+    sent, entry = call(
         functools.partial(finish_kernel, lines, levels),
         "finish",
-        [(lines * 16, half)] * 2,
+        [(lines * 16, half), (VECTOR_ROWS, half)],
         (edge, got, *mids, first, second, low),
         [pltpu.VMEM((LAST_ROWS, half), jnp.float32)] * 2,
     )
     got = lax.ppermute(sent, "gx", swap)
+    (kept,) = call(
+        functools.partial(own_kernel, lines), "own", [(lines * 16, half)], (entry, first, second, low)
+    )
     (out,) = call(
-        functools.partial(unpack_kernel, half),
-        "unpack",
+        functools.partial(store_kernel, half),
+        "store",
         [krylov.shape],
-        [x.reshape(lines, vectors, 2, half) for x in (kept, got)],
-        [pltpu.SemaphoreType.DMA((2,))],
-        specs=[ANY] * 2,
+        [kept.reshape(lines, vectors, 2, half)],
+        [pltpu.SemaphoreType.DMA((1,))],
+        specs=[ANY],
         out_specs=[HBM],
+    )
+    (out,) = call(
+        functools.partial(last_kernel, half),
+        "last",
+        [krylov.shape],
+        [got.reshape(lines, vectors, 2, half), out],
+        [pltpu.SemaphoreType.DMA((1,))],
+        specs=[ANY, HBM],
+        out_specs=[HBM],
+        aliases={1: 0},
     )
     return out
 

time: 25.4 us -> 25.1 us (0.988)
  waiting for transfers between devices: 14.7 us -> 12.9 us
  Pallas kernels: 2.89 us -> 4.31 us
    pallas_call x7 -> x10, Pallas kernels: 2.89 us -> 4.31 us  [call(): pl.pallas_call(kernel, name=name, out_shape=[jax.ShapeDtypeStruct(s, jnp....]
    ppermute x1, waiting for transfers between devices: 1.16 us -> 0.2 us  [per_device(): recv = lax.ppermute(pack(True), 'gx', swap)]
    ppermute x1, waiting for transfers between devices: 1.03 us -> 0.2 us  [per_device(): got = lax.ppermute(sent, 'gx', swap)]
  transfers between devices with their start and end apart: 6 -> 6, of which waited for: 6 -> 6; matrix products, arithmetic and copies ran while one was open for 0% -> 0% of each run, Pallas kernels for 0% -> 7%
where the time goes in v3:
time: 25.1 us; the launch traced here: 24.9 us
  waiting for transfers between devices  12.9 us (51%)
  starting transfers between devices  7.68 us (31%)
  Pallas kernels  4.31 us (17%)
    ppermute x3, waiting for transfers between devices, per_device(): got = lax.ppermute(edge, 'gy', [(j, j ^ 1 << level) for j in range(count)])  8.21 us
    ppermute x3, starting transfers between devices, per_device(): got = lax.ppermute(edge, 'gy', [(j, j ^ 1 << level) for j in range(count)])  6.64 us
    pallas_call x10, Pallas kernels, call(): pl.pallas_call(kernel, name=name, out_shape=[jax.ShapeDtypeStruct(s, jnp....  4.31 us
    ppermute x1, waiting for transfers between devices, per_device(): got = lax.ppermute(edge, ('gx', 'gy'), across)  4.27 us
    ppermute x1, starting transfers between devices, per_device(): recv = lax.ppermute(pack(True), 'gx', swap)  0.56 us
  transfers between devices with their start and end apart: 6, of which 6 were waited for; matrix products, arithmetic and copies ran while one was open for 0% of the time, Pallas kernels for 7%

profile of v3, /device:TPU:0, one launch (start us, length us, event | category | flops | bytes accessed | tf_op | source)
XLA Modules:
  0.0 24.9 jit_solution(13656403534457831710)
XLA Ops:
  0.0 1.0 %pack_away.1 = f32[16,16,2,128]{3,2,1,0:T(2,128)S(1)} custom-call(f32[1,16,8,2,256]{4,3,2,1,0:T(2,128)} %krylov.3, f32[1,16,2,2,256]{4,3,2,1,0:T(2,128)} %inverse.3, f32[1,16,2,2,256]{4,3,2,1,0:T(2,128)} %back.3, f32[1,16,2,2,256]{4,3,2,1,0:T(2,128)} %front.3, f32[1,16,2,2,256]{4,3,2,1,0:T(2,128)} %left.3, f32[1,16,2,2,256]{4,3,2,1,0:T(2,128)} %right.3), custom_call_target="tpu_custom_call" | custom-call | tf_op jit(solution)/shard_map/pack_away/pallas_call | solution.py:69
  1.0 0.6 %collective-permute-start = (f32[512,128]{1,0:T(8,128)S(1)}, f32[512,128]{1,0:T(8,128)S(1)}, u32[]{:S(2)}, u32[]{:S(2)}) collective-permute-start(f32[512,128]{1,0:T(8,128)S(1)} %bitcast.6), channel_id=1, source_target_pairs={{0,16},{16,0},{1,17},{17,1},{2,18},{18,2},{3,19},{19,3},{4,20},{20... | collective-permute-start | bytes 786440 | tf_op jit(solution)/shard_map/ppermute | solution.py:385
  1.5 1.0 %pack_own.1 = f32[16,16,2,128]{3,2,1,0:T(2,128)S(1)} custom-call(f32[1,16,8,2,256]{4,3,2,1,0:T(2,128)} %krylov.3, f32[1,16,2,2,256]{4,3,2,1,0:T(2,128)} %inverse.3, f32[1,16,2,2,256]{4,3,2,1,0:T(2,128)} %back.3, f32[1,16,2,2,256]{4,3,2,1,0:T(2,128)} %front.3, f32[1,16,2,2,256]{4,3,2,1,0:T(2,128)} %left.3, f32[1,16,2,2,256]{4,3,2,1,0:T(2,128)} %right.3), custom_call_target="tpu_custom_call" | custom-call | tf_op jit(solution)/shard_map/pack_own/pallas_call | solution.py:69
  2.5 0.2 collective-permute-done.recv
  2.7 0.5 %local.1 = (f32[168,128]{1,0:T(8,128)S(1)}, f32[512,128]{1,0:T(8,128)S(1)}, f32[512,128]{1,0:T(8,128)S(1)}, f32[256,128]{1,0:T(8,128)S(1)}) custom-call(f32[512,128]{1,0:T(8,128)S(1)} %bitcast.4, f32[512,128]{1,0:T(8,128)S(1)} %collective-permute-done.recv), custom_call_target="tpu_custom_call" | custom-call | tf_op jit(solution)/shard_map/local/pallas_call | solution.py:69
  3.2 2.9 %collective-permute-start.1 = (f32[168,128]{1,0:T(8,128)S(1)}, f32[168,128]{1,0:T(8,128)S(1)}, u32[]{:S(2)}, u32[]{:S(2)}) collective-permute-start(f32[168,128]{1,0:T(8,128)S(1)} %get-tuple-element.17.mine), channel_id=1, source_target_pairs={{0,1},{1,0},{2,3},{3,2},{4,5},{5,4},{6,7},{7,6},{8,9},{9,8},{10,11... | collective-permute-start | bytes 258056 | tf_op jit(solution)/shard_map/ppermute | solution.py:396
  6.1 2.8 %collective-permute-done.1.other = f32[168,128]{1,0:T(8,128)S(1)} collective-permute-done((f32[168,128]{1,0:T(8,128)S(1)}, f32[168,128]{1,0:T(8,128)S(1)}, u32[]{:S(2)}, u32[]{:S(2)}) %collective-permute-start.1) | collective-permute-done | bytes 86048 | tf_op jit(solution)/shard_map/ppermute | solution.py:396
  9.0 0.1 merge0.1
  9.1 1.8 %collective-permute-start.2 = (f32[168,128]{1,0:T(8,128)S(1)}, f32[168,128]{1,0:T(8,128)S(1)}, u32[]{:S(2)}, u32[]{:S(2)}) collective-permute-start(f32[168,128]{1,0:T(8,128)S(1)} %get-tuple-element.18.mine), channel_id=1, source_target_pairs={{0,2},{1,3},{2,0},{3,1},{4,6},{5,7},{6,4},{7,5},{8,10},{9,11},{10,... | collective-permute-start | bytes 258056 | tf_op jit(solution)/shard_map/ppermute | solution.py:396
  10.9 2.7 %collective-permute-done.2.other = f32[168,128]{1,0:T(8,128)S(1)} collective-permute-done((f32[168,128]{1,0:T(8,128)S(1)}, f32[168,128]{1,0:T(8,128)S(1)}, u32[]{:S(2)}, u32[]{:S(2)}) %collective-permute-start.2) | collective-permute-done | bytes 86048 | tf_op jit(solution)/shard_map/ppermute | solution.py:396
  13.6 0.1 merge1.1
  13.7 1.9 %collective-permute-start.3 = (f32[168,128]{1,0:T(8,128)S(1)}, f32[168,128]{1,0:T(8,128)S(1)}, u32[]{:S(2)}, u32[]{:S(2)}) collective-permute-start(f32[168,128]{1,0:T(8,128)S(1)} %get-tuple-element.19.mine), channel_id=1, source_target_pairs={{0,4},{1,5},{2,6},{3,7},{4,0},{5,1},{6,2},{7,3},{8,12},{9,13},{10,... | collective-permute-start | bytes 258056 | tf_op jit(solution)/shard_map/ppermute | solution.py:396
  15.6 2.7 %collective-permute-done.3.other = f32[168,128]{1,0:T(8,128)S(1)} collective-permute-done((f32[168,128]{1,0:T(8,128)S(1)}, f32[168,128]{1,0:T(8,128)S(1)}, u32[]{:S(2)}, u32[]{:S(2)}) %collective-permute-start.3) | collective-permute-done | bytes 86048 | tf_op jit(solution)/shard_map/ppermute | solution.py:396
  18.2 0.1 merge2.1
  18.3 0.1 collective-permute-start.4
  18.4 4.3 %collective-permute-done.4.other = f32[72,128]{1,0:T(8,128)S(1)} collective-permute-done((f32[72,128]{1,0:T(8,128)S(1)}, f32[72,128]{1,0:T(8,128)S(1)}, u32[]{:S(2)}, u32[]{:S(2)}) %collective-permute-start.4) | collective-permute-done | bytes 36896 | tf_op jit(solution)/shard_map/ppermute | solution.py:407
  22.7 0.2 finish.1
  22.8 0.4 %collective-permute-start.5 = (f32[256,128]{1,0:T(8,128)S(1)}, f32[256,128]{1,0:T(8,128)S(1)}, u32[]{:S(2)}, u32[]{:S(2)}) collective-permute-start(f32[256,128]{1,0:T(8,128)S(1)} %get-tuple-element.27), channel_id=1, source_target_pairs={{0,16},{16,0},{1,17},{17,1},{2,18},{18,2},{3,19},{19,3},{4,20},{20... | collective-permute-start | bytes 393224 | tf_op jit(solution)/shard_map/ppermute | solution.py:415
  23.3 0.1 own.1
  23.4 0.7 %store.1.before = f32[1,16,8,2,256]{4,3,2,1,0:T(2,128)} custom-call(f32[16,8,2,128]{3,2,1,0:T(2,128)S(1)} %bitcast.5), custom_call_target="tpu_custom_call" | custom-call | tf_op jit(solution)/shard_map/store/pallas_call | solution.py:69
  24.1 0.2 collective-permute-done.5
  24.3 0.7 %last.1 = f32[1,16,8,2,256]{4,3,2,1,0:T(2,128)} custom-call(f32[16,8,2,128]{3,2,1,0:T(2,128)S(1)} %bitcast.7, f32[1,16,8,2,256]{4,3,2,1,0:T(2,128)} %store.1.before), custom_call_target="tpu_custom_call", output_to_operand_aliasing={{}: (1, {})} | custom-call | tf_op jit(solution)/shard_map/last/pallas_call | solution.py:69
Async XLA Ops:
  1.0 1.7 %collective-permute-start = (f32[512,128]{1,0:T(8,128)S(1)}, f32[512,128]{1,0:T(8,128)S(1)}, u32[]{:S(2)}, u32[]{:S(2)}) collective-permute-start(f32[512,128]{1,0:T(8,128)S(1)} %bitcast.6), channel_id=1, source_target_pairs={{0,16},{16,0},{1,17},{17,1},{2,18},{18,2},{3,19},{19,3},{4,20},{20... | collective-permute-start | bytes 786440 | tf_op jit(solution)/shard_map/ppermute | solution.py:385
  3.2 5.7 %collective-permute-start.1 = (f32[168,128]{1,0:T(8,128)S(1)}, f32[168,128]{1,0:T(8,128)S(1)}, u32[]{:S(2)}, u32[]{:S(2)}) collective-permute-start(f32[168,128]{1,0:T(8,128)S(1)} %get-tuple-element.17.mine), channel_id=1, source_target_pairs={{0,1},{1,0},{2,3},{3,2},{4,5},{5,4},{6,7},{7,6},{8,9},{9,8},{10,11... | collective-permute-start | bytes 258056 | tf_op jit(solution)/shard_map/ppermute | solution.py:396
  9.1 4.6 %collective-permute-start.2 = (f32[168,128]{1,0:T(8,128)S(1)}, f32[168,128]{1,0:T(8,128)S(1)}, u32[]{:S(2)}, u32[]{:S(2)}) collective-permute-start(f32[168,128]{1,0:T(8,128)S(1)} %get-tuple-element.18.mine), channel_id=1, source_target_pairs={{0,2},{1,3},{2,0},{3,1},{4,6},{5,7},{6,4},{7,5},{8,10},{9,11},{10,... | collective-permute-start | bytes 258056 | tf_op jit(solution)/shard_map/ppermute | solution.py:396
  13.7 4.6 %collective-permute-start.3 = (f32[168,128]{1,0:T(8,128)S(1)}, f32[168,128]{1,0:T(8,128)S(1)}, u32[]{:S(2)}, u32[]{:S(2)}) collective-permute-start(f32[168,128]{1,0:T(8,128)S(1)} %get-tuple-element.19.mine), channel_id=1, source_target_pairs={{0,4},{1,5},{2,6},{3,7},{4,0},{5,1},{6,2},{7,3},{8,12},{9,13},{10,... | collective-permute-start | bytes 258056 | tf_op jit(solution)/shard_map/ppermute | solution.py:396
  18.3 4.3 %collective-permute-start.4 = (f32[72,128]{1,0:T(8,128)S(1)}, f32[72,128]{1,0:T(8,128)S(1)}, u32[]{:S(2)}, u32[]{:S(2)}) collective-permute-start(f32[72,128]{1,0:T(8,128)S(1)} %get-tuple-element.20.mine), channel_id=1, source_target_pairs={{0,24},{1,25},{2,26},{3,27},{4,28},{5,29},{6,30},{7,31},{8,16},{9,... | collective-permute-start | bytes 110600 | tf_op jit(solution)/shard_map/ppermute | solution.py:407
  22.8 1.4 %collective-permute-start.5 = (f32[256,128]{1,0:T(8,128)S(1)}, f32[256,128]{1,0:T(8,128)S(1)}, u32[]{:S(2)}, u32[]{:S(2)}) collective-permute-start(f32[256,128]{1,0:T(8,128)S(1)} %get-tuple-element.27), channel_id=1, source_target_pairs={{0,16},{16,0},{1,17},{17,1},{2,18},{18,2},{3,19},{19,3},{4,20},{20... | collective-permute-start | bytes 393224 | tf_op jit(solution)/shard_map/ppermute | solution.py:415

commit v4 on v3

--- a/solution.py
+++ b/solution.py
@@ -52,8 +52,8 @@
     return jnp.bitwise_xor(lax.axis_index("gx"), flip)
 
 
-def keep_record(ref, values):
-    for chain in range(6):
+def keep_record(ref, values, chains=range(6)):
+    for chain in chains:
         for a in (0, 1):
             carries, units = values[chain][a]
             ref[pl.ds(vector_row(chain, a), 8), :] = carries
@@ -103,86 +103,124 @@
         one.wait()
 
 
-def local_kernel(lines, vectors, keep, recv, edge, first, second, low, data, maps):
-    core = lax.axis_index("gx")
+def combine(ref, place, state):
+    out = []
+    for a in (0, 1):
+        left, right = (spread(ref, place(a, b), 8) for b in (0, 1))
+        out.append([left * x + right * y for x, y in zip(state[0], state[1])])
+    return out
+
+
+def add(x, y):
+    return [[p + q for p, q in zip(s, t)] for s, t in zip(x, y)]
+
+
+FORWARD, BACKWARD, ACROSS = range(3)
+
+
+def make_maps(lines, vectors, data, maps):
     pitch = 2 * vectors + 16
-    rows = lines * pitch
-    width = vectors + 2 * UNITS
-    mine, other = keep[...], recv[...]
-    data[pl.ds(0, rows), :] = jnp.where(core == 0, mine, other)
-    data[pl.ds(rows, rows), :] = jnp.where(core == 0, other, mine)
-
-    def block(plane, number):
-        start = plane * rows + 2 * vectors + 4 * number
+
+    def block(number):
+        start = 2 * vectors + 4 * number
         return [[data[pl.ds(start + 2 * a + b, lines, stride=pitch), :] for b in (0, 1)] for a in (0, 1)]
 
-    def keep_map(number, left, right):
+    inverse = block(0)
+    for number in (FORWARD, BACKWARD, ACROSS):
+        coupling = block(1 + number)
         for a in (0, 1):
             for b in (0, 1):
-                value = -(left[a][0] * right[0][b] + left[a][1] * right[1][b])
+                value = -(inverse[a][0] * coupling[0][b] + inverse[a][1] * coupling[1][b])
                 maps[pl.ds((4 * number + 2 * a + b) * lines, lines), :] = value
 
-    for plane in (0, 1):
-        inverse = block(plane, 0)
-        keep_map(2 * plane, inverse, block(plane, 1))
-        keep_map(2 * plane + 1, inverse, block(plane, 2))
-        keep_map(4 + plane, inverse, block(plane, 3))
-
-    def product(ref, place, state):
-        out = []
-        for a in (0, 1):
-            left, right = (spread(ref, place(a, b), 8) for b in (0, 1))
-            out.append([left * x + right * y for x, y in zip(state[0], state[1])])
-        return out
-
-    def mapped(number, line, state):
-        return product(maps, lambda a, b: (4 * number + 2 * a + b) * lines + line, state)
-
-    def add(x, y):
-        return [[p + q for p, q in zip(s, t)] for s, t in zip(x, y)]
-
+
+def mapped(lines, maps, number, line, state):
+    return combine(maps, lambda a, b: (4 * number + 2 * a + b) * lines + line, state)
+
+
+def scaled(vectors, data, line):
+    start = line * (2 * vectors + 16)
+    source = [[data[pl.ds(start + a, vectors, stride=2), :]] for a in (0, 1)]
+    got = combine(data, lambda a, b: start + 2 * vectors + 2 * a + b, source)
+    return [[s[0], jnp.zeros((8, 128), jnp.float32)] for s in got]
+
+
+def unit(chain):
     row = lax.broadcasted_iota(jnp.int32, (8, 128), 0)
     none = jnp.zeros((8, 128), jnp.float32)
-
-    def unit(chain):
-        one = [jnp.where(row == 2 * chain + a, 1.0, 0.0) for a in (0, 1)] if chain < UNITS else [none, none]
-        return [[none, one[a]] for a in (0, 1)]
-
-    def scaled(plane, line):
-        start = plane * rows + line * pitch
-        source = [[data[pl.ds(start + a, vectors, stride=2), :]] for a in (0, 1)]
-        got = product(data, lambda a, b: start + 2 * vectors + 2 * a + b, source)
-        return [[s[0], none] for s in got]
-
-    leaving = [None] * 6
-
-    def solve(plane, chain, source):
-        state, states = unit(chain), []
+    one = [jnp.where(row == 2 * chain + a, 1.0, 0.0) if chain < UNITS else none for a in (0, 1)]
+    return [[none, one[a]] for a in (0, 1)]
+
+
+def sweep_plane(lines, maps, chain, source, leaving):
+    state, states = unit(chain), []
+    for line in range(lines):
+        state = add(source(line), mapped(lines, maps, FORWARD, line, state))
+        states.append(state)
+    leaving[chain] = state
+    state, result = unit(chain + 1), [None] * lines
+    for line in reversed(range(lines)):
+        state = add(states[line], mapped(lines, maps, BACKWARD, line, state))
+        result[line] = state
+    leaving[chain + 1] = state
+    return result
+
+
+def state_rows(line, a, part):
+    return pl.ds((2 * line + a) * (8 + 2 * UNITS) + 8 * part, 8)
+
+
+def early_kernel(lines, vectors, keep, swept, edge, maps):
+    make_maps(lines, vectors, keep, maps)
+
+    @pl.when(lax.axis_index("gx") == 0)
+    def _():
+        leaving = [None] * 6
+        result = sweep_plane(lines, maps, T1, lambda line: scaled(vectors, keep, line), leaving)
+        keep_record(edge, leaving, (T1, U1))
         for line in range(lines):
-            state = add(source(line), mapped(2 * plane, line, state))
-            states.append(state)
-        leaving[chain] = state
-        state, result = unit(chain + 1), [None] * lines
-        for line in reversed(range(lines)):
-            state = add(states[line], mapped(2 * plane + 1, line, state))
-            result[line] = state
-        leaving[chain + 1] = state
-        return result
-
-    swept_low = solve(0, T1, lambda line: scaled(0, line))
-    for line in range(lines):
-        for a in (0, 1):
-            low[pl.ds((2 * line + a) * 8, 8), :] = swept_low[line][a][1]
-    swept_high = solve(1, T2, lambda line: add(scaled(1, line), mapped(5, line, swept_low[line])))
-    fixed = solve(0, T3, lambda line: mapped(4, line, swept_high[line]))
-    keep_record(edge, leaving)
-    for line in range(lines):
-        total = add(swept_low[line], fixed[line])
-        for a in (0, 1):
-            for half in (0, 1):
-                place = pl.ds((2 * line + a) * width + half * 8, 8)
-                first[place, :] = total[a][half]
-                second[place, :] = swept_high[line][a][half]
+            for a in (0, 1):
+                for part in (0, 1):
+                    swept[state_rows(line, a, part), :] = result[line][a][part]
+
+
+def local_kernel(lines, vectors, keep, recv, swept, early, own_maps, edge, first, second, low, other_maps):
+    make_maps(lines, vectors, recv, other_maps)
+    for own in (0, 1):
+
+        @pl.when(lax.axis_index("gx") == own)
+        def _():
+            leaving = [None] * 6
+            maps = (other_maps, own_maps) if own else (own_maps, other_maps)
+            if own == 0:
+                swept_low = [
+                    [[swept[state_rows(line, a, part), :] for part in (0, 1)] for a in (0, 1)] for line in range(lines)
+                ]
+                for chain in (T1, U1):
+                    leaving[chain] = [
+                        [early[pl.ds(vector_row(chain, a), 8), :], early[pl.ds(unit_row(chain, a), 8), :]] for a in (0, 1)
+                    ]
+            else:
+                swept_low = sweep_plane(lines, maps[0], T1, lambda line: scaled(vectors, recv, line), leaving)
+            high_data = keep if own else recv
+            swept_high = sweep_plane(
+                lines,
+                maps[1],
+                T2,
+                lambda line: add(scaled(vectors, high_data, line), mapped(lines, maps[1], ACROSS, line, swept_low[line])),
+                leaving,
+            )
+            fixed = sweep_plane(
+                lines, maps[0], T3, lambda line: mapped(lines, maps[0], ACROSS, line, swept_high[line]), leaving
+            )
+            keep_record(edge, leaving)
+            for line in range(lines):
+                total = add(swept_low[line], fixed[line])
+                for a in (0, 1):
+                    low[pl.ds((2 * line + a) * 8, 8), :] = swept_low[line][a][1]
+                    for part in (0, 1):
+                        first[state_rows(line, a, part), :] = total[a][part]
+                        second[state_rows(line, a, part), :] = swept_high[line][a][part]
 
 
 def times(ref, row, step, state):
@@ -384,12 +422,18 @@
 
     recv = lax.ppermute(pack(True), "gx", swap)
     keep = pack(False)
+    swept, early, own_maps = call(
+        functools.partial(early_kernel, lines, vectors),
+        "early",
+        [(2 * lines * width, half), (ROWS, half), (12 * lines, half)],
+        (keep,),
+    )
     edge, first, second, low = call(
         functools.partial(local_kernel, lines, vectors),
         "local",
         [(ROWS, half), (2 * lines * width, half), (2 * lines * width, half), (2 * lines * 8, half)],
-        (keep, recv),
-        [pltpu.VMEM((2 * keep.shape[0], half), jnp.float32), pltpu.VMEM((24 * lines, half), jnp.float32)],
+        (keep, recv, swept, early, own_maps),
+        [pltpu.VMEM((12 * lines, half), jnp.float32)],
     )
     mids = []
     for level in range(levels - 1):

time: 25.1 us -> 25 us (level)
    pallas_call x10 -> x11, Pallas kernels: 4.31 us -> 4.37 us  [call(): pl.pallas_call(kernel, name=name, out_shape=[jax.ShapeDtypeStruct(s, jnp....]
  transfers between devices with their start and end apart: 6 -> 6, of which waited for: 6 -> 5; matrix products, arithmetic and copies ran while one was open for 0% -> 0% of each run, Pallas kernels for 7% -> 8%
where the time goes in v4:
time: 25 us; the launch traced here: 24.8 us
  waiting for transfers between devices  12.7 us (51%)
  starting transfers between devices  7.67 us (31%)
  Pallas kernels  4.37 us (17%)
    ppermute x3, waiting for transfers between devices, per_device(): got = lax.ppermute(edge, 'gy', [(j, j ^ 1 << level) for j in range(count)])  8.26 us
    ppermute x3, starting transfers between devices, per_device(): got = lax.ppermute(edge, 'gy', [(j, j ^ 1 << level) for j in range(count)])  6.62 us
    pallas_call x11, Pallas kernels, call(): pl.pallas_call(kernel, name=name, out_shape=[jax.ShapeDtypeStruct(s, jnp....  4.37 us
    ppermute x1, waiting for transfers between devices, per_device(): got = lax.ppermute(edge, ('gx', 'gy'), across)  4.27 us
    ppermute x1, starting transfers between devices, per_device(): recv = lax.ppermute(pack(True), 'gx', swap)  0.56 us
  transfers between devices with their start and end apart: 6, of which 5 were waited for; matrix products, arithmetic and copies ran while one was open for 0% of the time, Pallas kernels for 8%

profile of v4, /device:TPU:0, one launch (start us, length us, event | category | flops | bytes accessed | tf_op | source)
XLA Modules:
  0.0 24.8 jit_solution(7686713062508396058)
XLA Ops:
  0.0 1.0 %pack_away.1 = f32[16,16,2,128]{3,2,1,0:T(2,128)S(1)} custom-call(f32[1,16,8,2,256]{4,3,2,1,0:T(2,128)} %krylov.3, f32[1,16,2,2,256]{4,3,2,1,0:T(2,128)} %inverse.3, f32[1,16,2,2,256]{4,3,2,1,0:T(2,128)} %back.3, f32[1,16,2,2,256]{4,3,2,1,0:T(2,128)} %front.3, f32[1,16,2,2,256]{4,3,2,1,0:T(2,128)} %left.3, f32[1,16,2,2,256]{4,3,2,1,0:T(2,128)} %right.3), custom_call_target="tpu_custom_call" | custom-call | tf_op jit(solution)/shard_map/pack_away/pallas_call | solution.py:69
  1.0 0.6 %collective-permute-start = (f32[512,128]{1,0:T(8,128)S(1)}, f32[512,128]{1,0:T(8,128)S(1)}, u32[]{:S(2)}, u32[]{:S(2)}) collective-permute-start(f32[512,128]{1,0:T(8,128)S(1)} %bitcast.7), channel_id=1, source_target_pairs={{0,16},{16,0},{1,17},{17,1},{2,18},{18,2},{3,19},{19,3},{4,20},{20... | collective-permute-start | bytes 786440 | tf_op jit(solution)/shard_map/ppermute | solution.py:423
  1.5 1.0 %pack_own.1 = f32[16,16,2,128]{3,2,1,0:T(2,128)S(1)} custom-call(f32[1,16,8,2,256]{4,3,2,1,0:T(2,128)} %krylov.3, f32[1,16,2,2,256]{4,3,2,1,0:T(2,128)} %inverse.3, f32[1,16,2,2,256]{4,3,2,1,0:T(2,128)} %back.3, f32[1,16,2,2,256]{4,3,2,1,0:T(2,128)} %front.3, f32[1,16,2,2,256]{4,3,2,1,0:T(2,128)} %left.3, f32[1,16,2,2,256]{4,3,2,1,0:T(2,128)} %right.3), custom_call_target="tpu_custom_call" | custom-call | tf_op jit(solution)/shard_map/pack_own/pallas_call | solution.py:69
  2.5 0.2 early.1
  2.7 0.0 collective-permute-done.recv
  2.7 0.4 %local.1 = (f32[168,128]{1,0:T(8,128)S(1)}, f32[512,128]{1,0:T(8,128)S(1)}, f32[512,128]{1,0:T(8,128)S(1)}, f32[256,128]{1,0:T(8,128)S(1)}) custom-call(f32[512,128]{1,0:T(8,128)S(1)} %bitcast.5, f32[512,128]{1,0:T(8,128)S(1)} %collective-permute-done.recv, f32[512,128]{1,0:T(8,128)S(1)} %get-tuple-element.20.swept, f32[168,128]{1,0:T(8,128)S(1)} %get-tuple-element.21.early, ...), custom_call_target="tpu_custom_call" | custom-call | tf_op jit(solution)/shard_map/local/pallas_call | solution.py:69
  3.1 2.9 %collective-permute-start.1 = (f32[168,128]{1,0:T(8,128)S(1)}, f32[168,128]{1,0:T(8,128)S(1)}, u32[]{:S(2)}, u32[]{:S(2)}) collective-permute-start(f32[168,128]{1,0:T(8,128)S(1)} %get-tuple-element.23.mine), channel_id=1, source_target_pairs={{0,1},{1,0},{2,3},{3,2},{4,5},{5,4},{6,7},{7,6},{8,9},{9,8},{10,11... | collective-permute-start | bytes 258056 | tf_op jit(solution)/shard_map/ppermute | solution.py:440
  6.0 2.9 %collective-permute-done.1.other = f32[168,128]{1,0:T(8,128)S(1)} collective-permute-done((f32[168,128]{1,0:T(8,128)S(1)}, f32[168,128]{1,0:T(8,128)S(1)}, u32[]{:S(2)}, u32[]{:S(2)}) %collective-permute-start.1) | collective-permute-done | bytes 86048 | tf_op jit(solution)/shard_map/ppermute | solution.py:440
  8.9 0.1 merge0.1
  9.0 1.8 %collective-permute-start.2 = (f32[168,128]{1,0:T(8,128)S(1)}, f32[168,128]{1,0:T(8,128)S(1)}, u32[]{:S(2)}, u32[]{:S(2)}) collective-permute-start(f32[168,128]{1,0:T(8,128)S(1)} %get-tuple-element.24.mine), channel_id=1, source_target_pairs={{0,2},{1,3},{2,0},{3,1},{4,6},{5,7},{6,4},{7,5},{8,10},{9,11},{10,... | collective-permute-start | bytes 258056 | tf_op jit(solution)/shard_map/ppermute | solution.py:440
  10.8 2.7 %collective-permute-done.2.other = f32[168,128]{1,0:T(8,128)S(1)} collective-permute-done((f32[168,128]{1,0:T(8,128)S(1)}, f32[168,128]{1,0:T(8,128)S(1)}, u32[]{:S(2)}, u32[]{:S(2)}) %collective-permute-start.2) | collective-permute-done | bytes 86048 | tf_op jit(solution)/shard_map/ppermute | solution.py:440
  13.5 0.1 merge1.1
  13.6 1.9 %collective-permute-start.3 = (f32[168,128]{1,0:T(8,128)S(1)}, f32[168,128]{1,0:T(8,128)S(1)}, u32[]{:S(2)}, u32[]{:S(2)}) collective-permute-start(f32[168,128]{1,0:T(8,128)S(1)} %get-tuple-element.25.mine), channel_id=1, source_target_pairs={{0,4},{1,5},{2,6},{3,7},{4,0},{5,1},{6,2},{7,3},{8,12},{9,13},{10,... | collective-permute-start | bytes 258056 | tf_op jit(solution)/shard_map/ppermute | solution.py:440
  15.5 2.7 %collective-permute-done.3.other = f32[168,128]{1,0:T(8,128)S(1)} collective-permute-done((f32[168,128]{1,0:T(8,128)S(1)}, f32[168,128]{1,0:T(8,128)S(1)}, u32[]{:S(2)}, u32[]{:S(2)}) %collective-permute-start.3) | collective-permute-done | bytes 86048 | tf_op jit(solution)/shard_map/ppermute | solution.py:440
  18.1 0.1 merge2.1
  18.2 0.1 collective-permute-start.4
  18.3 4.3 %collective-permute-done.4.other = f32[72,128]{1,0:T(8,128)S(1)} collective-permute-done((f32[72,128]{1,0:T(8,128)S(1)}, f32[72,128]{1,0:T(8,128)S(1)}, u32[]{:S(2)}, u32[]{:S(2)}) %collective-permute-start.4) | collective-permute-done | bytes 36896 | tf_op jit(solution)/shard_map/ppermute | solution.py:451
  22.6 0.2 finish.1
  22.8 0.4 %collective-permute-start.5 = (f32[256,128]{1,0:T(8,128)S(1)}, f32[256,128]{1,0:T(8,128)S(1)}, u32[]{:S(2)}, u32[]{:S(2)}) collective-permute-start(f32[256,128]{1,0:T(8,128)S(1)} %get-tuple-element.33), channel_id=1, source_target_pairs={{0,16},{16,0},{1,17},{17,1},{2,18},{18,2},{3,19},{19,3},{4,20},{20... | collective-permute-start | bytes 393224 | tf_op jit(solution)/shard_map/ppermute | solution.py:459
  23.2 0.1 own.1
  23.3 0.7 %store.1.before = f32[1,16,8,2,256]{4,3,2,1,0:T(2,128)} custom-call(f32[16,8,2,128]{3,2,1,0:T(2,128)S(1)} %bitcast.6), custom_call_target="tpu_custom_call" | custom-call | tf_op jit(solution)/shard_map/store/pallas_call | solution.py:69
  24.0 0.2 collective-permute-done.5
  24.2 0.7 %last.1 = f32[1,16,8,2,256]{4,3,2,1,0:T(2,128)} custom-call(f32[16,8,2,128]{3,2,1,0:T(2,128)S(1)} %bitcast.8, f32[1,16,8,2,256]{4,3,2,1,0:T(2,128)} %store.1.before), custom_call_target="tpu_custom_call", output_to_operand_aliasing={{}: (1, {})} | custom-call | tf_op jit(solution)/shard_map/last/pallas_call | solution.py:69
Async XLA Ops:
  1.0 1.7 %collective-permute-start = (f32[512,128]{1,0:T(8,128)S(1)}, f32[512,128]{1,0:T(8,128)S(1)}, u32[]{:S(2)}, u32[]{:S(2)}) collective-permute-start(f32[512,128]{1,0:T(8,128)S(1)} %bitcast.7), channel_id=1, source_target_pairs={{0,16},{16,0},{1,17},{17,1},{2,18},{18,2},{3,19},{19,3},{4,20},{20... | collective-permute-start | bytes 786440 | tf_op jit(solution)/shard_map/ppermute | solution.py:423
  3.1 5.8 %collective-permute-start.1 = (f32[168,128]{1,0:T(8,128)S(1)}, f32[168,128]{1,0:T(8,128)S(1)}, u32[]{:S(2)}, u32[]{:S(2)}) collective-permute-start(f32[168,128]{1,0:T(8,128)S(1)} %get-tuple-element.23.mine), channel_id=1, source_target_pairs={{0,1},{1,0},{2,3},{3,2},{4,5},{5,4},{6,7},{7,6},{8,9},{9,8},{10,11... | collective-permute-start | bytes 258056 | tf_op jit(solution)/shard_map/ppermute | solution.py:440
  9.0 4.6 %collective-permute-start.2 = (f32[168,128]{1,0:T(8,128)S(1)}, f32[168,128]{1,0:T(8,128)S(1)}, u32[]{:S(2)}, u32[]{:S(2)}) collective-permute-start(f32[168,128]{1,0:T(8,128)S(1)} %get-tuple-element.24.mine), channel_id=1, source_target_pairs={{0,2},{1,3},{2,0},{3,1},{4,6},{5,7},{6,4},{7,5},{8,10},{9,11},{10,... | collective-permute-start | bytes 258056 | tf_op jit(solution)/shard_map/ppermute | solution.py:440
  13.6 4.6 %collective-permute-start.3 = (f32[168,128]{1,0:T(8,128)S(1)}, f32[168,128]{1,0:T(8,128)S(1)}, u32[]{:S(2)}, u32[]{:S(2)}) collective-permute-start(f32[168,128]{1,0:T(8,128)S(1)} %get-tuple-element.25.mine), channel_id=1, source_target_pairs={{0,4},{1,5},{2,6},{3,7},{4,0},{5,1},{6,2},{7,3},{8,12},{9,13},{10,... | collective-permute-start | bytes 258056 | tf_op jit(solution)/shard_map/ppermute | solution.py:440
  18.2 4.3 %collective-permute-start.4 = (f32[72,128]{1,0:T(8,128)S(1)}, f32[72,128]{1,0:T(8,128)S(1)}, u32[]{:S(2)}, u32[]{:S(2)}) collective-permute-start(f32[72,128]{1,0:T(8,128)S(1)} %get-tuple-element.26.mine), channel_id=1, source_target_pairs={{0,24},{1,25},{2,26},{3,27},{4,28},{5,29},{6,30},{7,31},{8,16},{9,... | collective-permute-start | bytes 110600 | tf_op jit(solution)/shard_map/ppermute | solution.py:451
  22.8 1.4 %collective-permute-start.5 = (f32[256,128]{1,0:T(8,128)S(1)}, f32[256,128]{1,0:T(8,128)S(1)}, u32[]{:S(2)}, u32[]{:S(2)}) collective-permute-start(f32[256,128]{1,0:T(8,128)S(1)} %get-tuple-element.33), channel_id=1, source_target_pairs={{0,16},{16,0},{1,17},{17,1},{2,18},{18,2},{3,19},{19,3},{4,20},{20... | collective-permute-start | bytes 393224 | tf_op jit(solution)/shard_map/ppermute | solution.py:459

commit v5 on v4

--- a/solution.py
+++ b/solution.py
@@ -292,37 +292,71 @@
     edge[units, :] = jnp.where(next_low, pair[0][...], pair[1][...])
 
 
-def write_plane(lines, own, enters, first, second, low, target):
+def compose_kernel(lines, levels, *refs):
+    mids, (first, second, low, own, away) = refs[: levels - 1], refs[levels - 1 :]
+    place, core = lax.axis_index("gy"), lax.axis_index("gx")
+    row = lax.broadcasted_iota(jnp.int32, (8, 128), 0)
+    none = jnp.zeros((8, 128), jnp.float32)
+    in_low = jnp.bitwise_and(place, 1 << (levels - 1)) == 0
+
+    def select(condition, x, y):
+        return [[jnp.where(condition, p, q) for p, q in zip(s, t)] for s, t in zip(x, y)]
+
+    enters = []
+    for direction, number in CHAINS:
+        one = [jnp.where(row == 2 * number + a, 1.0, 0.0) for a in (0, 1)]
+        here = in_low if direction else ~in_low
+        enters.append([[none, jnp.where(here, one[a], 0.0)] for a in (0, 1)])
+    for level in reversed(range(levels - 1)):
+        ref = mids[level]
+        m = []
+        for chain in range(6):
+            base = [[ref[pl.ds(vector_row(chain, a), 8), :], none] for a in (0, 1)]
+            terms = [response(ref, chain, c, enters[c]) for c in feeds(chain)]
+            if chain >= UNITS:
+                terms += [response(ref, chain, c, enters[c]) for c in range(UNITS, chain + 1)]
+            m.append(total(base, *terms))
+        is_low = jnp.bitwise_and(place, 1 << level) == 0
+        enters = [
+            select(is_low, enters[c], m[c]) if CHAINS[c][0] == 0 else select(is_low, m[c], enters[c])
+            for c in range(6)
+        ]
+
     width = 8 + 2 * UNITS
-
-    def columns(ref, start, chains):
-        value = None
-        for place, chain in chains:
-            for b in (0, 1):
-                term = spread(ref, start + 2 * place + b, 8) * enters[chain][b][0]
-                value = term if value is None else value + term
-        return value
-
-    core = lax.axis_index("gx")
     units = [(c, c) for c in range(UNITS)]
-    for plane in (0, 1):
-
-        @pl.when(core == (plane if own else 1 - plane))
-        def _():
-            source = second if plane else first
-            for line in range(lines):
-                for a in (0, 1):
-                    start = (2 * line + a) * width
-                    value = source[pl.ds(start, 8), :] + columns(source, start + 8, units)
-                    if plane == 0:
-                        value = value + columns(low, (2 * line + a) * 8, [(T1, T3), (U1, U3)])
-                    target[pl.ds(line * 16 + a, 8, stride=2), :] = value
-
-
-def finish_kernel(lines, levels, mine, other, *refs):
-    mids, (first, second, low, sent, entry, ups, downs) = refs[: levels - 1], refs[levels - 1 :]
-    place = lax.axis_index("gy")
-    is_low = jnp.bitwise_and(place, 1 << (levels - 1)) == 0
+    for line in range(lines):
+        for a in (0, 1):
+            start = (2 * line + a) * width
+            planes = []
+            for source, extra in ((first, [(T1, T3), (U1, U3)]), (second, [])):
+                value = [source[pl.ds(start, 8), :], none]
+                pairs = [(source, start + 8, pair) for pair in units]
+                pairs += [(low, (2 * line + a) * 8, pair) for pair in extra]
+                for ref, begin, (column, chain) in pairs:
+                    for b in (0, 1):
+                        factor = spread(ref, begin + 2 * column + b, 8)
+                        value = [v + factor * e for v, e in zip(value, enters[chain][b])]
+                planes.append(value)
+            for part in (0, 1):
+                mine, other = planes[0][part], planes[1][part]
+                own[state_rows(line, a, part), :] = jnp.where(core == 0, mine, other)
+                away[state_rows(line, a, part), :] = jnp.where(core == 0, other, mine)
+
+
+def apply_map(lines, ref, entry, target):
+    width = 8 + 2 * UNITS
+    for line in range(lines):
+        for a in (0, 1):
+            start = (2 * line + a) * width
+            value = ref[pl.ds(start, 8), :]
+            for number in range(3):
+                for b in (0, 1):
+                    value = value + spread(ref, start + 8 + 2 * number + b, 8) * entry[number][b]
+            target[pl.ds(line * 16 + a, 8, stride=2), :] = value
+
+
+def finish_kernel(lines, levels, mine, other, away, sent, entry, ups, downs):
+    is_low = jnp.bitwise_and(lax.axis_index("gy"), 1 << (levels - 1)) == 0
     x, y = mine[...], other[...]
     ups[...] = jnp.where(is_low, x, y)
     downs[...] = jnp.where(is_low, y, x)
@@ -348,41 +382,23 @@
     m[U2] = total(base(downs, U2, U1), down(U2, T1, m[T1]), down(U2, T2, m[T2]))
     m[T3] = total(base(ups, T3, T1), up(T3, U1, m[U1]), up(T3, U2, m[U2]))
     m[U3] = total(base(downs, U3, U1), down(U3, T1, m[T1]), down(U3, T2, m[T2]), down(U3, T3, m[T3]))
-
-    def select(condition, x, y):
-        return [[jnp.where(condition, p, q) for p, q in zip(s, t)] for s, t in zip(x, y)]
-
-    none = [[jnp.zeros((8, 128), jnp.float32)], [jnp.zeros((8, 128), jnp.float32)]]
-    enters = [none] * 6
-    for level in reversed(range(levels)):
-        if level < levels - 1:
-            ref = mids[level]
-            m = []
-            for chain in range(6):
-                terms = [response(ref, chain, c, enters[c]) for c in feeds(chain)]
-                if chain >= UNITS:
-                    terms += [response(ref, chain, c, enters[c]) for c in range(UNITS, chain + 1)]
-                m.append(total(base(ref, chain, T1), *terms))
-        is_low = jnp.bitwise_and(place, 1 << level) == 0
-        enters = [
-            select(is_low, enters[c], m[c]) if CHAINS[c][0] == 0 else select(is_low, m[c], enters[c])
-            for c in range(6)
-        ]
-
-    write_plane(lines, False, enters, first, second, low, sent)
-    for chain in range(6):
-        for a in (0, 1):
-            entry[pl.ds(vector_row(chain, a), 8), :] = enters[chain][a][0]
+    enters = [
+        [jnp.where(is_low, m[2 * number + 1][b][0], m[2 * number][b][0]) for b in (0, 1)] for number in range(3)
+    ]
+    apply_map(lines, away, enters, sent)
+    for number in range(3):
+        for b in (0, 1):
+            entry[pl.ds((2 * number + b) * 8, 8), :] = enters[number][b]
+
+
+def own_kernel(lines, entry, own, kept):
+    enters = [[entry[pl.ds((2 * number + b) * 8, 8), :] for b in (0, 1)] for number in range(3)]
+    apply_map(lines, own, enters, kept)
 
 
 def part_copy(half, position, value, out, sem):
     lanes = pl.ds(pl.multiple_of(position * half, half), half)
     return pltpu.make_async_copy(value, out.at[0, :, :, :, lanes], sem)
-
-
-def own_kernel(lines, entry, first, second, low, kept):
-    enters = [[[entry[pl.ds(vector_row(chain, a), 8), :]] for a in (0, 1)] for chain in range(6)]
-    write_plane(lines, True, enters, first, second, low, kept)
 
 
 def store_kernel(half, kept, out, sem):
@@ -449,17 +465,21 @@
         mids.append(mid)
     across = [(core * count + j, (1 - core) * count + (j ^ (count // 2))) for core in (0, 1) for j in range(count)]
     got = lax.ppermute(edge, ("gx", "gy"), across)
+    own, away = call(
+        functools.partial(compose_kernel, lines, levels),
+        "compose",
+        [(2 * lines * width, half)] * 2,
+        (*mids, first, second, low),
+    )
     sent, entry = call(
         functools.partial(finish_kernel, lines, levels),
         "finish",
-        [(lines * 16, half), (VECTOR_ROWS, half)],
-        (edge, got, *mids, first, second, low),
+        [(lines * 16, half), (VECTOR_ROWS // 2, half)],
+        (edge, got, away),
         [pltpu.VMEM((LAST_ROWS, half), jnp.float32)] * 2,
     )
     got = lax.ppermute(sent, "gx", swap)
-    (kept,) = call(
-        functools.partial(own_kernel, lines), "own", [(lines * 16, half)], (entry, first, second, low)
-    )
+    (kept,) = call(functools.partial(own_kernel, lines), "own", [(lines * 16, half)], (entry, own))
     (out,) = call(
         functools.partial(store_kernel, half),
         "store",

time: 25 us -> 24.9 us (level)
  waiting for transfers between devices: 12.7 us -> 12.3 us
  Pallas kernels: 4.37 us -> 4.74 us
    ppermute x1, waiting for transfers between devices: 4.27 us -> 3.75 us  [per_device(): got = lax.ppermute(edge, ('gx', 'gy'), across)]
    pallas_call x11 -> x12, Pallas kernels: 4.37 us -> 4.74 us  [call(): pl.pallas_call(kernel, name=name, out_shape=[jax.ShapeDtypeStruct(s, jnp....]
  transfers between devices with their start and end apart: 6 -> 6, of which waited for: 5 -> 5; matrix products, arithmetic and copies ran while one was open for 0% -> 0% of each run, Pallas kernels for 8% -> 10%
where the time goes in v5:
time: 24.9 us; the launch traced here: 24.7 us
  waiting for transfers between devices  12.3 us (49%)
  starting transfers between devices  7.63 us (31%)
  Pallas kernels  4.74 us (19%)
    ppermute x3, waiting for transfers between devices, per_device(): got = lax.ppermute(edge, 'gy', [(j, j ^ 1 << level) for j in range(count)])  8.26 us
    ppermute x3, starting transfers between devices, per_device(): got = lax.ppermute(edge, 'gy', [(j, j ^ 1 << level) for j in range(count)])  6.62 us
    pallas_call x12, Pallas kernels, call(): pl.pallas_call(kernel, name=name, out_shape=[jax.ShapeDtypeStruct(s, jnp....  4.74 us
    ppermute x1, waiting for transfers between devices, per_device(): got = lax.ppermute(edge, ('gx', 'gy'), across)  3.75 us
    ppermute x1, starting transfers between devices, per_device(): recv = lax.ppermute(pack(True), 'gx', swap)  0.56 us
  transfers between devices with their start and end apart: 6, of which 5 were waited for; matrix products, arithmetic and copies ran while one was open for 0% of the time, Pallas kernels for 10%

profile of v5, /device:TPU:0, one launch (start us, length us, event | category | flops | bytes accessed | tf_op | source)
XLA Modules:
  0.0 24.7 jit_solution(2630977845435446932)
XLA Ops:
  0.0 1.0 %pack_away.1 = f32[16,16,2,128]{3,2,1,0:T(2,128)S(1)} custom-call(f32[1,16,8,2,256]{4,3,2,1,0:T(2,128)} %krylov.3, f32[1,16,2,2,256]{4,3,2,1,0:T(2,128)} %inverse.3, f32[1,16,2,2,256]{4,3,2,1,0:T(2,128)} %back.3, f32[1,16,2,2,256]{4,3,2,1,0:T(2,128)} %front.3, f32[1,16,2,2,256]{4,3,2,1,0:T(2,128)} %left.3, f32[1,16,2,2,256]{4,3,2,1,0:T(2,128)} %right.3), custom_call_target="tpu_custom_call" | custom-call | tf_op jit(solution)/shard_map/pack_away/pallas_call | solution.py:69
  1.0 0.6 %collective-permute-start = (f32[512,128]{1,0:T(8,128)S(1)}, f32[512,128]{1,0:T(8,128)S(1)}, u32[]{:S(2)}, u32[]{:S(2)}) collective-permute-start(f32[512,128]{1,0:T(8,128)S(1)} %bitcast.7), channel_id=1, source_target_pairs={{0,16},{16,0},{1,17},{17,1},{2,18},{18,2},{3,19},{19,3},{4,20},{20... | collective-permute-start | bytes 786440 | tf_op jit(solution)/shard_map/ppermute | solution.py:439
  1.5 1.0 %pack_own.1 = f32[16,16,2,128]{3,2,1,0:T(2,128)S(1)} custom-call(f32[1,16,8,2,256]{4,3,2,1,0:T(2,128)} %krylov.3, f32[1,16,2,2,256]{4,3,2,1,0:T(2,128)} %inverse.3, f32[1,16,2,2,256]{4,3,2,1,0:T(2,128)} %back.3, f32[1,16,2,2,256]{4,3,2,1,0:T(2,128)} %front.3, f32[1,16,2,2,256]{4,3,2,1,0:T(2,128)} %left.3, f32[1,16,2,2,256]{4,3,2,1,0:T(2,128)} %right.3), custom_call_target="tpu_custom_call" | custom-call | tf_op jit(solution)/shard_map/pack_own/pallas_call | solution.py:69
  2.5 0.2 early.1
  2.7 0.0 collective-permute-done.recv
  2.7 0.4 %local.1 = (f32[168,128]{1,0:T(8,128)S(1)}, f32[512,128]{1,0:T(8,128)S(1)}, f32[512,128]{1,0:T(8,128)S(1)}, f32[256,128]{1,0:T(8,128)S(1)}) custom-call(f32[512,128]{1,0:T(8,128)S(1)} %bitcast.5, f32[512,128]{1,0:T(8,128)S(1)} %collective-permute-done.recv, f32[512,128]{1,0:T(8,128)S(1)} %get-tuple-element.22.swept, f32[168,128]{1,0:T(8,128)S(1)} %get-tuple-element.23.early, ...), custom_call_target="tpu_custom_call" | custom-call | tf_op jit(solution)/shard_map/local/pallas_call | solution.py:69
  3.1 2.9 %collective-permute-start.1 = (f32[168,128]{1,0:T(8,128)S(1)}, f32[168,128]{1,0:T(8,128)S(1)}, u32[]{:S(2)}, u32[]{:S(2)}) collective-permute-start(f32[168,128]{1,0:T(8,128)S(1)} %get-tuple-element.25.mine), channel_id=1, source_target_pairs={{0,1},{1,0},{2,3},{3,2},{4,5},{5,4},{6,7},{7,6},{8,9},{9,8},{10,11... | collective-permute-start | bytes 258056 | tf_op jit(solution)/shard_map/ppermute | solution.py:456
  6.0 2.9 %collective-permute-done.1.other = f32[168,128]{1,0:T(8,128)S(1)} collective-permute-done((f32[168,128]{1,0:T(8,128)S(1)}, f32[168,128]{1,0:T(8,128)S(1)}, u32[]{:S(2)}, u32[]{:S(2)}) %collective-permute-start.1) | collective-permute-done | bytes 86048 | tf_op jit(solution)/shard_map/ppermute | solution.py:456
  8.9 0.1 merge0.1
  9.0 1.8 %collective-permute-start.2 = (f32[168,128]{1,0:T(8,128)S(1)}, f32[168,128]{1,0:T(8,128)S(1)}, u32[]{:S(2)}, u32[]{:S(2)}) collective-permute-start(f32[168,128]{1,0:T(8,128)S(1)} %get-tuple-element.26.mine), channel_id=1, source_target_pairs={{0,2},{1,3},{2,0},{3,1},{4,6},{5,7},{6,4},{7,5},{8,10},{9,11},{10,... | collective-permute-start | bytes 258056 | tf_op jit(solution)/shard_map/ppermute | solution.py:456
  10.8 2.7 %collective-permute-done.2.other = f32[168,128]{1,0:T(8,128)S(1)} collective-permute-done((f32[168,128]{1,0:T(8,128)S(1)}, f32[168,128]{1,0:T(8,128)S(1)}, u32[]{:S(2)}, u32[]{:S(2)}) %collective-permute-start.2) | collective-permute-done | bytes 86048 | tf_op jit(solution)/shard_map/ppermute | solution.py:456
  13.5 0.1 merge1.1
  13.6 1.9 %collective-permute-start.3 = (f32[168,128]{1,0:T(8,128)S(1)}, f32[168,128]{1,0:T(8,128)S(1)}, u32[]{:S(2)}, u32[]{:S(2)}) collective-permute-start(f32[168,128]{1,0:T(8,128)S(1)} %get-tuple-element.27.mine), channel_id=1, source_target_pairs={{0,4},{1,5},{2,6},{3,7},{4,0},{5,1},{6,2},{7,3},{8,12},{9,13},{10,... | collective-permute-start | bytes 258056 | tf_op jit(solution)/shard_map/ppermute | solution.py:456
  15.5 2.7 %collective-permute-done.3.other = f32[168,128]{1,0:T(8,128)S(1)} collective-permute-done((f32[168,128]{1,0:T(8,128)S(1)}, f32[168,128]{1,0:T(8,128)S(1)}, u32[]{:S(2)}, u32[]{:S(2)}) %collective-permute-start.3) | collective-permute-done | bytes 86048 | tf_op jit(solution)/shard_map/ppermute | solution.py:456
  18.1 0.1 merge2.1
  18.2 0.1 collective-permute-start.4
  18.3 0.5 %compose.1 = (f32[512,128]{1,0:T(8,128)S(1)}, f32[512,128]{1,0:T(8,128)S(1)}) custom-call(f32[168,128]{1,0:T(8,128)S(1)} %get-tuple-element.29.refs_0_, f32[168,128]{1,0:T(8,128)S(1)} %get-tuple-element.30.refs_1_, f32[168,128]{1,0:T(8,128)S(1)} %get-tuple-element.31.refs_2_, f32[512,128]{1,0:T(8,128)S(1)} %get-tuple-element.32.refs_3_, ...), custom_call_target="tpu_custom_call" | custom-call | tf_op jit(solution)/shard_map/compose/pallas_call | solution.py:69
  18.8 3.8 %collective-permute-done.4.other = f32[72,128]{1,0:T(8,128)S(1)} collective-permute-done((f32[72,128]{1,0:T(8,128)S(1)}, f32[72,128]{1,0:T(8,128)S(1)}, u32[]{:S(2)}, u32[]{:S(2)}) %collective-permute-start.4) | collective-permute-done | bytes 36896 | tf_op jit(solution)/shard_map/ppermute | solution.py:467
  22.6 0.1 finish.1
  22.7 0.4 %collective-permute-start.5 = (f32[256,128]{1,0:T(8,128)S(1)}, f32[256,128]{1,0:T(8,128)S(1)}, u32[]{:S(2)}, u32[]{:S(2)}) collective-permute-start(f32[256,128]{1,0:T(8,128)S(1)} %get-tuple-element.36), channel_id=1, source_target_pairs={{0,16},{16,0},{1,17},{17,1},{2,18},{18,2},{3,19},{19,3},{4,20},{20... | collective-permute-start | bytes 393224 | tf_op jit(solution)/shard_map/ppermute | solution.py:481
  23.0 0.1 own.1
  23.1 0.7 %store.1.before = f32[1,16,8,2,256]{4,3,2,1,0:T(2,128)} custom-call(f32[16,8,2,128]{3,2,1,0:T(2,128)S(1)} %bitcast.6), custom_call_target="tpu_custom_call" | custom-call | tf_op jit(solution)/shard_map/store/pallas_call | solution.py:69
  23.8 0.3 %collective-permute-done.5 = f32[256,128]{1,0:T(8,128)S(1)} collective-permute-done((f32[256,128]{1,0:T(8,128)S(1)}, f32[256,128]{1,0:T(8,128)S(1)}, u32[]{:S(2)}, u32[]{:S(2)}) %collective-permute-start.5) | collective-permute-done | bytes 131104 | tf_op jit(solution)/shard_map/ppermute | solution.py:481
  24.1 0.7 %last.1 = f32[1,16,8,2,256]{4,3,2,1,0:T(2,128)} custom-call(f32[16,8,2,128]{3,2,1,0:T(2,128)S(1)} %bitcast.8, f32[1,16,8,2,256]{4,3,2,1,0:T(2,128)} %store.1.before), custom_call_target="tpu_custom_call", output_to_operand_aliasing={{}: (1, {})} | custom-call | tf_op jit(solution)/shard_map/last/pallas_call | solution.py:69
Async XLA Ops:
  1.0 1.7 %collective-permute-start = (f32[512,128]{1,0:T(8,128)S(1)}, f32[512,128]{1,0:T(8,128)S(1)}, u32[]{:S(2)}, u32[]{:S(2)}) collective-permute-start(f32[512,128]{1,0:T(8,128)S(1)} %bitcast.7), channel_id=1, source_target_pairs={{0,16},{16,0},{1,17},{17,1},{2,18},{18,2},{3,19},{19,3},{4,20},{20... | collective-permute-start | bytes 786440 | tf_op jit(solution)/shard_map/ppermute | solution.py:439
  3.1 5.8 %collective-permute-start.1 = (f32[168,128]{1,0:T(8,128)S(1)}, f32[168,128]{1,0:T(8,128)S(1)}, u32[]{:S(2)}, u32[]{:S(2)}) collective-permute-start(f32[168,128]{1,0:T(8,128)S(1)} %get-tuple-element.25.mine), channel_id=1, source_target_pairs={{0,1},{1,0},{2,3},{3,2},{4,5},{5,4},{6,7},{7,6},{8,9},{9,8},{10,11... | collective-permute-start | bytes 258056 | tf_op jit(solution)/shard_map/ppermute | solution.py:456
  9.0 4.6 %collective-permute-start.2 = (f32[168,128]{1,0:T(8,128)S(1)}, f32[168,128]{1,0:T(8,128)S(1)}, u32[]{:S(2)}, u32[]{:S(2)}) collective-permute-start(f32[168,128]{1,0:T(8,128)S(1)} %get-tuple-element.26.mine), channel_id=1, source_target_pairs={{0,2},{1,3},{2,0},{3,1},{4,6},{5,7},{6,4},{7,5},{8,10},{9,11},{10,... | collective-permute-start | bytes 258056 | tf_op jit(solution)/shard_map/ppermute | solution.py:456
  13.6 4.6 %collective-permute-start.3 = (f32[168,128]{1,0:T(8,128)S(1)}, f32[168,128]{1,0:T(8,128)S(1)}, u32[]{:S(2)}, u32[]{:S(2)}) collective-permute-start(f32[168,128]{1,0:T(8,128)S(1)} %get-tuple-element.27.mine), channel_id=1, source_target_pairs={{0,4},{1,5},{2,6},{3,7},{4,0},{5,1},{6,2},{7,3},{8,12},{9,13},{10,... | collective-permute-start | bytes 258056 | tf_op jit(solution)/shard_map/ppermute | solution.py:456
  18.2 4.3 %collective-permute-start.4 = (f32[72,128]{1,0:T(8,128)S(1)}, f32[72,128]{1,0:T(8,128)S(1)}, u32[]{:S(2)}, u32[]{:S(2)}) collective-permute-start(f32[72,128]{1,0:T(8,128)S(1)} %get-tuple-element.28.mine), channel_id=1, source_target_pairs={{0,24},{1,25},{2,26},{3,27},{4,28},{5,29},{6,30},{7,31},{8,16},{9,... | collective-permute-start | bytes 110600 | tf_op jit(solution)/shard_map/ppermute | solution.py:467
  22.7 1.4 %collective-permute-start.5 = (f32[256,128]{1,0:T(8,128)S(1)}, f32[256,128]{1,0:T(8,128)S(1)}, u32[]{:S(2)}, u32[]{:S(2)}) collective-permute-start(f32[256,128]{1,0:T(8,128)S(1)} %get-tuple-element.36), channel_id=1, source_target_pairs={{0,16},{16,0},{1,17},{17,1},{2,18},{18,2},{3,19},{19,3},{4,20},{20... | collective-permute-start | bytes 393224 | tf_op jit(solution)/shard_map/ppermute | solution.py:481

commit v6 on v5

--- a/solution.py
+++ b/solution.py
@@ -65,10 +65,9 @@
     return ref[pl.ds(row, count, stride=0), :]
 
 
-def call(kernel, name, outs, ins, scratch=(), specs=None, out_specs=None, aliases={}):
+def call(kernel, outs, ins, scratch=(), specs=None, out_specs=None, aliases={}):
     return pl.pallas_call(
         kernel,
-        name=name,
         out_shape=[jax.ShapeDtypeStruct(s, jnp.float32) for s in outs],
         in_specs=specs or [VMEM] * len(ins),
         out_specs=out_specs or [VMEM] * len(outs),
@@ -355,7 +354,7 @@
             target[pl.ds(line * 16 + a, 8, stride=2), :] = value
 
 
-def finish_kernel(lines, levels, mine, other, away, sent, entry, ups, downs):
+def finish_kernel(levels, mine, other, entry, ups, downs):
     is_low = jnp.bitwise_and(lax.axis_index("gy"), 1 << (levels - 1)) == 0
     x, y = mine[...], other[...]
     ups[...] = jnp.where(is_low, x, y)
@@ -385,7 +384,6 @@
     enters = [
         [jnp.where(is_low, m[2 * number + 1][b][0], m[2 * number][b][0]) for b in (0, 1)] for number in range(3)
     ]
-    apply_map(lines, away, enters, sent)
     for number in range(3):
         for b in (0, 1):
             entry[pl.ds((2 * number + b) * 8, 8), :] = enters[number][b]
@@ -428,7 +426,6 @@
     def pack(away):
         (out,) = call(
             functools.partial(pack_kernel, half, vectors, away),
-            "pack_away" if away else "pack_own",
             [(lines, vectors + 8, 2, half)],
             arguments,
             [pltpu.SemaphoreType.DMA((5,))],
@@ -440,13 +437,11 @@
     keep = pack(False)
     swept, early, own_maps = call(
         functools.partial(early_kernel, lines, vectors),
-        "early",
         [(2 * lines * width, half), (ROWS, half), (12 * lines, half)],
         (keep,),
     )
     edge, first, second, low = call(
         functools.partial(local_kernel, lines, vectors),
-        "local",
         [(ROWS, half), (2 * lines * width, half), (2 * lines * width, half), (2 * lines * 8, half)],
         (keep, recv, swept, early, own_maps),
         [pltpu.VMEM((12 * lines, half), jnp.float32)],
@@ -457,7 +452,6 @@
         last = level == levels - 2
         edge, mid = call(
             functools.partial(merge_kernel, 1 << level, last),
-            f"merge{level}",
             [(LAST_ROWS if last else ROWS, half), (ROWS, half)],
             (edge, got),
             [pltpu.VMEM((ROWS, half), jnp.float32)] * 2 + [pltpu.VMEM((LAST_UNITS, half), jnp.float32)] * (2 * last),
@@ -466,34 +460,34 @@
     across = [(core * count + j, (1 - core) * count + (j ^ (count // 2))) for core in (0, 1) for j in range(count)]
     got = lax.ppermute(edge, ("gx", "gy"), across)
     own, away = call(
-        functools.partial(compose_kernel, lines, levels),
-        "compose",
-        [(2 * lines * width, half)] * 2,
-        (*mids, first, second, low),
-    )
-    sent, entry = call(
-        functools.partial(finish_kernel, lines, levels),
-        "finish",
-        [(lines * 16, half), (VECTOR_ROWS // 2, half)],
-        (edge, got, away),
+        functools.partial(compose_kernel, lines, levels), [(2 * lines * width, half)] * 2, (*mids, first, second, low)
+    )
+    away = lax.ppermute(away, "gx", swap)
+    (entry,) = call(
+        functools.partial(finish_kernel, levels),
+        [(VECTOR_ROWS // 2, half)],
+        (edge, got),
         [pltpu.VMEM((LAST_ROWS, half), jnp.float32)] * 2,
     )
-    got = lax.ppermute(sent, "gx", swap)
-    (kept,) = call(functools.partial(own_kernel, lines), "own", [(lines * 16, half)], (entry, own))
+    got_entry = lax.ppermute(entry, "gx", swap)
+
+    def plane_half(carries, ref):
+        (value,) = call(functools.partial(own_kernel, lines), [(lines * 16, half)], (carries, ref))
+        return value.reshape(lines, vectors, 2, half)
+
+    kept = plane_half(entry, own)
     (out,) = call(
         functools.partial(store_kernel, half),
-        "store",
         [krylov.shape],
-        [kept.reshape(lines, vectors, 2, half)],
+        [kept],
         [pltpu.SemaphoreType.DMA((1,))],
         specs=[ANY],
         out_specs=[HBM],
     )
     (out,) = call(
         functools.partial(last_kernel, half),
-        "last",
         [krylov.shape],
-        [got.reshape(lines, vectors, 2, half), out],
+        [plane_half(got_entry, away), out],
         [pltpu.SemaphoreType.DMA((1,))],
         specs=[ANY, HBM],
         out_specs=[HBM],

time: 24.9 us -> 25.6 us (1.028)
  starting transfers between devices: 7.63 us -> 10.5 us
  waiting for transfers between devices: 12.3 us -> 10.2 us
    ppermute x1, starting transfers between devices: 0.07 us -> 2.94 us  [per_device(): got = lax.ppermute(edge, ('gx', 'gy'), across)]
    ppermute x1, waiting for transfers between devices: 3.75 us -> 1.65 us  [per_device(): got = lax.ppermute(edge, ('gx', 'gy'), across)]
    pallas_call x12 -> x13, Pallas kernels: 4.74 us -> 4.76 us  [call(): pl.pallas_call(kernel, out_shape=[jax.ShapeDtypeStruct(s, jnp.float32) fo...]
  transfers between devices with their start and end apart: 6 -> 7, of which waited for: 5 -> 5; matrix products, arithmetic and copies ran while one was open for 0% -> 0% of each run, Pallas kernels for 10% -> 8%
where the time goes in v6:
time: 25.6 us; the launch traced here: 25.5 us
  starting transfers between devices  10.5 us (41%)
  waiting for transfers between devices  10.2 us (40%)
  Pallas kernels  4.76 us (19%)
    ppermute x3, waiting for transfers between devices, per_device(): got = lax.ppermute(edge, 'gy', [(j, j ^ 1 << level) for j in range(count)])  8.26 us
    ppermute x3, starting transfers between devices, per_device(): got = lax.ppermute(edge, 'gy', [(j, j ^ 1 << level) for j in range(count)])  6.62 us
    pallas_call x13, Pallas kernels, call(): pl.pallas_call(kernel, out_shape=[jax.ShapeDtypeStruct(s, jnp.float32) fo...  4.76 us
    ppermute x1, starting transfers between devices, per_device(): got = lax.ppermute(edge, ('gx', 'gy'), across)  2.94 us
    ppermute x1, waiting for transfers between devices, per_device(): got = lax.ppermute(edge, ('gx', 'gy'), across)  1.65 us
    ppermute x1, starting transfers between devices, per_device(): recv = lax.ppermute(pack(True), 'gx', swap)  0.56 us
  transfers between devices with their start and end apart: 7, of which 5 were waited for; matrix products, arithmetic and copies ran while one was open for 0% of the time, Pallas kernels for 8%

profile of v6, /device:TPU:0, one launch (start us, length us, event | category | flops | bytes accessed | tf_op | source)
XLA Modules:
  0.0 25.5 jit_solution(13425830553621568256)
XLA Ops:
  0.0 1.0 %shard_map.65 = f32[16,16,2,128]{3,2,1,0:T(2,128)S(1)} custom-call(f32[1,16,8,2,256]{4,3,2,1,0:T(2,128)} %krylov.3, f32[1,16,2,2,256]{4,3,2,1,0:T(2,128)} %inverse.3, f32[1,16,2,2,256]{4,3,2,1,0:T(2,128)} %back.3, f32[1,16,2,2,256]{4,3,2,1,0:T(2,128)} %front.3, f32[1,16,2,2,256]{4,3,2,1,0:T(2,128)} %left.3, f32[1,16,2,2,256]{4,3,2,1,0:T(2,128)} %right.3), custom_call_target="tpu_custom_call" | custom-call | tf_op jit(solution)/shard_map/pallas_call | solution.py:69
  1.0 0.6 %collective-permute-start = (f32[512,128]{1,0:T(8,128)S(1)}, f32[512,128]{1,0:T(8,128)S(1)}, u32[]{:S(2)}, u32[]{:S(2)}) collective-permute-start(f32[512,128]{1,0:T(8,128)S(1)} %bitcast.8), channel_id=1, source_target_pairs={{0,16},{16,0},{1,17},{17,1},{2,18},{18,2},{3,19},{19,3},{4,20},{20... | collective-permute-start | bytes 786440 | tf_op jit(solution)/shard_map/ppermute | solution.py:436
  1.5 1.0 %shard_map.64 = f32[16,16,2,128]{3,2,1,0:T(2,128)S(1)} custom-call(f32[1,16,8,2,256]{4,3,2,1,0:T(2,128)} %krylov.3, f32[1,16,2,2,256]{4,3,2,1,0:T(2,128)} %inverse.3, f32[1,16,2,2,256]{4,3,2,1,0:T(2,128)} %back.3, f32[1,16,2,2,256]{4,3,2,1,0:T(2,128)} %front.3, f32[1,16,2,2,256]{4,3,2,1,0:T(2,128)} %left.3, f32[1,16,2,2,256]{4,3,2,1,0:T(2,128)} %right.3), custom_call_target="tpu_custom_call" | custom-call | tf_op jit(solution)/shard_map/pallas_call | solution.py:69
  2.5 0.2 shard_map.66
  2.7 0.0 collective-permute-done.recv
  2.7 0.4 %shard_map.67 = (f32[168,128]{1,0:T(8,128)S(1)}, f32[512,128]{1,0:T(8,128)S(1)}, f32[512,128]{1,0:T(8,128)S(1)}, f32[256,128]{1,0:T(8,128)S(1)}) custom-call(f32[512,128]{1,0:T(8,128)S(1)} %bitcast.5, f32[512,128]{1,0:T(8,128)S(1)} %collective-permute-done.recv, f32[512,128]{1,0:T(8,128)S(1)} %get-tuple-element.20.swept, ...), custom_call_target="tpu_custom_call" | custom-call | tf_op jit(solution)/shard_map/pallas_call | solution.py:69
  3.1 2.9 %collective-permute-start.1 = (f32[168,128]{1,0:T(8,128)S(1)}, f32[168,128]{1,0:T(8,128)S(1)}, u32[]{:S(2)}, u32[]{:S(2)}) collective-permute-start(f32[168,128]{1,0:T(8,128)S(1)} %get-tuple-element.23.mine), channel_id=1, source_target_pairs={{0,1},{1,0},{2,3},{3,2},{4,5},{5,4},{6,7},{7,6},{8,9},{9,8},{10,11... | collective-permute-start | bytes 258056 | tf_op jit(solution)/shard_map/ppermute | solution.py:451
  6.0 2.9 %collective-permute-done.1.other = f32[168,128]{1,0:T(8,128)S(1)} collective-permute-done((f32[168,128]{1,0:T(8,128)S(1)}, f32[168,128]{1,0:T(8,128)S(1)}, u32[]{:S(2)}, u32[]{:S(2)}) %collective-permute-start.1) | collective-permute-done | bytes 86048 | tf_op jit(solution)/shard_map/ppermute | solution.py:451
  8.9 0.1 shard_map.68
  9.0 1.8 %collective-permute-start.2 = (f32[168,128]{1,0:T(8,128)S(1)}, f32[168,128]{1,0:T(8,128)S(1)}, u32[]{:S(2)}, u32[]{:S(2)}) collective-permute-start(f32[168,128]{1,0:T(8,128)S(1)} %get-tuple-element.24.mine), channel_id=1, source_target_pairs={{0,2},{1,3},{2,0},{3,1},{4,6},{5,7},{6,4},{7,5},{8,10},{9,11},{10,... | collective-permute-start | bytes 258056 | tf_op jit(solution)/shard_map/ppermute | solution.py:451
  10.8 2.7 %collective-permute-done.2.other = f32[168,128]{1,0:T(8,128)S(1)} collective-permute-done((f32[168,128]{1,0:T(8,128)S(1)}, f32[168,128]{1,0:T(8,128)S(1)}, u32[]{:S(2)}, u32[]{:S(2)}) %collective-permute-start.2) | collective-permute-done | bytes 86048 | tf_op jit(solution)/shard_map/ppermute | solution.py:451
  13.5 0.1 shard_map.69
  13.6 1.9 %collective-permute-start.3 = (f32[168,128]{1,0:T(8,128)S(1)}, f32[168,128]{1,0:T(8,128)S(1)}, u32[]{:S(2)}, u32[]{:S(2)}) collective-permute-start(f32[168,128]{1,0:T(8,128)S(1)} %get-tuple-element.25.mine), channel_id=1, source_target_pairs={{0,4},{1,5},{2,6},{3,7},{4,0},{5,1},{6,2},{7,3},{8,12},{9,13},{10,... | collective-permute-start | bytes 258056 | tf_op jit(solution)/shard_map/ppermute | solution.py:451
  15.5 2.7 %collective-permute-done.3.other = f32[168,128]{1,0:T(8,128)S(1)} collective-permute-done((f32[168,128]{1,0:T(8,128)S(1)}, f32[168,128]{1,0:T(8,128)S(1)}, u32[]{:S(2)}, u32[]{:S(2)}) %collective-permute-start.3) | collective-permute-done | bytes 86048 | tf_op jit(solution)/shard_map/ppermute | solution.py:451
  18.1 0.1 shard_map.70
  18.2 0.5 %shard_map.72 = (f32[512,128]{1,0:T(8,128)S(1)}, f32[512,128]{1,0:T(8,128)S(1)}) custom-call(f32[168,128]{1,0:T(8,128)S(1)} %get-tuple-element.27.refs_0_, f32[168,128]{1,0:T(8,128)S(1)} %get-tuple-element.28.refs_1_, f32[168,128]{1,0:T(8,128)S(1)} %get-tuple-element.29.refs_2_, f32[512,128]{1,0:T(8,128)S(1)} %get-tuple-element.30.refs_3_, ...), custom_call_target="tpu_custom_call" | custom-call | tf_op jit(solution)/shard_map/pallas_call | solution.py:69
  18.8 0.1 collective-permute-start.6
  18.8 2.9 %collective-permute-start.4 = (f32[72,128]{1,0:T(8,128)S(1)}, f32[72,128]{1,0:T(8,128)S(1)}, u32[]{:S(2)}, u32[]{:S(2)}) collective-permute-start(f32[72,128]{1,0:T(8,128)S(1)} %get-tuple-element.26.mine), channel_id=1, source_target_pairs={{0,24},{1,25},{2,26},{3,27},{4,28},{5,29},{6,30},{7,31},{8,16},{9,... | collective-permute-start | bytes 110600 | tf_op jit(solution)/shard_map/ppermute | solution.py:461
  21.8 1.7 %collective-permute-done.4.other = f32[72,128]{1,0:T(8,128)S(1)} collective-permute-done((f32[72,128]{1,0:T(8,128)S(1)}, f32[72,128]{1,0:T(8,128)S(1)}, u32[]{:S(2)}, u32[]{:S(2)}) %collective-permute-start.4) | collective-permute-done | bytes 36896 | tf_op jit(solution)/shard_map/ppermute | solution.py:461
  23.5 0.3 %collective-permute-start.5 = (f32[48,128]{1,0:T(8,128)S(1)}, f32[48,128]{1,0:T(8,128)S(1)}, u32[]{:S(2)}, u32[]{:S(2)}) collective-permute-start(f32[48,128]{1,0:T(8,128)S(1)} %shard_map.71.entry), channel_id=1, source_target_pairs={{0,16},{16,0},{1,17},{17,1},{2,18},{18,2},{3,19},{19,3},{4,20},{20... | collective-permute-start | bytes 73736 | tf_op jit(solution)/shard_map/ppermute | solution.py:472
  23.7 0.1 shard_map.74
  23.8 0.7 %shard_map.75.before = f32[1,16,8,2,256]{4,3,2,1,0:T(2,128)} custom-call(f32[16,8,2,128]{3,2,1,0:T(2,128)S(1)} %bitcast.7), custom_call_target="tpu_custom_call" | custom-call | tf_op jit(solution)/shard_map/pallas_call | solution.py:69
  24.5 0.2 collective-permute-done.5.entry
  24.7 0.0 collective-permute-done.6.own
  24.7 0.1 shard_map.73
  24.8 0.7 %shard_map.76 = f32[1,16,8,2,256]{4,3,2,1,0:T(2,128)} custom-call(f32[16,8,2,128]{3,2,1,0:T(2,128)S(1)} %bitcast.6, f32[1,16,8,2,256]{4,3,2,1,0:T(2,128)} %shard_map.75.before), custom_call_target="tpu_custom_call", output_to_operand_aliasing={{}: (1, {})} | custom-call | tf_op jit(solution)/shard_map/pallas_call | solution.py:69
  (1 shorter events, 0.0 us)
Async XLA Ops:
  1.0 1.7 %collective-permute-start = (f32[512,128]{1,0:T(8,128)S(1)}, f32[512,128]{1,0:T(8,128)S(1)}, u32[]{:S(2)}, u32[]{:S(2)}) collective-permute-start(f32[512,128]{1,0:T(8,128)S(1)} %bitcast.8), channel_id=1, source_target_pairs={{0,16},{16,0},{1,17},{17,1},{2,18},{18,2},{3,19},{19,3},{4,20},{20... | collective-permute-start | bytes 786440 | tf_op jit(solution)/shard_map/ppermute | solution.py:436
  3.1 5.8 %collective-permute-start.1 = (f32[168,128]{1,0:T(8,128)S(1)}, f32[168,128]{1,0:T(8,128)S(1)}, u32[]{:S(2)}, u32[]{:S(2)}) collective-permute-start(f32[168,128]{1,0:T(8,128)S(1)} %get-tuple-element.23.mine), channel_id=1, source_target_pairs={{0,1},{1,0},{2,3},{3,2},{4,5},{5,4},{6,7},{7,6},{8,9},{9,8},{10,11... | collective-permute-start | bytes 258056 | tf_op jit(solution)/shard_map/ppermute | solution.py:451
  9.0 4.6 %collective-permute-start.2 = (f32[168,128]{1,0:T(8,128)S(1)}, f32[168,128]{1,0:T(8,128)S(1)}, u32[]{:S(2)}, u32[]{:S(2)}) collective-permute-start(f32[168,128]{1,0:T(8,128)S(1)} %get-tuple-element.24.mine), channel_id=1, source_target_pairs={{0,2},{1,3},{2,0},{3,1},{4,6},{5,7},{6,4},{7,5},{8,10},{9,11},{10,... | collective-permute-start | bytes 258056 | tf_op jit(solution)/shard_map/ppermute | solution.py:451
  13.6 4.6 %collective-permute-start.3 = (f32[168,128]{1,0:T(8,128)S(1)}, f32[168,128]{1,0:T(8,128)S(1)}, u32[]{:S(2)}, u32[]{:S(2)}) collective-permute-start(f32[168,128]{1,0:T(8,128)S(1)} %get-tuple-element.25.mine), channel_id=1, source_target_pairs={{0,4},{1,5},{2,6},{3,7},{4,0},{5,1},{6,2},{7,3},{8,12},{9,13},{10,... | collective-permute-start | bytes 258056 | tf_op jit(solution)/shard_map/ppermute | solution.py:451
  18.8 6.0 %collective-permute-start.6 = (f32[512,128]{1,0:T(8,128)S(1)}, f32[512,128]{1,0:T(8,128)S(1)}, u32[]{:S(2)}, u32[]{:S(2)}) collective-permute-start(f32[512,128]{1,0:T(8,128)S(1)} %get-tuple-element.33), channel_id=1, source_target_pairs={{0,16},{16,0},{1,17},{17,1},{2,18},{18,2},{3,19},{19,3},{4,20},{20... | collective-permute-start | bytes 786440 | tf_op jit(solution)/shard_map/ppermute | solution.py:465
  18.8 4.6 %collective-permute-start.4 = (f32[72,128]{1,0:T(8,128)S(1)}, f32[72,128]{1,0:T(8,128)S(1)}, u32[]{:S(2)}, u32[]{:S(2)}) collective-permute-start(f32[72,128]{1,0:T(8,128)S(1)} %get-tuple-element.26.mine), channel_id=1, source_target_pairs={{0,24},{1,25},{2,26},{3,27},{4,28},{5,29},{6,30},{7,31},{8,16},{9,... | collective-permute-start | bytes 110600 | tf_op jit(solution)/shard_map/ppermute | solution.py:461
  23.5 1.3 %collective-permute-start.5 = (f32[48,128]{1,0:T(8,128)S(1)}, f32[48,128]{1,0:T(8,128)S(1)}, u32[]{:S(2)}, u32[]{:S(2)}) collective-permute-start(f32[48,128]{1,0:T(8,128)S(1)} %shard_map.71.entry), channel_id=1, source_target_pairs={{0,16},{16,0},{1,17},{17,1},{2,18},{18,2},{3,19},{19,3},{4,20},{20... | collective-permute-start | bytes 73736 | tf_op jit(solution)/shard_map/ppermute | solution.py:472

commit v7 on v6

--- a/solution.py
+++ b/solution.py
@@ -111,7 +111,7 @@
 
 
 def add(x, y):
-    return [[p + q for p, q in zip(s, t)] for s, t in zip(x, y)]
+    return [[p + q for p, q in zip(s, t)] + t[len(s) :] for s, t in zip(x, y)]
 
 
 FORWARD, BACKWARD, ACROSS = range(3)
@@ -140,8 +140,7 @@
 def scaled(vectors, data, line):
     start = line * (2 * vectors + 16)
     source = [[data[pl.ds(start + a, vectors, stride=2), :]] for a in (0, 1)]
-    got = combine(data, lambda a, b: start + 2 * vectors + 2 * a + b, source)
-    return [[s[0], jnp.zeros((8, 128), jnp.float32)] for s in got]
+    return combine(data, lambda a, b: start + 2 * vectors + 2 * a + b, source)
 
 
 def unit(chain):
@@ -154,12 +153,14 @@
 def sweep_plane(lines, maps, chain, source, leaving):
     state, states = unit(chain), []
     for line in range(lines):
-        state = add(source(line), mapped(lines, maps, FORWARD, line, state))
+        first = line == 0 and chain >= UNITS
+        state = source(line) if first else add(source(line), mapped(lines, maps, FORWARD, line, state))
         states.append(state)
     leaving[chain] = state
     state, result = unit(chain + 1), [None] * lines
     for line in reversed(range(lines)):
-        state = add(states[line], mapped(lines, maps, BACKWARD, line, state))
+        first = line == lines - 1 and chain + 1 >= UNITS
+        state = states[line] if first else add(states[line], mapped(lines, maps, BACKWARD, line, state))
         result[line] = state
     leaving[chain + 1] = state
     return result
@@ -243,11 +244,17 @@
     return first
 
 
-def merge_kernel(bit, last, mine, other, edge, mids, lower, upper, *pair):
+def merge_kernel(bit, last, mine, other, edge, mids, *pair):
     is_low = jnp.bitwise_and(lax.axis_index("gy"), bit) == 0
-    x, y = mine[...], other[...]
-    lower[...] = jnp.where(is_low, x, y)
-    upper[...] = jnp.where(is_low, y, x)
+    for low_side in (True, False):
+
+        @pl.when(is_low if low_side else ~is_low)
+        def _():
+            lower, upper = (mine, other) if low_side else (other, mine)
+            merge_records(bit, last, lower, upper, edge, mids, *pair)
+
+
+def merge_records(bit, last, lower, upper, edge, mids, *pair):
     row = lax.broadcasted_iota(jnp.int32, (8, 128), 0)
     up = jnp.bitwise_and(row, 2) == 0
 
@@ -454,7 +461,7 @@
             functools.partial(merge_kernel, 1 << level, last),
             [(LAST_ROWS if last else ROWS, half), (ROWS, half)],
             (edge, got),
-            [pltpu.VMEM((ROWS, half), jnp.float32)] * 2 + [pltpu.VMEM((LAST_UNITS, half), jnp.float32)] * (2 * last),
+            [pltpu.VMEM((LAST_UNITS, half), jnp.float32)] * (2 * last),
         )
         mids.append(mid)
     across = [(core * count + j, (1 - core) * count + (j ^ (count // 2))) for core in (0, 1) for j in range(count)]

time: 25.6 us -> 25.5 us (level)
  no operation moved by 1% of the time
where the time goes in v7:
time: 25.5 us; the launch traced here: 25.4 us
  starting transfers between devices  10.5 us (41%)
  waiting for transfers between devices  10.2 us (40%)
  Pallas kernels  4.7 us (18%)
    ppermute x3, waiting for transfers between devices, per_device(): got = lax.ppermute(edge, 'gy', [(j, j ^ 1 << level) for j in range(count)])  8.27 us
    ppermute x3, starting transfers between devices, per_device(): got = lax.ppermute(edge, 'gy', [(j, j ^ 1 << level) for j in range(count)])  6.62 us
    pallas_call x13, Pallas kernels, call(): pl.pallas_call(kernel, out_shape=[jax.ShapeDtypeStruct(s, jnp.float32) fo...  4.7 us
    ppermute x1, starting transfers between devices, per_device(): got = lax.ppermute(edge, ('gx', 'gy'), across)  2.94 us
    ppermute x1, waiting for transfers between devices, per_device(): got = lax.ppermute(edge, ('gx', 'gy'), across)  1.65 us
    ppermute x1, starting transfers between devices, per_device(): recv = lax.ppermute(pack(True), 'gx', swap)  0.56 us
  transfers between devices with their start and end apart: 7, of which 5 were waited for; matrix products, arithmetic and copies ran while one was open for 0% of the time, Pallas kernels for 8%

profile of v7, /device:TPU:0, one launch (start us, length us, event | category | flops | bytes accessed | tf_op | source)
XLA Modules:
  0.0 25.4 jit_solution(17587804644835212556)
XLA Ops:
  0.0 1.0 %shard_map.65 = f32[16,16,2,128]{3,2,1,0:T(2,128)S(1)} custom-call(f32[1,16,8,2,256]{4,3,2,1,0:T(2,128)} %krylov.3, f32[1,16,2,2,256]{4,3,2,1,0:T(2,128)} %inverse.3, f32[1,16,2,2,256]{4,3,2,1,0:T(2,128)} %back.3, f32[1,16,2,2,256]{4,3,2,1,0:T(2,128)} %front.3, f32[1,16,2,2,256]{4,3,2,1,0:T(2,128)} %left.3, f32[1,16,2,2,256]{4,3,2,1,0:T(2,128)} %right.3), custom_call_target="tpu_custom_call" | custom-call | tf_op jit(solution)/shard_map/pallas_call | solution.py:69
  1.0 0.6 %collective-permute-start = (f32[512,128]{1,0:T(8,128)S(1)}, f32[512,128]{1,0:T(8,128)S(1)}, u32[]{:S(2)}, u32[]{:S(2)}) collective-permute-start(f32[512,128]{1,0:T(8,128)S(1)} %bitcast.8), channel_id=1, source_target_pairs={{0,16},{16,0},{1,17},{17,1},{2,18},{18,2},{3,19},{19,3},{4,20},{20... | collective-permute-start | bytes 786440 | tf_op jit(solution)/shard_map/ppermute | solution.py:443
  1.5 1.0 %shard_map.64 = f32[16,16,2,128]{3,2,1,0:T(2,128)S(1)} custom-call(f32[1,16,8,2,256]{4,3,2,1,0:T(2,128)} %krylov.3, f32[1,16,2,2,256]{4,3,2,1,0:T(2,128)} %inverse.3, f32[1,16,2,2,256]{4,3,2,1,0:T(2,128)} %back.3, f32[1,16,2,2,256]{4,3,2,1,0:T(2,128)} %front.3, f32[1,16,2,2,256]{4,3,2,1,0:T(2,128)} %left.3, f32[1,16,2,2,256]{4,3,2,1,0:T(2,128)} %right.3), custom_call_target="tpu_custom_call" | custom-call | tf_op jit(solution)/shard_map/pallas_call | solution.py:69
  2.5 0.2 shard_map.66
  2.7 0.0 collective-permute-done.recv
  2.7 0.4 %shard_map.67 = (f32[168,128]{1,0:T(8,128)S(1)}, f32[512,128]{1,0:T(8,128)S(1)}, f32[512,128]{1,0:T(8,128)S(1)}, f32[256,128]{1,0:T(8,128)S(1)}) custom-call(f32[512,128]{1,0:T(8,128)S(1)} %bitcast.5, f32[512,128]{1,0:T(8,128)S(1)} %collective-permute-done.recv, f32[512,128]{1,0:T(8,128)S(1)} %get-tuple-element.20.swept, ...), custom_call_target="tpu_custom_call" | custom-call | tf_op jit(solution)/shard_map/pallas_call | solution.py:69
  3.1 2.9 %collective-permute-start.1 = (f32[168,128]{1,0:T(8,128)S(1)}, f32[168,128]{1,0:T(8,128)S(1)}, u32[]{:S(2)}, u32[]{:S(2)}) collective-permute-start(f32[168,128]{1,0:T(8,128)S(1)} %get-tuple-element.23.mine), channel_id=1, source_target_pairs={{0,1},{1,0},{2,3},{3,2},{4,5},{5,4},{6,7},{7,6},{8,9},{9,8},{10,11... | collective-permute-start | bytes 258056 | tf_op jit(solution)/shard_map/ppermute | solution.py:458
  6.0 2.9 %collective-permute-done.1.other = f32[168,128]{1,0:T(8,128)S(1)} collective-permute-done((f32[168,128]{1,0:T(8,128)S(1)}, f32[168,128]{1,0:T(8,128)S(1)}, u32[]{:S(2)}, u32[]{:S(2)}) %collective-permute-start.1) | collective-permute-done | bytes 86048 | tf_op jit(solution)/shard_map/ppermute | solution.py:458
  8.9 0.1 shard_map.68
  8.9 1.8 %collective-permute-start.2 = (f32[168,128]{1,0:T(8,128)S(1)}, f32[168,128]{1,0:T(8,128)S(1)}, u32[]{:S(2)}, u32[]{:S(2)}) collective-permute-start(f32[168,128]{1,0:T(8,128)S(1)} %get-tuple-element.24.mine), channel_id=1, source_target_pairs={{0,2},{1,3},{2,0},{3,1},{4,6},{5,7},{6,4},{7,5},{8,10},{9,11},{10,... | collective-permute-start | bytes 258056 | tf_op jit(solution)/shard_map/ppermute | solution.py:458
  10.8 2.7 %collective-permute-done.2.other = f32[168,128]{1,0:T(8,128)S(1)} collective-permute-done((f32[168,128]{1,0:T(8,128)S(1)}, f32[168,128]{1,0:T(8,128)S(1)}, u32[]{:S(2)}, u32[]{:S(2)}) %collective-permute-start.2) | collective-permute-done | bytes 86048 | tf_op jit(solution)/shard_map/ppermute | solution.py:458
  13.5 0.1 shard_map.69
  13.6 1.9 %collective-permute-start.3 = (f32[168,128]{1,0:T(8,128)S(1)}, f32[168,128]{1,0:T(8,128)S(1)}, u32[]{:S(2)}, u32[]{:S(2)}) collective-permute-start(f32[168,128]{1,0:T(8,128)S(1)} %get-tuple-element.25.mine), channel_id=1, source_target_pairs={{0,4},{1,5},{2,6},{3,7},{4,0},{5,1},{6,2},{7,3},{8,12},{9,13},{10,... | collective-permute-start | bytes 258056 | tf_op jit(solution)/shard_map/ppermute | solution.py:458
  15.4 2.7 %collective-permute-done.3.other = f32[168,128]{1,0:T(8,128)S(1)} collective-permute-done((f32[168,128]{1,0:T(8,128)S(1)}, f32[168,128]{1,0:T(8,128)S(1)}, u32[]{:S(2)}, u32[]{:S(2)}) %collective-permute-start.3) | collective-permute-done | bytes 86048 | tf_op jit(solution)/shard_map/ppermute | solution.py:458
  18.1 0.1 shard_map.70
  18.2 0.5 %shard_map.72 = (f32[512,128]{1,0:T(8,128)S(1)}, f32[512,128]{1,0:T(8,128)S(1)}) custom-call(f32[168,128]{1,0:T(8,128)S(1)} %get-tuple-element.27.refs_0_, f32[168,128]{1,0:T(8,128)S(1)} %get-tuple-element.28.refs_1_, f32[168,128]{1,0:T(8,128)S(1)} %get-tuple-element.29.refs_2_, f32[512,128]{1,0:T(8,128)S(1)} %get-tuple-element.30.refs_3_, ...), custom_call_target="tpu_custom_call" | custom-call | tf_op jit(solution)/shard_map/pallas_call | solution.py:69
  18.7 0.1 collective-permute-start.6
  18.8 2.9 %collective-permute-start.4 = (f32[72,128]{1,0:T(8,128)S(1)}, f32[72,128]{1,0:T(8,128)S(1)}, u32[]{:S(2)}, u32[]{:S(2)}) collective-permute-start(f32[72,128]{1,0:T(8,128)S(1)} %get-tuple-element.26.mine), channel_id=1, source_target_pairs={{0,24},{1,25},{2,26},{3,27},{4,28},{5,29},{6,30},{7,31},{8,16},{9,... | collective-permute-start | bytes 110600 | tf_op jit(solution)/shard_map/ppermute | solution.py:468
  21.7 1.7 %collective-permute-done.4.other = f32[72,128]{1,0:T(8,128)S(1)} collective-permute-done((f32[72,128]{1,0:T(8,128)S(1)}, f32[72,128]{1,0:T(8,128)S(1)}, u32[]{:S(2)}, u32[]{:S(2)}) %collective-permute-start.4) | collective-permute-done | bytes 36896 | tf_op jit(solution)/shard_map/ppermute | solution.py:468
  23.4 0.3 %collective-permute-start.5 = (f32[48,128]{1,0:T(8,128)S(1)}, f32[48,128]{1,0:T(8,128)S(1)}, u32[]{:S(2)}, u32[]{:S(2)}) collective-permute-start(f32[48,128]{1,0:T(8,128)S(1)} %shard_map.71.entry), channel_id=1, source_target_pairs={{0,16},{16,0},{1,17},{17,1},{2,18},{18,2},{3,19},{19,3},{4,20},{20... | collective-permute-start | bytes 73736 | tf_op jit(solution)/shard_map/ppermute | solution.py:479
  23.7 0.1 shard_map.74
  23.7 0.7 %shard_map.75.before = f32[1,16,8,2,256]{4,3,2,1,0:T(2,128)} custom-call(f32[16,8,2,128]{3,2,1,0:T(2,128)S(1)} %bitcast.7), custom_call_target="tpu_custom_call" | custom-call | tf_op jit(solution)/shard_map/pallas_call | solution.py:69
  24.4 0.2 collective-permute-done.5.entry
  24.7 0.0 collective-permute-done.6.own
  24.7 0.1 shard_map.73
  24.7 0.7 %shard_map.76 = f32[1,16,8,2,256]{4,3,2,1,0:T(2,128)} custom-call(f32[16,8,2,128]{3,2,1,0:T(2,128)S(1)} %bitcast.6, f32[1,16,8,2,256]{4,3,2,1,0:T(2,128)} %shard_map.75.before), custom_call_target="tpu_custom_call", output_to_operand_aliasing={{}: (1, {})} | custom-call | tf_op jit(solution)/shard_map/pallas_call | solution.py:69
  (1 shorter events, 0.0 us)
Async XLA Ops:
  1.0 1.7 %collective-permute-start = (f32[512,128]{1,0:T(8,128)S(1)}, f32[512,128]{1,0:T(8,128)S(1)}, u32[]{:S(2)}, u32[]{:S(2)}) collective-permute-start(f32[512,128]{1,0:T(8,128)S(1)} %bitcast.8), channel_id=1, source_target_pairs={{0,16},{16,0},{1,17},{17,1},{2,18},{18,2},{3,19},{19,3},{4,20},{20... | collective-permute-start | bytes 786440 | tf_op jit(solution)/shard_map/ppermute | solution.py:443
  3.1 5.8 %collective-permute-start.1 = (f32[168,128]{1,0:T(8,128)S(1)}, f32[168,128]{1,0:T(8,128)S(1)}, u32[]{:S(2)}, u32[]{:S(2)}) collective-permute-start(f32[168,128]{1,0:T(8,128)S(1)} %get-tuple-element.23.mine), channel_id=1, source_target_pairs={{0,1},{1,0},{2,3},{3,2},{4,5},{5,4},{6,7},{7,6},{8,9},{9,8},{10,11... | collective-permute-start | bytes 258056 | tf_op jit(solution)/shard_map/ppermute | solution.py:458
  8.9 4.6 %collective-permute-start.2 = (f32[168,128]{1,0:T(8,128)S(1)}, f32[168,128]{1,0:T(8,128)S(1)}, u32[]{:S(2)}, u32[]{:S(2)}) collective-permute-start(f32[168,128]{1,0:T(8,128)S(1)} %get-tuple-element.24.mine), channel_id=1, source_target_pairs={{0,2},{1,3},{2,0},{3,1},{4,6},{5,7},{6,4},{7,5},{8,10},{9,11},{10,... | collective-permute-start | bytes 258056 | tf_op jit(solution)/shard_map/ppermute | solution.py:458
  13.6 4.6 %collective-permute-start.3 = (f32[168,128]{1,0:T(8,128)S(1)}, f32[168,128]{1,0:T(8,128)S(1)}, u32[]{:S(2)}, u32[]{:S(2)}) collective-permute-start(f32[168,128]{1,0:T(8,128)S(1)} %get-tuple-element.25.mine), channel_id=1, source_target_pairs={{0,4},{1,5},{2,6},{3,7},{4,0},{5,1},{6,2},{7,3},{8,12},{9,13},{10,... | collective-permute-start | bytes 258056 | tf_op jit(solution)/shard_map/ppermute | solution.py:458
  18.7 6.0 %collective-permute-start.6 = (f32[512,128]{1,0:T(8,128)S(1)}, f32[512,128]{1,0:T(8,128)S(1)}, u32[]{:S(2)}, u32[]{:S(2)}) collective-permute-start(f32[512,128]{1,0:T(8,128)S(1)} %get-tuple-element.33), channel_id=1, source_target_pairs={{0,16},{16,0},{1,17},{17,1},{2,18},{18,2},{3,19},{19,3},{4,20},{20... | collective-permute-start | bytes 786440 | tf_op jit(solution)/shard_map/ppermute | solution.py:472
  18.8 4.6 %collective-permute-start.4 = (f32[72,128]{1,0:T(8,128)S(1)}, f32[72,128]{1,0:T(8,128)S(1)}, u32[]{:S(2)}, u32[]{:S(2)}) collective-permute-start(f32[72,128]{1,0:T(8,128)S(1)} %get-tuple-element.26.mine), channel_id=1, source_target_pairs={{0,24},{1,25},{2,26},{3,27},{4,28},{5,29},{6,30},{7,31},{8,16},{9,... | collective-permute-start | bytes 110600 | tf_op jit(solution)/shard_map/ppermute | solution.py:468
  23.4 1.3 %collective-permute-start.5 = (f32[48,128]{1,0:T(8,128)S(1)}, f32[48,128]{1,0:T(8,128)S(1)}, u32[]{:S(2)}, u32[]{:S(2)}) collective-permute-start(f32[48,128]{1,0:T(8,128)S(1)} %shard_map.71.entry), channel_id=1, source_target_pairs={{0,16},{16,0},{1,17},{17,1},{2,18},{18,2},{3,19},{19,3},{4,20},{20... | collective-permute-start | bytes 73736 | tf_op jit(solution)/shard_map/ppermute | solution.py:479

commit v8 on v7

--- a/solution.py
+++ b/solution.py
@@ -184,7 +184,7 @@
                     swept[state_rows(line, a, part), :] = result[line][a][part]
 
 
-def local_kernel(lines, vectors, keep, recv, swept, early, own_maps, edge, first, second, low, other_maps):
+def local_kernel(lines, vectors, keep, recv, swept, early, own_maps, edge, fixed_low, second, low, other_maps):
     make_maps(lines, vectors, recv, other_maps)
     for own in (0, 1):
 
@@ -215,12 +215,12 @@
             )
             keep_record(edge, leaving)
             for line in range(lines):
-                total = add(swept_low[line], fixed[line])
                 for a in (0, 1):
-                    low[pl.ds((2 * line + a) * 8, 8), :] = swept_low[line][a][1]
                     for part in (0, 1):
-                        first[state_rows(line, a, part), :] = total[a][part]
+                        fixed_low[state_rows(line, a, part), :] = fixed[line][a][part]
                         second[state_rows(line, a, part), :] = swept_high[line][a][part]
+                        if own:
+                            low[state_rows(line, a, part), :] = swept_low[line][a][part]
 
 
 def times(ref, row, step, state):
@@ -299,8 +299,10 @@
 
 
 def compose_kernel(lines, levels, *refs):
-    mids, (first, second, low, own, away) = refs[: levels - 1], refs[levels - 1 :]
+    mids, (fixed, second, early, late, own, away, first, low) = refs[: levels - 1], refs[levels - 1 :]
     place, core = lax.axis_index("gy"), lax.axis_index("gx")
+    low[...] = jnp.where(core == 0, early[...], late[...])
+    first[...] = low[...] + fixed[...]
     row = lax.broadcasted_iota(jnp.int32, (8, 128), 0)
     none = jnp.zeros((8, 128), jnp.float32)
     in_low = jnp.bitwise_and(place, 1 << (levels - 1)) == 0
@@ -337,7 +339,7 @@
             for source, extra in ((first, [(T1, T3), (U1, U3)]), (second, [])):
                 value = [source[pl.ds(start, 8), :], none]
                 pairs = [(source, start + 8, pair) for pair in units]
-                pairs += [(low, (2 * line + a) * 8, pair) for pair in extra]
+                pairs += [(low, start + 8, pair) for pair in extra]
                 for ref, begin, (column, chain) in pairs:
                     for b in (0, 1):
                         factor = spread(ref, begin + 2 * column + b, 8)
@@ -447,9 +449,9 @@
         [(2 * lines * width, half), (ROWS, half), (12 * lines, half)],
         (keep,),
     )
-    edge, first, second, low = call(
+    edge, fixed, second, late = call(
         functools.partial(local_kernel, lines, vectors),
-        [(ROWS, half), (2 * lines * width, half), (2 * lines * width, half), (2 * lines * 8, half)],
+        [(ROWS, half), (2 * lines * width, half), (2 * lines * width, half), (2 * lines * width, half)],
         (keep, recv, swept, early, own_maps),
         [pltpu.VMEM((12 * lines, half), jnp.float32)],
     )
@@ -467,7 +469,10 @@
     across = [(core * count + j, (1 - core) * count + (j ^ (count // 2))) for core in (0, 1) for j in range(count)]
     got = lax.ppermute(edge, ("gx", "gy"), across)
     own, away = call(
-        functools.partial(compose_kernel, lines, levels), [(2 * lines * width, half)] * 2, (*mids, first, second, low)
+        functools.partial(compose_kernel, lines, levels),
+        [(2 * lines * width, half)] * 2,
+        (*mids, fixed, second, swept, late),
+        [pltpu.VMEM((2 * lines * width, half), jnp.float32)] * 2,
     )
     away = lax.ppermute(away, "gx", swap)
     (entry,) = call(

time: 25.5 us -> 25.6 us (level)
  no operation moved by 1% of the time
where the time goes in v8:
time: 25.6 us; the launch traced here: 25.4 us
  starting transfers between devices  10.5 us (41%)
  waiting for transfers between devices  10.2 us (40%)
  Pallas kernels  4.73 us (18%)
    ppermute x3, waiting for transfers between devices, per_device(): got = lax.ppermute(edge, 'gy', [(j, j ^ 1 << level) for j in range(count)])  8.27 us
    ppermute x3, starting transfers between devices, per_device(): got = lax.ppermute(edge, 'gy', [(j, j ^ 1 << level) for j in range(count)])  6.62 us
    pallas_call x13, Pallas kernels, call(): pl.pallas_call(kernel, out_shape=[jax.ShapeDtypeStruct(s, jnp.float32) fo...  4.73 us
    ppermute x1, starting transfers between devices, per_device(): got = lax.ppermute(edge, ('gx', 'gy'), across)  2.94 us
    ppermute x1, waiting for transfers between devices, per_device(): got = lax.ppermute(edge, ('gx', 'gy'), across)  1.65 us
    ppermute x1, starting transfers between devices, per_device(): recv = lax.ppermute(pack(True), 'gx', swap)  0.56 us
  transfers between devices with their start and end apart: 7, of which 5 were waited for; matrix products, arithmetic and copies ran while one was open for 0% of the time, Pallas kernels for 8%

profile of v8, /device:TPU:0, one launch (start us, length us, event | category | flops | bytes accessed | tf_op | source)
XLA Modules:
  0.0 25.4 jit_solution(9125151677020408437)
XLA Ops:
  0.0 1.0 %shard_map.65 = f32[16,16,2,128]{3,2,1,0:T(2,128)S(1)} custom-call(f32[1,16,8,2,256]{4,3,2,1,0:T(2,128)} %krylov.3, f32[1,16,2,2,256]{4,3,2,1,0:T(2,128)} %inverse.3, f32[1,16,2,2,256]{4,3,2,1,0:T(2,128)} %back.3, f32[1,16,2,2,256]{4,3,2,1,0:T(2,128)} %front.3, f32[1,16,2,2,256]{4,3,2,1,0:T(2,128)} %left.3, f32[1,16,2,2,256]{4,3,2,1,0:T(2,128)} %right.3), custom_call_target="tpu_custom_call" | custom-call | tf_op jit(solution)/shard_map/pallas_call | solution.py:69
  1.0 0.6 %collective-permute-start = (f32[512,128]{1,0:T(8,128)S(1)}, f32[512,128]{1,0:T(8,128)S(1)}, u32[]{:S(2)}, u32[]{:S(2)}) collective-permute-start(f32[512,128]{1,0:T(8,128)S(1)} %bitcast.8), channel_id=1, source_target_pairs={{0,16},{16,0},{1,17},{17,1},{2,18},{18,2},{3,19},{19,3},{4,20},{20... | collective-permute-start | bytes 786440 | tf_op jit(solution)/shard_map/ppermute | solution.py:445
  1.5 1.0 %shard_map.64 = f32[16,16,2,128]{3,2,1,0:T(2,128)S(1)} custom-call(f32[1,16,8,2,256]{4,3,2,1,0:T(2,128)} %krylov.3, f32[1,16,2,2,256]{4,3,2,1,0:T(2,128)} %inverse.3, f32[1,16,2,2,256]{4,3,2,1,0:T(2,128)} %back.3, f32[1,16,2,2,256]{4,3,2,1,0:T(2,128)} %front.3, f32[1,16,2,2,256]{4,3,2,1,0:T(2,128)} %left.3, f32[1,16,2,2,256]{4,3,2,1,0:T(2,128)} %right.3), custom_call_target="tpu_custom_call" | custom-call | tf_op jit(solution)/shard_map/pallas_call | solution.py:69
  2.5 0.2 shard_map.66
  2.7 0.0 collective-permute-done.recv
  2.7 0.4 %shard_map.67 = (f32[168,128]{1,0:T(8,128)S(1)}, f32[512,128]{1,0:T(8,128)S(1)}, f32[512,128]{1,0:T(8,128)S(1)}, f32[512,128]{1,0:T(8,128)S(1)}) custom-call(f32[512,128]{1,0:T(8,128)S(1)} %bitcast.5, f32[512,128]{1,0:T(8,128)S(1)} %collective-permute-done.recv, f32[512,128]{1,0:T(8,128)S(1)} %get-tuple-element.20.swept.refs_5_, ...), custom_call_target="tpu_custom_call" | custom-call | tf_op jit(solution)/shard_map/pallas_call | solution.py:69
  3.1 2.9 %collective-permute-start.1 = (f32[168,128]{1,0:T(8,128)S(1)}, f32[168,128]{1,0:T(8,128)S(1)}, u32[]{:S(2)}, u32[]{:S(2)}) collective-permute-start(f32[168,128]{1,0:T(8,128)S(1)} %get-tuple-element.23.mine), channel_id=1, source_target_pairs={{0,1},{1,0},{2,3},{3,2},{4,5},{5,4},{6,7},{7,6},{8,9},{9,8},{10,11... | collective-permute-start | bytes 258056 | tf_op jit(solution)/shard_map/ppermute | solution.py:460
  6.0 2.9 %collective-permute-done.1.other = f32[168,128]{1,0:T(8,128)S(1)} collective-permute-done((f32[168,128]{1,0:T(8,128)S(1)}, f32[168,128]{1,0:T(8,128)S(1)}, u32[]{:S(2)}, u32[]{:S(2)}) %collective-permute-start.1) | collective-permute-done | bytes 86048 | tf_op jit(solution)/shard_map/ppermute | solution.py:460
  8.9 0.1 shard_map.68
  8.9 1.8 %collective-permute-start.2 = (f32[168,128]{1,0:T(8,128)S(1)}, f32[168,128]{1,0:T(8,128)S(1)}, u32[]{:S(2)}, u32[]{:S(2)}) collective-permute-start(f32[168,128]{1,0:T(8,128)S(1)} %get-tuple-element.24.mine), channel_id=1, source_target_pairs={{0,2},{1,3},{2,0},{3,1},{4,6},{5,7},{6,4},{7,5},{8,10},{9,11},{10,... | collective-permute-start | bytes 258056 | tf_op jit(solution)/shard_map/ppermute | solution.py:460
  10.8 2.7 %collective-permute-done.2.other = f32[168,128]{1,0:T(8,128)S(1)} collective-permute-done((f32[168,128]{1,0:T(8,128)S(1)}, f32[168,128]{1,0:T(8,128)S(1)}, u32[]{:S(2)}, u32[]{:S(2)}) %collective-permute-start.2) | collective-permute-done | bytes 86048 | tf_op jit(solution)/shard_map/ppermute | solution.py:460
  13.5 0.1 shard_map.69
  13.6 1.9 %collective-permute-start.3 = (f32[168,128]{1,0:T(8,128)S(1)}, f32[168,128]{1,0:T(8,128)S(1)}, u32[]{:S(2)}, u32[]{:S(2)}) collective-permute-start(f32[168,128]{1,0:T(8,128)S(1)} %get-tuple-element.25.mine), channel_id=1, source_target_pairs={{0,4},{1,5},{2,6},{3,7},{4,0},{5,1},{6,2},{7,3},{8,12},{9,13},{10,... | collective-permute-start | bytes 258056 | tf_op jit(solution)/shard_map/ppermute | solution.py:460
  15.4 2.7 %collective-permute-done.3.other = f32[168,128]{1,0:T(8,128)S(1)} collective-permute-done((f32[168,128]{1,0:T(8,128)S(1)}, f32[168,128]{1,0:T(8,128)S(1)}, u32[]{:S(2)}, u32[]{:S(2)}) %collective-permute-start.3) | collective-permute-done | bytes 86048 | tf_op jit(solution)/shard_map/ppermute | solution.py:460
  18.1 0.1 shard_map.70
  18.2 0.6 %shard_map.72 = (f32[512,128]{1,0:T(8,128)S(1)}, f32[512,128]{1,0:T(8,128)S(1)}) custom-call(f32[168,128]{1,0:T(8,128)S(1)} %get-tuple-element.27.refs_0_, f32[168,128]{1,0:T(8,128)S(1)} %get-tuple-element.28.refs_1_, f32[168,128]{1,0:T(8,128)S(1)} %get-tuple-element.29.refs_2_, f32[512,128]{1,0:T(8,128)S(1)} %get-tuple-element.30.refs_3_, ...), custom_call_target="tpu_custom_call" | custom-call | tf_op jit(solution)/shard_map/pallas_call | solution.py:69
  18.7 0.1 collective-permute-start.6
  18.8 2.9 %collective-permute-start.4 = (f32[72,128]{1,0:T(8,128)S(1)}, f32[72,128]{1,0:T(8,128)S(1)}, u32[]{:S(2)}, u32[]{:S(2)}) collective-permute-start(f32[72,128]{1,0:T(8,128)S(1)} %get-tuple-element.26.mine), channel_id=1, source_target_pairs={{0,24},{1,25},{2,26},{3,27},{4,28},{5,29},{6,30},{7,31},{8,16},{9,... | collective-permute-start | bytes 110600 | tf_op jit(solution)/shard_map/ppermute | solution.py:470
  21.8 1.7 %collective-permute-done.4.other = f32[72,128]{1,0:T(8,128)S(1)} collective-permute-done((f32[72,128]{1,0:T(8,128)S(1)}, f32[72,128]{1,0:T(8,128)S(1)}, u32[]{:S(2)}, u32[]{:S(2)}) %collective-permute-start.4) | collective-permute-done | bytes 36896 | tf_op jit(solution)/shard_map/ppermute | solution.py:470
  23.4 0.3 %collective-permute-start.5 = (f32[48,128]{1,0:T(8,128)S(1)}, f32[48,128]{1,0:T(8,128)S(1)}, u32[]{:S(2)}, u32[]{:S(2)}) collective-permute-start(f32[48,128]{1,0:T(8,128)S(1)} %shard_map.71.entry), channel_id=1, source_target_pairs={{0,16},{16,0},{1,17},{17,1},{2,18},{18,2},{3,19},{19,3},{4,20},{20... | collective-permute-start | bytes 73736 | tf_op jit(solution)/shard_map/ppermute | solution.py:484
  23.7 0.1 shard_map.74
  23.8 0.7 %shard_map.75.before = f32[1,16,8,2,256]{4,3,2,1,0:T(2,128)} custom-call(f32[16,8,2,128]{3,2,1,0:T(2,128)S(1)} %bitcast.7), custom_call_target="tpu_custom_call" | custom-call | tf_op jit(solution)/shard_map/pallas_call | solution.py:69
  24.5 0.2 collective-permute-done.5.entry
  24.7 0.0 collective-permute-done.6.own
  24.7 0.1 shard_map.73
  24.8 0.7 %shard_map.76 = f32[1,16,8,2,256]{4,3,2,1,0:T(2,128)} custom-call(f32[16,8,2,128]{3,2,1,0:T(2,128)S(1)} %bitcast.6, f32[1,16,8,2,256]{4,3,2,1,0:T(2,128)} %shard_map.75.before), custom_call_target="tpu_custom_call", output_to_operand_aliasing={{}: (1, {})} | custom-call | tf_op jit(solution)/shard_map/pallas_call | solution.py:69
  (1 shorter events, 0.0 us)
Async XLA Ops:
  1.0 1.7 %collective-permute-start = (f32[512,128]{1,0:T(8,128)S(1)}, f32[512,128]{1,0:T(8,128)S(1)}, u32[]{:S(2)}, u32[]{:S(2)}) collective-permute-start(f32[512,128]{1,0:T(8,128)S(1)} %bitcast.8), channel_id=1, source_target_pairs={{0,16},{16,0},{1,17},{17,1},{2,18},{18,2},{3,19},{19,3},{4,20},{20... | collective-permute-start | bytes 786440 | tf_op jit(solution)/shard_map/ppermute | solution.py:445
  3.1 5.8 %collective-permute-start.1 = (f32[168,128]{1,0:T(8,128)S(1)}, f32[168,128]{1,0:T(8,128)S(1)}, u32[]{:S(2)}, u32[]{:S(2)}) collective-permute-start(f32[168,128]{1,0:T(8,128)S(1)} %get-tuple-element.23.mine), channel_id=1, source_target_pairs={{0,1},{1,0},{2,3},{3,2},{4,5},{5,4},{6,7},{7,6},{8,9},{9,8},{10,11... | collective-permute-start | bytes 258056 | tf_op jit(solution)/shard_map/ppermute | solution.py:460
  8.9 4.6 %collective-permute-start.2 = (f32[168,128]{1,0:T(8,128)S(1)}, f32[168,128]{1,0:T(8,128)S(1)}, u32[]{:S(2)}, u32[]{:S(2)}) collective-permute-start(f32[168,128]{1,0:T(8,128)S(1)} %get-tuple-element.24.mine), channel_id=1, source_target_pairs={{0,2},{1,3},{2,0},{3,1},{4,6},{5,7},{6,4},{7,5},{8,10},{9,11},{10,... | collective-permute-start | bytes 258056 | tf_op jit(solution)/shard_map/ppermute | solution.py:460
  13.6 4.6 %collective-permute-start.3 = (f32[168,128]{1,0:T(8,128)S(1)}, f32[168,128]{1,0:T(8,128)S(1)}, u32[]{:S(2)}, u32[]{:S(2)}) collective-permute-start(f32[168,128]{1,0:T(8,128)S(1)} %get-tuple-element.25.mine), channel_id=1, source_target_pairs={{0,4},{1,5},{2,6},{3,7},{4,0},{5,1},{6,2},{7,3},{8,12},{9,13},{10,... | collective-permute-start | bytes 258056 | tf_op jit(solution)/shard_map/ppermute | solution.py:460
  18.7 6.0 %collective-permute-start.6 = (f32[512,128]{1,0:T(8,128)S(1)}, f32[512,128]{1,0:T(8,128)S(1)}, u32[]{:S(2)}, u32[]{:S(2)}) collective-permute-start(f32[512,128]{1,0:T(8,128)S(1)} %get-tuple-element.33), channel_id=1, source_target_pairs={{0,16},{16,0},{1,17},{17,1},{2,18},{18,2},{3,19},{19,3},{4,20},{20... | collective-permute-start | bytes 786440 | tf_op jit(solution)/shard_map/ppermute | solution.py:477
  18.8 4.6 %collective-permute-start.4 = (f32[72,128]{1,0:T(8,128)S(1)}, f32[72,128]{1,0:T(8,128)S(1)}, u32[]{:S(2)}, u32[]{:S(2)}) collective-permute-start(f32[72,128]{1,0:T(8,128)S(1)} %get-tuple-element.26.mine), channel_id=1, source_target_pairs={{0,24},{1,25},{2,26},{3,27},{4,28},{5,29},{6,30},{7,31},{8,16},{9,... | collective-permute-start | bytes 110600 | tf_op jit(solution)/shard_map/ppermute | solution.py:470
  23.4 1.3 %collective-permute-start.5 = (f32[48,128]{1,0:T(8,128)S(1)}, f32[48,128]{1,0:T(8,128)S(1)}, u32[]{:S(2)}, u32[]{:S(2)}) collective-permute-start(f32[48,128]{1,0:T(8,128)S(1)} %shard_map.71.entry), channel_id=1, source_target_pairs={{0,16},{16,0},{1,17},{17,1},{2,18},{18,2},{3,19},{19,3},{4,20},{20... | collective-permute-start | bytes 73736 | tf_op jit(solution)/shard_map/ppermute | solution.py:484

commit v9 on v7

--- a/solution.py
+++ b/solution.py
@@ -412,8 +412,9 @@
     one.wait()
 
 
-def last_kernel(half, got, before, out, sem):
-    one = part_copy(half, 1 - half_of(), got, out, sem.at[0])
+def last_kernel(lines, half, entry, away, before, out, value, sem):
+    own_kernel(lines, entry, away, value)
+    one = part_copy(half, 1 - half_of(), value.reshape(lines, value.shape[0] // (2 * lines), 2, half), out, sem.at[0])
     one.start()
     one.wait()
 
@@ -492,13 +493,13 @@
         out_specs=[HBM],
     )
     (out,) = call(
-        functools.partial(last_kernel, half),
+        functools.partial(last_kernel, lines, half),
         [krylov.shape],
-        [plane_half(got_entry, away), out],
-        [pltpu.SemaphoreType.DMA((1,))],
-        specs=[ANY, HBM],
+        [got_entry, away, out],
+        [pltpu.VMEM((lines * 16, half), jnp.float32), pltpu.SemaphoreType.DMA((1,))],
+        specs=[VMEM, VMEM, HBM],
         out_specs=[HBM],
-        aliases={1: 0},
+        aliases={2: 0},
     )
     return out
 

time: 25.5 us -> 25.5 us (level)
    pallas_call x13 -> x12, Pallas kernels: 4.7 us -> 4.68 us  [call(): pl.pallas_call(kernel, out_shape=[jax.ShapeDtypeStruct(s, jnp.float32) fo...]
where the time goes in v9:
time: 25.5 us; the launch traced here: 25.4 us
  starting transfers between devices  10.5 us (41%)
  waiting for transfers between devices  10.2 us (40%)
  Pallas kernels  4.68 us (18%)
    ppermute x3, waiting for transfers between devices, per_device(): got = lax.ppermute(edge, 'gy', [(j, j ^ 1 << level) for j in range(count)])  8.27 us
    ppermute x3, starting transfers between devices, per_device(): got = lax.ppermute(edge, 'gy', [(j, j ^ 1 << level) for j in range(count)])  6.62 us
    pallas_call x12, Pallas kernels, call(): pl.pallas_call(kernel, out_shape=[jax.ShapeDtypeStruct(s, jnp.float32) fo...  4.68 us
    ppermute x1, starting transfers between devices, per_device(): got = lax.ppermute(edge, ('gx', 'gy'), across)  2.94 us
    ppermute x1, waiting for transfers between devices, per_device(): got = lax.ppermute(edge, ('gx', 'gy'), across)  1.65 us
    ppermute x1, starting transfers between devices, per_device(): recv = lax.ppermute(pack(True), 'gx', swap)  0.56 us
  transfers between devices with their start and end apart: 7, of which 5 were waited for; matrix products, arithmetic and copies ran while one was open for 0% of the time, Pallas kernels for 8%

profile of v9, /device:TPU:0, one launch (start us, length us, event | category | flops | bytes accessed | tf_op | source)
XLA Modules:
  0.0 25.4 jit_solution(7974646547872228672)
XLA Ops:
  0.0 1.0 %shard_map.65 = f32[16,16,2,128]{3,2,1,0:T(2,128)S(1)} custom-call(f32[1,16,8,2,256]{4,3,2,1,0:T(2,128)} %krylov.3, f32[1,16,2,2,256]{4,3,2,1,0:T(2,128)} %inverse.3, f32[1,16,2,2,256]{4,3,2,1,0:T(2,128)} %back.3, f32[1,16,2,2,256]{4,3,2,1,0:T(2,128)} %front.3, f32[1,16,2,2,256]{4,3,2,1,0:T(2,128)} %left.3, f32[1,16,2,2,256]{4,3,2,1,0:T(2,128)} %right.3), custom_call_target="tpu_custom_call" | custom-call | tf_op jit(solution)/shard_map/pallas_call | solution.py:69
  1.0 0.6 %collective-permute-start = (f32[512,128]{1,0:T(8,128)S(1)}, f32[512,128]{1,0:T(8,128)S(1)}, u32[]{:S(2)}, u32[]{:S(2)}) collective-permute-start(f32[512,128]{1,0:T(8,128)S(1)} %bitcast.6), channel_id=1, source_target_pairs={{0,16},{16,0},{1,17},{17,1},{2,18},{18,2},{3,19},{19,3},{4,20},{20... | collective-permute-start | bytes 786440 | tf_op jit(solution)/shard_map/ppermute | solution.py:444
  1.5 1.0 %shard_map.64 = f32[16,16,2,128]{3,2,1,0:T(2,128)S(1)} custom-call(f32[1,16,8,2,256]{4,3,2,1,0:T(2,128)} %krylov.3, f32[1,16,2,2,256]{4,3,2,1,0:T(2,128)} %inverse.3, f32[1,16,2,2,256]{4,3,2,1,0:T(2,128)} %back.3, f32[1,16,2,2,256]{4,3,2,1,0:T(2,128)} %front.3, f32[1,16,2,2,256]{4,3,2,1,0:T(2,128)} %left.3, f32[1,16,2,2,256]{4,3,2,1,0:T(2,128)} %right.3), custom_call_target="tpu_custom_call" | custom-call | tf_op jit(solution)/shard_map/pallas_call | solution.py:69
  2.5 0.2 shard_map.66
  2.7 0.0 collective-permute-done.recv
  2.7 0.4 %shard_map.67 = (f32[168,128]{1,0:T(8,128)S(1)}, f32[512,128]{1,0:T(8,128)S(1)}, f32[512,128]{1,0:T(8,128)S(1)}, f32[256,128]{1,0:T(8,128)S(1)}) custom-call(f32[512,128]{1,0:T(8,128)S(1)} %bitcast.4, f32[512,128]{1,0:T(8,128)S(1)} %collective-permute-done.recv, f32[512,128]{1,0:T(8,128)S(1)} %get-tuple-element.20.swept, ...), custom_call_target="tpu_custom_call" | custom-call | tf_op jit(solution)/shard_map/pallas_call | solution.py:69
  3.1 2.9 %collective-permute-start.1 = (f32[168,128]{1,0:T(8,128)S(1)}, f32[168,128]{1,0:T(8,128)S(1)}, u32[]{:S(2)}, u32[]{:S(2)}) collective-permute-start(f32[168,128]{1,0:T(8,128)S(1)} %get-tuple-element.23.mine), channel_id=1, source_target_pairs={{0,1},{1,0},{2,3},{3,2},{4,5},{5,4},{6,7},{7,6},{8,9},{9,8},{10,11... | collective-permute-start | bytes 258056 | tf_op jit(solution)/shard_map/ppermute | solution.py:459
  6.0 2.9 %collective-permute-done.1.other = f32[168,128]{1,0:T(8,128)S(1)} collective-permute-done((f32[168,128]{1,0:T(8,128)S(1)}, f32[168,128]{1,0:T(8,128)S(1)}, u32[]{:S(2)}, u32[]{:S(2)}) %collective-permute-start.1) | collective-permute-done | bytes 86048 | tf_op jit(solution)/shard_map/ppermute | solution.py:459
  8.9 0.1 shard_map.68
  8.9 1.8 %collective-permute-start.2 = (f32[168,128]{1,0:T(8,128)S(1)}, f32[168,128]{1,0:T(8,128)S(1)}, u32[]{:S(2)}, u32[]{:S(2)}) collective-permute-start(f32[168,128]{1,0:T(8,128)S(1)} %get-tuple-element.24.mine), channel_id=1, source_target_pairs={{0,2},{1,3},{2,0},{3,1},{4,6},{5,7},{6,4},{7,5},{8,10},{9,11},{10,... | collective-permute-start | bytes 258056 | tf_op jit(solution)/shard_map/ppermute | solution.py:459
  10.8 2.7 %collective-permute-done.2.other = f32[168,128]{1,0:T(8,128)S(1)} collective-permute-done((f32[168,128]{1,0:T(8,128)S(1)}, f32[168,128]{1,0:T(8,128)S(1)}, u32[]{:S(2)}, u32[]{:S(2)}) %collective-permute-start.2) | collective-permute-done | bytes 86048 | tf_op jit(solution)/shard_map/ppermute | solution.py:459
  13.5 0.1 shard_map.69
  13.6 1.9 %collective-permute-start.3 = (f32[168,128]{1,0:T(8,128)S(1)}, f32[168,128]{1,0:T(8,128)S(1)}, u32[]{:S(2)}, u32[]{:S(2)}) collective-permute-start(f32[168,128]{1,0:T(8,128)S(1)} %get-tuple-element.25.mine), channel_id=1, source_target_pairs={{0,4},{1,5},{2,6},{3,7},{4,0},{5,1},{6,2},{7,3},{8,12},{9,13},{10,... | collective-permute-start | bytes 258056 | tf_op jit(solution)/shard_map/ppermute | solution.py:459
  15.4 2.7 %collective-permute-done.3.other = f32[168,128]{1,0:T(8,128)S(1)} collective-permute-done((f32[168,128]{1,0:T(8,128)S(1)}, f32[168,128]{1,0:T(8,128)S(1)}, u32[]{:S(2)}, u32[]{:S(2)}) %collective-permute-start.3) | collective-permute-done | bytes 86048 | tf_op jit(solution)/shard_map/ppermute | solution.py:459
  18.1 0.1 shard_map.70
  18.2 0.5 %shard_map.72 = (f32[512,128]{1,0:T(8,128)S(1)}, f32[512,128]{1,0:T(8,128)S(1)}) custom-call(f32[168,128]{1,0:T(8,128)S(1)} %get-tuple-element.27.refs_0_, f32[168,128]{1,0:T(8,128)S(1)} %get-tuple-element.28.refs_1_, f32[168,128]{1,0:T(8,128)S(1)} %get-tuple-element.29.refs_2_, f32[512,128]{1,0:T(8,128)S(1)} %get-tuple-element.30.refs_3_, ...), custom_call_target="tpu_custom_call" | custom-call | tf_op jit(solution)/shard_map/pallas_call | solution.py:69
  18.7 0.1 collective-permute-start.6
  18.8 2.9 %collective-permute-start.4 = (f32[72,128]{1,0:T(8,128)S(1)}, f32[72,128]{1,0:T(8,128)S(1)}, u32[]{:S(2)}, u32[]{:S(2)}) collective-permute-start(f32[72,128]{1,0:T(8,128)S(1)} %get-tuple-element.26.mine), channel_id=1, source_target_pairs={{0,24},{1,25},{2,26},{3,27},{4,28},{5,29},{6,30},{7,31},{8,16},{9,... | collective-permute-start | bytes 110600 | tf_op jit(solution)/shard_map/ppermute | solution.py:469
  21.7 1.7 %collective-permute-done.4.other = f32[72,128]{1,0:T(8,128)S(1)} collective-permute-done((f32[72,128]{1,0:T(8,128)S(1)}, f32[72,128]{1,0:T(8,128)S(1)}, u32[]{:S(2)}, u32[]{:S(2)}) %collective-permute-start.4) | collective-permute-done | bytes 36896 | tf_op jit(solution)/shard_map/ppermute | solution.py:469
  23.4 0.3 %collective-permute-start.5 = (f32[48,128]{1,0:T(8,128)S(1)}, f32[48,128]{1,0:T(8,128)S(1)}, u32[]{:S(2)}, u32[]{:S(2)}) collective-permute-start(f32[48,128]{1,0:T(8,128)S(1)} %shard_map.71.entry), channel_id=1, source_target_pairs={{0,16},{16,0},{1,17},{17,1},{2,18},{18,2},{3,19},{19,3},{4,20},{20... | collective-permute-start | bytes 73736 | tf_op jit(solution)/shard_map/ppermute | solution.py:480
  23.7 0.1 shard_map.73
  23.7 0.7 %shard_map.74.before = f32[1,16,8,2,256]{4,3,2,1,0:T(2,128)} custom-call(f32[16,8,2,128]{3,2,1,0:T(2,128)S(1)} %bitcast.5), custom_call_target="tpu_custom_call" | custom-call | tf_op jit(solution)/shard_map/pallas_call | solution.py:69
  24.4 0.2 collective-permute-done.5.entry
  24.7 0.0 collective-permute-done.6.away
  24.7 0.7 %shard_map.75 = f32[1,16,8,2,256]{4,3,2,1,0:T(2,128)} custom-call(f32[48,128]{1,0:T(8,128)S(1)} %collective-permute-done.5.entry, f32[512,128]{1,0:T(8,128)S(1)} %collective-permute-done.6.away, f32[1,16,8,2,256]{4,3,2,1,0:T(2,128)} %shard_map.74.before), custom_call_target="tpu_custom_call", output_to_operand_aliasing={{}: (2, {})} | custom-call | tf_op jit(solution)/shard_map/pallas_call | solution.py:69
  (1 shorter events, 0.0 us)
Async XLA Ops:
  1.0 1.7 %collective-permute-start = (f32[512,128]{1,0:T(8,128)S(1)}, f32[512,128]{1,0:T(8,128)S(1)}, u32[]{:S(2)}, u32[]{:S(2)}) collective-permute-start(f32[512,128]{1,0:T(8,128)S(1)} %bitcast.6), channel_id=1, source_target_pairs={{0,16},{16,0},{1,17},{17,1},{2,18},{18,2},{3,19},{19,3},{4,20},{20... | collective-permute-start | bytes 786440 | tf_op jit(solution)/shard_map/ppermute | solution.py:444
  3.1 5.8 %collective-permute-start.1 = (f32[168,128]{1,0:T(8,128)S(1)}, f32[168,128]{1,0:T(8,128)S(1)}, u32[]{:S(2)}, u32[]{:S(2)}) collective-permute-start(f32[168,128]{1,0:T(8,128)S(1)} %get-tuple-element.23.mine), channel_id=1, source_target_pairs={{0,1},{1,0},{2,3},{3,2},{4,5},{5,4},{6,7},{7,6},{8,9},{9,8},{10,11... | collective-permute-start | bytes 258056 | tf_op jit(solution)/shard_map/ppermute | solution.py:459
  8.9 4.6 %collective-permute-start.2 = (f32[168,128]{1,0:T(8,128)S(1)}, f32[168,128]{1,0:T(8,128)S(1)}, u32[]{:S(2)}, u32[]{:S(2)}) collective-permute-start(f32[168,128]{1,0:T(8,128)S(1)} %get-tuple-element.24.mine), channel_id=1, source_target_pairs={{0,2},{1,3},{2,0},{3,1},{4,6},{5,7},{6,4},{7,5},{8,10},{9,11},{10,... | collective-permute-start | bytes 258056 | tf_op jit(solution)/shard_map/ppermute | solution.py:459
  13.6 4.6 %collective-permute-start.3 = (f32[168,128]{1,0:T(8,128)S(1)}, f32[168,128]{1,0:T(8,128)S(1)}, u32[]{:S(2)}, u32[]{:S(2)}) collective-permute-start(f32[168,128]{1,0:T(8,128)S(1)} %get-tuple-element.25.mine), channel_id=1, source_target_pairs={{0,4},{1,5},{2,6},{3,7},{4,0},{5,1},{6,2},{7,3},{8,12},{9,13},{10,... | collective-permute-start | bytes 258056 | tf_op jit(solution)/shard_map/ppermute | solution.py:459
  18.7 6.0 %collective-permute-start.6 = (f32[512,128]{1,0:T(8,128)S(1)}, f32[512,128]{1,0:T(8,128)S(1)}, u32[]{:S(2)}, u32[]{:S(2)}) collective-permute-start(f32[512,128]{1,0:T(8,128)S(1)} %get-tuple-element.33), channel_id=1, source_target_pairs={{0,16},{16,0},{1,17},{17,1},{2,18},{18,2},{3,19},{19,3},{4,20},{20... | collective-permute-start | bytes 786440 | tf_op jit(solution)/shard_map/ppermute | solution.py:473
  18.8 4.6 %collective-permute-start.4 = (f32[72,128]{1,0:T(8,128)S(1)}, f32[72,128]{1,0:T(8,128)S(1)}, u32[]{:S(2)}, u32[]{:S(2)}) collective-permute-start(f32[72,128]{1,0:T(8,128)S(1)} %get-tuple-element.26.mine), channel_id=1, source_target_pairs={{0,24},{1,25},{2,26},{3,27},{4,28},{5,29},{6,30},{7,31},{8,16},{9,... | collective-permute-start | bytes 110600 | tf_op jit(solution)/shard_map/ppermute | solution.py:469
  23.4 1.3 %collective-permute-start.5 = (f32[48,128]{1,0:T(8,128)S(1)}, f32[48,128]{1,0:T(8,128)S(1)}, u32[]{:S(2)}, u32[]{:S(2)}) collective-permute-start(f32[48,128]{1,0:T(8,128)S(1)} %shard_map.71.entry), channel_id=1, source_target_pairs={{0,16},{16,0},{1,17},{17,1},{2,18},{18,2},{3,19},{19,3},{4,20},{20... | collective-permute-start | bytes 73736 | tf_op jit(solution)/shard_map/ppermute | solution.py:480

commit v10 on v8

--- a/solution.py
+++ b/solution.py
@@ -414,8 +414,9 @@
     one.wait()
 
 
-def last_kernel(half, got, before, out, sem):
-    one = part_copy(half, 1 - half_of(), got, out, sem.at[0])
+def last_kernel(lines, half, entry, away, before, out, value, sem):
+    own_kernel(lines, entry, away, value)
+    one = part_copy(half, 1 - half_of(), value.reshape(lines, value.shape[0] // (2 * lines), 2, half), out, sem.at[0])
     one.start()
     one.wait()
 
@@ -497,13 +498,13 @@
         out_specs=[HBM],
     )
     (out,) = call(
-        functools.partial(last_kernel, half),
+        functools.partial(last_kernel, lines, half),
         [krylov.shape],
-        [plane_half(got_entry, away), out],
-        [pltpu.SemaphoreType.DMA((1,))],
-        specs=[ANY, HBM],
+        [got_entry, away, out],
+        [pltpu.VMEM((lines * 16, half), jnp.float32), pltpu.SemaphoreType.DMA((1,))],
+        specs=[VMEM, VMEM, HBM],
         out_specs=[HBM],
-        aliases={1: 0},
+        aliases={2: 0},
     )
     return out
 

time: 25.6 us -> 25.6 us (level)
    pallas_call x13 -> x12, Pallas kernels: 4.73 us -> 4.72 us  [call(): pl.pallas_call(kernel, out_shape=[jax.ShapeDtypeStruct(s, jnp.float32) fo...]
where the time goes in v10:
time: 25.6 us; the launch traced here: 25.4 us
  starting transfers between devices  10.5 us (41%)
  waiting for transfers between devices  10.2 us (40%)
  Pallas kernels  4.72 us (18%)
    ppermute x3, waiting for transfers between devices, per_device(): got = lax.ppermute(edge, 'gy', [(j, j ^ 1 << level) for j in range(count)])  8.27 us
    ppermute x3, starting transfers between devices, per_device(): got = lax.ppermute(edge, 'gy', [(j, j ^ 1 << level) for j in range(count)])  6.62 us
    pallas_call x12, Pallas kernels, call(): pl.pallas_call(kernel, out_shape=[jax.ShapeDtypeStruct(s, jnp.float32) fo...  4.72 us
    ppermute x1, starting transfers between devices, per_device(): got = lax.ppermute(edge, ('gx', 'gy'), across)  2.94 us
    ppermute x1, waiting for transfers between devices, per_device(): got = lax.ppermute(edge, ('gx', 'gy'), across)  1.65 us
    ppermute x1, starting transfers between devices, per_device(): recv = lax.ppermute(pack(True), 'gx', swap)  0.56 us
  transfers between devices with their start and end apart: 7, of which 5 were waited for; matrix products, arithmetic and copies ran while one was open for 0% of the time, Pallas kernels for 8%

profile of v10, /device:TPU:0, one launch (start us, length us, event | category | flops | bytes accessed | tf_op | source)
XLA Modules:
  0.0 25.4 jit_solution(15296389779763807150)
XLA Ops:
  0.0 1.0 %shard_map.65 = f32[16,16,2,128]{3,2,1,0:T(2,128)S(1)} custom-call(f32[1,16,8,2,256]{4,3,2,1,0:T(2,128)} %krylov.3, f32[1,16,2,2,256]{4,3,2,1,0:T(2,128)} %inverse.3, f32[1,16,2,2,256]{4,3,2,1,0:T(2,128)} %back.3, f32[1,16,2,2,256]{4,3,2,1,0:T(2,128)} %front.3, f32[1,16,2,2,256]{4,3,2,1,0:T(2,128)} %left.3, f32[1,16,2,2,256]{4,3,2,1,0:T(2,128)} %right.3), custom_call_target="tpu_custom_call" | custom-call | tf_op jit(solution)/shard_map/pallas_call | solution.py:69
  1.0 0.6 %collective-permute-start = (f32[512,128]{1,0:T(8,128)S(1)}, f32[512,128]{1,0:T(8,128)S(1)}, u32[]{:S(2)}, u32[]{:S(2)}) collective-permute-start(f32[512,128]{1,0:T(8,128)S(1)} %bitcast.6), channel_id=1, source_target_pairs={{0,16},{16,0},{1,17},{17,1},{2,18},{18,2},{3,19},{19,3},{4,20},{20... | collective-permute-start | bytes 786440 | tf_op jit(solution)/shard_map/ppermute | solution.py:446
  1.5 1.0 %shard_map.64 = f32[16,16,2,128]{3,2,1,0:T(2,128)S(1)} custom-call(f32[1,16,8,2,256]{4,3,2,1,0:T(2,128)} %krylov.3, f32[1,16,2,2,256]{4,3,2,1,0:T(2,128)} %inverse.3, f32[1,16,2,2,256]{4,3,2,1,0:T(2,128)} %back.3, f32[1,16,2,2,256]{4,3,2,1,0:T(2,128)} %front.3, f32[1,16,2,2,256]{4,3,2,1,0:T(2,128)} %left.3, f32[1,16,2,2,256]{4,3,2,1,0:T(2,128)} %right.3), custom_call_target="tpu_custom_call" | custom-call | tf_op jit(solution)/shard_map/pallas_call | solution.py:69
  2.5 0.2 shard_map.66
  2.7 0.0 collective-permute-done.recv
  2.7 0.4 %shard_map.67 = (f32[168,128]{1,0:T(8,128)S(1)}, f32[512,128]{1,0:T(8,128)S(1)}, f32[512,128]{1,0:T(8,128)S(1)}, f32[512,128]{1,0:T(8,128)S(1)}) custom-call(f32[512,128]{1,0:T(8,128)S(1)} %bitcast.4, f32[512,128]{1,0:T(8,128)S(1)} %collective-permute-done.recv, f32[512,128]{1,0:T(8,128)S(1)} %get-tuple-element.20.swept.refs_5_, ...), custom_call_target="tpu_custom_call" | custom-call | tf_op jit(solution)/shard_map/pallas_call | solution.py:69
  3.1 2.9 %collective-permute-start.1 = (f32[168,128]{1,0:T(8,128)S(1)}, f32[168,128]{1,0:T(8,128)S(1)}, u32[]{:S(2)}, u32[]{:S(2)}) collective-permute-start(f32[168,128]{1,0:T(8,128)S(1)} %get-tuple-element.23.mine), channel_id=1, source_target_pairs={{0,1},{1,0},{2,3},{3,2},{4,5},{5,4},{6,7},{7,6},{8,9},{9,8},{10,11... | collective-permute-start | bytes 258056 | tf_op jit(solution)/shard_map/ppermute | solution.py:461
  6.0 2.9 %collective-permute-done.1.other = f32[168,128]{1,0:T(8,128)S(1)} collective-permute-done((f32[168,128]{1,0:T(8,128)S(1)}, f32[168,128]{1,0:T(8,128)S(1)}, u32[]{:S(2)}, u32[]{:S(2)}) %collective-permute-start.1) | collective-permute-done | bytes 86048 | tf_op jit(solution)/shard_map/ppermute | solution.py:461
  8.9 0.1 shard_map.68
  8.9 1.8 %collective-permute-start.2 = (f32[168,128]{1,0:T(8,128)S(1)}, f32[168,128]{1,0:T(8,128)S(1)}, u32[]{:S(2)}, u32[]{:S(2)}) collective-permute-start(f32[168,128]{1,0:T(8,128)S(1)} %get-tuple-element.24.mine), channel_id=1, source_target_pairs={{0,2},{1,3},{2,0},{3,1},{4,6},{5,7},{6,4},{7,5},{8,10},{9,11},{10,... | collective-permute-start | bytes 258056 | tf_op jit(solution)/shard_map/ppermute | solution.py:461
  10.8 2.7 %collective-permute-done.2.other = f32[168,128]{1,0:T(8,128)S(1)} collective-permute-done((f32[168,128]{1,0:T(8,128)S(1)}, f32[168,128]{1,0:T(8,128)S(1)}, u32[]{:S(2)}, u32[]{:S(2)}) %collective-permute-start.2) | collective-permute-done | bytes 86048 | tf_op jit(solution)/shard_map/ppermute | solution.py:461
  13.5 0.1 shard_map.69
  13.6 1.9 %collective-permute-start.3 = (f32[168,128]{1,0:T(8,128)S(1)}, f32[168,128]{1,0:T(8,128)S(1)}, u32[]{:S(2)}, u32[]{:S(2)}) collective-permute-start(f32[168,128]{1,0:T(8,128)S(1)} %get-tuple-element.25.mine), channel_id=1, source_target_pairs={{0,4},{1,5},{2,6},{3,7},{4,0},{5,1},{6,2},{7,3},{8,12},{9,13},{10,... | collective-permute-start | bytes 258056 | tf_op jit(solution)/shard_map/ppermute | solution.py:461
  15.4 2.7 %collective-permute-done.3.other = f32[168,128]{1,0:T(8,128)S(1)} collective-permute-done((f32[168,128]{1,0:T(8,128)S(1)}, f32[168,128]{1,0:T(8,128)S(1)}, u32[]{:S(2)}, u32[]{:S(2)}) %collective-permute-start.3) | collective-permute-done | bytes 86048 | tf_op jit(solution)/shard_map/ppermute | solution.py:461
  18.1 0.1 shard_map.70
  18.2 0.6 %shard_map.72 = (f32[512,128]{1,0:T(8,128)S(1)}, f32[512,128]{1,0:T(8,128)S(1)}) custom-call(f32[168,128]{1,0:T(8,128)S(1)} %get-tuple-element.27.refs_0_, f32[168,128]{1,0:T(8,128)S(1)} %get-tuple-element.28.refs_1_, f32[168,128]{1,0:T(8,128)S(1)} %get-tuple-element.29.refs_2_, f32[512,128]{1,0:T(8,128)S(1)} %get-tuple-element.30.refs_3_, ...), custom_call_target="tpu_custom_call" | custom-call | tf_op jit(solution)/shard_map/pallas_call | solution.py:69
  18.7 0.1 collective-permute-start.6
  18.8 2.9 %collective-permute-start.4 = (f32[72,128]{1,0:T(8,128)S(1)}, f32[72,128]{1,0:T(8,128)S(1)}, u32[]{:S(2)}, u32[]{:S(2)}) collective-permute-start(f32[72,128]{1,0:T(8,128)S(1)} %get-tuple-element.26.mine), channel_id=1, source_target_pairs={{0,24},{1,25},{2,26},{3,27},{4,28},{5,29},{6,30},{7,31},{8,16},{9,... | collective-permute-start | bytes 110600 | tf_op jit(solution)/shard_map/ppermute | solution.py:471
  21.8 1.7 %collective-permute-done.4.other = f32[72,128]{1,0:T(8,128)S(1)} collective-permute-done((f32[72,128]{1,0:T(8,128)S(1)}, f32[72,128]{1,0:T(8,128)S(1)}, u32[]{:S(2)}, u32[]{:S(2)}) %collective-permute-start.4) | collective-permute-done | bytes 36896 | tf_op jit(solution)/shard_map/ppermute | solution.py:471
  23.4 0.3 %collective-permute-start.5 = (f32[48,128]{1,0:T(8,128)S(1)}, f32[48,128]{1,0:T(8,128)S(1)}, u32[]{:S(2)}, u32[]{:S(2)}) collective-permute-start(f32[48,128]{1,0:T(8,128)S(1)} %shard_map.71.entry), channel_id=1, source_target_pairs={{0,16},{16,0},{1,17},{17,1},{2,18},{18,2},{3,19},{19,3},{4,20},{20... | collective-permute-start | bytes 73736 | tf_op jit(solution)/shard_map/ppermute | solution.py:485
  23.7 0.1 shard_map.73
  23.8 0.7 %shard_map.74.before = f32[1,16,8,2,256]{4,3,2,1,0:T(2,128)} custom-call(f32[16,8,2,128]{3,2,1,0:T(2,128)S(1)} %bitcast.5), custom_call_target="tpu_custom_call" | custom-call | tf_op jit(solution)/shard_map/pallas_call | solution.py:69
  24.5 0.2 collective-permute-done.5.entry
  24.7 0.0 collective-permute-done.6.away
  24.7 0.7 %shard_map.75 = f32[1,16,8,2,256]{4,3,2,1,0:T(2,128)} custom-call(f32[48,128]{1,0:T(8,128)S(1)} %collective-permute-done.5.entry, f32[512,128]{1,0:T(8,128)S(1)} %collective-permute-done.6.away, f32[1,16,8,2,256]{4,3,2,1,0:T(2,128)} %shard_map.74.before), custom_call_target="tpu_custom_call", output_to_operand_aliasing={{}: (2, {})} | custom-call | tf_op jit(solution)/shard_map/pallas_call | solution.py:69
  (1 shorter events, 0.0 us)
Async XLA Ops:
  1.0 1.7 %collective-permute-start = (f32[512,128]{1,0:T(8,128)S(1)}, f32[512,128]{1,0:T(8,128)S(1)}, u32[]{:S(2)}, u32[]{:S(2)}) collective-permute-start(f32[512,128]{1,0:T(8,128)S(1)} %bitcast.6), channel_id=1, source_target_pairs={{0,16},{16,0},{1,17},{17,1},{2,18},{18,2},{3,19},{19,3},{4,20},{20... | collective-permute-start | bytes 786440 | tf_op jit(solution)/shard_map/ppermute | solution.py:446
  3.1 5.8 %collective-permute-start.1 = (f32[168,128]{1,0:T(8,128)S(1)}, f32[168,128]{1,0:T(8,128)S(1)}, u32[]{:S(2)}, u32[]{:S(2)}) collective-permute-start(f32[168,128]{1,0:T(8,128)S(1)} %get-tuple-element.23.mine), channel_id=1, source_target_pairs={{0,1},{1,0},{2,3},{3,2},{4,5},{5,4},{6,7},{7,6},{8,9},{9,8},{10,11... | collective-permute-start | bytes 258056 | tf_op jit(solution)/shard_map/ppermute | solution.py:461
  8.9 4.6 %collective-permute-start.2 = (f32[168,128]{1,0:T(8,128)S(1)}, f32[168,128]{1,0:T(8,128)S(1)}, u32[]{:S(2)}, u32[]{:S(2)}) collective-permute-start(f32[168,128]{1,0:T(8,128)S(1)} %get-tuple-element.24.mine), channel_id=1, source_target_pairs={{0,2},{1,3},{2,0},{3,1},{4,6},{5,7},{6,4},{7,5},{8,10},{9,11},{10,... | collective-permute-start | bytes 258056 | tf_op jit(solution)/shard_map/ppermute | solution.py:461
  13.6 4.6 %collective-permute-start.3 = (f32[168,128]{1,0:T(8,128)S(1)}, f32[168,128]{1,0:T(8,128)S(1)}, u32[]{:S(2)}, u32[]{:S(2)}) collective-permute-start(f32[168,128]{1,0:T(8,128)S(1)} %get-tuple-element.25.mine), channel_id=1, source_target_pairs={{0,4},{1,5},{2,6},{3,7},{4,0},{5,1},{6,2},{7,3},{8,12},{9,13},{10,... | collective-permute-start | bytes 258056 | tf_op jit(solution)/shard_map/ppermute | solution.py:461
  18.7 6.0 %collective-permute-start.6 = (f32[512,128]{1,0:T(8,128)S(1)}, f32[512,128]{1,0:T(8,128)S(1)}, u32[]{:S(2)}, u32[]{:S(2)}) collective-permute-start(f32[512,128]{1,0:T(8,128)S(1)} %get-tuple-element.33), channel_id=1, source_target_pairs={{0,16},{16,0},{1,17},{17,1},{2,18},{18,2},{3,19},{19,3},{4,20},{20... | collective-permute-start | bytes 786440 | tf_op jit(solution)/shard_map/ppermute | solution.py:478
  18.8 4.6 %collective-permute-start.4 = (f32[72,128]{1,0:T(8,128)S(1)}, f32[72,128]{1,0:T(8,128)S(1)}, u32[]{:S(2)}, u32[]{:S(2)}) collective-permute-start(f32[72,128]{1,0:T(8,128)S(1)} %get-tuple-element.26.mine), channel_id=1, source_target_pairs={{0,24},{1,25},{2,26},{3,27},{4,28},{5,29},{6,30},{7,31},{8,16},{9,... | collective-permute-start | bytes 110600 | tf_op jit(solution)/shard_map/ppermute | solution.py:471
  23.4 1.3 %collective-permute-start.5 = (f32[48,128]{1,0:T(8,128)S(1)}, f32[48,128]{1,0:T(8,128)S(1)}, u32[]{:S(2)}, u32[]{:S(2)}) collective-permute-start(f32[48,128]{1,0:T(8,128)S(1)} %shard_map.71.entry), channel_id=1, source_target_pairs={{0,16},{16,0},{1,17},{17,1},{2,18},{18,2},{3,19},{19,3},{4,20},{20... | collective-permute-start | bytes 73736 | tf_op jit(solution)/shard_map/ppermute | solution.py:485
